TPU v7x, 32 devices: a whole 2x2x4 slice. The times are simulated.
32 devices in a mesh: tile: 8 (over y, x, core), depth: 4 (over z).
Axes of the slice: x: 2, y: 2, z: 4, core: 2. Of those that a mesh axis runs over, the one named last changes fastest.
Arguments:
- transmission: float32 [2, 4, 1024, 512], P(None, 'depth', 'tile'), may hold values from -1.2 to 1.2, as said below
- probe_wave: float32 [2, 128, 128], replicated, may hold values from -6 to 6
- fresnel_phase: float32 [128, 128], replicated, may hold values from -3.140625 to 3.140625
- measured: float32 [32, 128, 128], P('tile'), may hold values from 0.1 to 4
- positions: int32 [32, 2], P('tile'), may hold values from 0 to 1023, as said below
- extents: int32 [8, 2], P('tile'), may hold values from 32 to 64
Outputs:
- object_grad: float32 [2, 4, 1024, 512], P(None, 'depth', 'tile')
Inputs may be any that keep to these rules, and one draw needn't show every extreme that they name: `transmission`: real and imaginary parts of a pixel form a complex number of modulus 0.7 to 1.2. `positions`: probe p belongs to tile t = p // 4. Its first row r satisfies ((r - 128 t + 64) mod 1024) - 64 between -64 and 64, both ends reached in every draw; its first column lies between 0 and 384.
All inputs are finite; a program needn't handle non-finite values.
Results may differ from a plain program's by a relative error of at most 0.025.
Values may be sent and summed in bfloat16 or wider, within the bound.
No kernel may reach another device: no remote copies, remote signals or barrier semaphores. Data moves between devices by JAX's collectives and lax.ppermute only.
A program may use at most 64 MiB of HBM per device.

v0:
```python
import math

import jax
import jax.numpy as jnp
import numpy as np
from jax import lax
from jax.experimental import pallas as pl
from jax.experimental.pallas import tpu as pltpu
from jax.sharding import PartitionSpec as P

BAND = 64
LANES = 128
SPAN = 1 << 16


SMEM = pl.BlockSpec(memory_space=pltpu.SMEM)
VMEM = pl.BlockSpec(memory_space=pltpu.VMEM)
PARAMS = pltpu.CompilerParams(vmem_limit_bytes=12 << 20)


def tables(length):
    indices = np.arange(length)
    angles = (indices[:, None] * indices[None, :] % length) * (2.0 * math.pi / length)
    cosine, sine = np.cos(angles), np.sin(angles)
    ahead = np.block([[cosine, sine], [-sine, cosine]]).astype(np.float32)
    back = np.block([[cosine, -sine], [sine, cosine]]).astype(np.float32)
    found = []
    for matrix in (ahead, back):
        high = matrix.astype(jnp.bfloat16)
        found += [high, (matrix - high.astype(np.float32)).astype(jnp.bfloat16)]
    return found


def first_row(positions, probe, tile, strip, tiles):
    rows = strip * tiles
    start = positions[0, probe] - tile * strip + BAND
    start = jnp.where(start < 0, start + rows, start)
    return jnp.where(start >= rows, start - rows, start)


def placed(codes, place):
    code = codes[place : place + 1, :1][0, 0]
    row = lax.div(code, SPAN)
    column = code - row * SPAN
    block = lax.div(column, LANES)
    return row, block, column - block * LANES


def edge_half(row, strip):
    upper = row < BAND
    return jnp.where(upper, 0, BAND), jnp.where(upper, row, row + strip - BAND)


def turned_pair(wide, part, block, rows, offset, lane):
    turn = lax.rem(LANES - offset, LANES)
    left = pltpu.roll(wide[part, block, rows], turn, 1)
    right = pltpu.roll(wide[part, block + 1, rows], turn, 1)
    return jnp.where(lane < LANES - offset, left, right)


def cut_kernel(order, tiles, positions, own, out, codes, early, wide):
    strip, columns = own.shape[2:]
    window = out.shape[2]
    tile, depth = lax.axis_index("tile"), lax.axis_index("depth")
    for block in range(columns // LANES):
        for part in range(2):
            wide[part, block, BAND : BAND + strip] = own[part, 0, :, block * LANES : (block + 1) * LANES]
    lane = lax.broadcasted_iota(jnp.int32, (window, LANES), 1)
    for place, mask in enumerate(order):
        probe = depth ^ mask
        row, column = first_row(positions, probe, tile, strip, tiles), positions[1, probe]
        codes[place : place + 1] = jnp.full((1, LANES), row * SPAN + column, jnp.int32)
        block = lax.div(column, LANES)
        offset = column - block * LANES
        for part in range(2):
            out[place, part] = turned_pair(wide, part, block, pl.ds(row, window), offset, lane)
        if place == 0:
            half, _ = edge_half(row, strip)
            other = pl.multiple_of(window - BAND - half, BAND)
            early[...] = out[0, :, pl.ds(other, BAND)].astype(early.dtype)


def prep_kernel(strip, extents, codes, probe_wave, fresnel_phase, incident, turn):
    window = probe_wave.shape[1]
    row, _, _ = placed(codes, codes.shape[0] - 1)
    line = row - BAND + lax.broadcasted_iota(jnp.int32, (window, window), 0)
    inside = (line >= -extents[0, 0]) & (line < strip + extents[0, 1])
    for part in range(2):
        incident[part] = jnp.where(inside, probe_wave[part], 0.0)
    scale = 1.0 / window**2
    turn[0] = jnp.cos(fresnel_phase[...]) * scale
    turn[1] = jnp.sin(fresnel_phase[...]) * scale


def join_kernel(strip, codes, windows, outer, inner, *refs):
    outs, wide = refs[:-1], refs[-1]
    columns = outer.shape[3]
    window = windows.shape[2]
    odd = lax.rem(lax.axis_index("tile"), 2)
    for block in range(columns // LANES):
        cols = slice(block * LANES, (block + 1) * LANES)
        for part in range(2):
            far = pl.multiple_of(odd * (strip + BAND), BAND)
            near = pl.multiple_of((1 - odd) * (strip + BAND), BAND)
            wide[part, block, pl.ds(far, BAND)] = outer[part, 0, :, cols].astype(jnp.float32)
            wide[part, block, pl.ds(near, BAND)] = inner[part, 0, :, cols].astype(jnp.float32)
    lane = lax.broadcasted_iota(jnp.int32, (BAND, LANES), 1)
    line = lax.broadcasted_iota(jnp.int32, (BAND, LANES), 0)
    for place, out in enumerate(outs):
        row, block, offset = placed(codes, place)
        half, start = edge_half(row, strip)
        within = row + half + line
        outside = (within < BAND) | (within >= BAND + strip)
        half = pl.multiple_of(half, BAND)
        other = pl.multiple_of(window - BAND - half, BAND)
        for part in range(2):
            band = turned_pair(wide, part, block, pl.ds(start, BAND), offset, lane)
            joined = jnp.where(outside, band, windows[place, part, pl.ds(half, BAND)]).astype(jnp.bfloat16)
            if place == 0:
                out[part] = joined
                continue
            out[part, pl.ds(half, BAND)] = joined
            out[part, pl.ds(other, BAND)] = windows[place, part, pl.ds(other, BAND)].astype(jnp.bfloat16)


def split(value):
    high = value.astype(jnp.bfloat16)
    return high, (value - high.astype(jnp.float32)).astype(jnp.bfloat16)


def dot(left, right):
    return jnp.dot(left, right, preferred_element_type=jnp.float32)


def from_left(real, imag, matrix, exact):
    half = real.shape[1]
    stacked = jnp.concatenate([real, imag], axis=0)
    if exact:
        high, low = split(stacked)
        both = dot(matrix[0], jnp.concatenate([high, low], axis=1))
        stacked = both[:, :half] + both[:, half:] + dot(matrix[1], high)
    else:
        stacked = dot(matrix[0], stacked.astype(jnp.bfloat16))
    size = real.shape[0]
    return stacked[:size], stacked[size:]


def from_right(real, imag, matrix, exact):
    size = real.shape[0]
    stacked = jnp.concatenate([real, imag], axis=1)
    if exact:
        high, low = split(stacked)
        both = dot(jnp.concatenate([high, low], axis=0), matrix[0])
        stacked = both[:size] + both[size:] + dot(high, matrix[1])
    else:
        stacked = dot(stacked.astype(jnp.bfloat16), matrix[0])
    half = real.shape[1]
    return stacked[:, :half], stacked[:, half:]


def wave_kernel(order, strip, codes, incident, turn, measured, *refs):
    depths = len(order)
    matrices, arrived, outs = refs[:4], refs[4 : 5 + depths], refs[5 + depths : 6 + 2 * depths]
    layers, waves = refs[6 + 2 * depths :]
    window = incident.shape[1]
    ahead = [matrices[0][...], matrices[1][...]]
    back = [matrices[2][...], matrices[3][...]]
    depth = lax.axis_index("depth")

    def transform(value, exact):
        return from_right(*from_left(*value, ahead, exact), back, exact)

    def inverse(value, exact):
        return from_right(*from_left(*value, back, exact), ahead, exact)

    half, _ = edge_half(placed(codes, depths - 1)[0], strip)
    half = pl.multiple_of(half, BAND)
    other = pl.multiple_of(window - BAND - half, BAND)
    for mask, value in zip(order[1:], arrived[2:]):
        layers[depth ^ mask] = value[...].astype(jnp.float32)
    layers[depth ^ order[0], :, pl.ds(half, BAND)] = arrived[0][...].astype(jnp.float32)
    layers[depth ^ order[0], :, pl.ds(other, BAND)] = arrived[1][...].astype(jnp.float32)
    real, imag = incident[0], incident[1]
    cosine, sine = turn[0], turn[1]
    scale = 1.0 / window
    for index in range(depths):
        waves[index, 0], waves[index, 1] = real, imag
        layer_real, layer_imag = layers[index, 0], layers[index, 1]
        mixed = (real * layer_real - imag * layer_imag, real * layer_imag + imag * layer_real)
        real, imag = transform(mixed, True)
        if index + 1 < depths:
            turned = (real * cosine - imag * sine, imag * cosine + real * sine)
            real, imag = inverse(turned, True)
    real, imag = real * scale, imag * scale
    misfit = (real * real + imag * imag - measured[depth]) * scale
    adjoint = inverse((misfit * real, misfit * imag), False)
    for index in reversed(range(depths)):
        adj_real, adj_imag = adjoint
        held_real, held_imag = waves[index, 0], waves[index, 1]
        waves[index, 0] = held_real * adj_real + held_imag * adj_imag
        waves[index, 1] = held_real * adj_imag - held_imag * adj_real
        if index > 0:
            layer_real, layer_imag = layers[index, 0], layers[index, 1]
            real, imag = transform(
                (layer_real * adj_real + layer_imag * adj_imag, layer_real * adj_imag - layer_imag * adj_real),
                False,
            )
            adjoint = inverse((real * cosine + imag * sine, imag * cosine - real * sine), False)
    outs[0][...] = waves[depth ^ order[0], :, pl.ds(half, BAND)].astype(jnp.bfloat16)
    outs[1][...] = waves[depth ^ order[0], :, pl.ds(other, BAND)].astype(jnp.bfloat16)
    for mask, out in zip(order[1:], outs[2:]):
        out[...] = waves[depth ^ mask].astype(jnp.bfloat16)


def added(wide, part, block, rows, value, offset, lane):
    value = pltpu.roll(value, offset, 1)
    wide[part, block, rows] += jnp.where(lane >= offset, value, 0.0)
    wide[part, block + 1, rows] += jnp.where(lane < offset, value, 0.0)


def shed_kernel(strip, codes, *refs):
    arrived, (outer, inner, wide) = refs[:-3], refs[-3:]
    columns = outer.shape[3]
    odd = lax.rem(lax.axis_index("tile"), 2)
    wide[:, :, :BAND] = jnp.zeros_like(wide[:, :, :BAND])
    wide[:, :, BAND + strip :] = jnp.zeros_like(wide[:, :, :BAND])
    lane = lax.broadcasted_iota(jnp.int32, (BAND, LANES), 1)
    for place, value in enumerate(arrived):
        row, block, offset = placed(codes, place)
        half, start = edge_half(row, strip)
        half = pl.multiple_of(half, BAND)
        for part in range(2):
            piece = value[part] if place == 0 else value[part, pl.ds(half, BAND)]
            piece = piece.astype(jnp.float32)
            added(wide, part, block, pl.ds(start, BAND), piece, offset, lane)
    far = pl.multiple_of(odd * (strip + BAND), BAND)
    near = pl.multiple_of((1 - odd) * (strip + BAND), BAND)
    for block in range(columns // LANES):
        cols = slice(block * LANES, (block + 1) * LANES)
        for part in range(2):
            outer[part, 0, :, cols] = wide[part, block, pl.ds(far, BAND)].astype(jnp.bfloat16)
            inner[part, 0, :, cols] = wide[part, block, pl.ds(near, BAND)].astype(jnp.bfloat16)


def add_kernel(codes, early, late, *refs):
    arrived, (own, wide) = refs[:-2], refs[-2:]
    strip, columns = own.shape[2:]
    window = arrived[0].shape[1]
    wide[...] = jnp.zeros_like(wide)
    lane = lax.broadcasted_iota(jnp.int32, (window, LANES), 1)
    row, block, offset = placed(codes, 0)
    half, _ = edge_half(row, strip)
    for value, start in ((early, half), (late, window - BAND - half)):
        for part in range(2):
            piece = value[part].astype(jnp.float32)
            added(wide, part, block, pl.ds(row + start, BAND), piece, offset, lane[:BAND])
    for place, value in enumerate(arrived):
        row, block, offset = placed(codes, place + 1)
        for part in range(2):
            added(wide, part, block, pl.ds(row, window), value[part].astype(jnp.float32), offset, lane)
    for block in range(columns // LANES):
        for part in range(2):
            own[part, 0, :, block * LANES : (block + 1) * LANES] = wide[part, block, BAND : BAND + strip]


def edge_kernel(own, outer, inner, out):
    strip = own.shape[2]
    odd = lax.rem(lax.axis_index("tile"), 2)
    out[...] = own[...]
    far = pl.multiple_of(odd * (strip - BAND), BAND)
    near = pl.multiple_of((1 - odd) * (strip - BAND), BAND)
    out[:, :, pl.ds(far, BAND)] += outer[...].astype(jnp.float32)
    out[:, :, pl.ds(near, BAND)] += inner[...].astype(jnp.float32)


def call(kernel, outs, operands, scratch=(), scalars=0):
    return pl.pallas_call(
        kernel,
        out_shape=outs,
        in_specs=[SMEM] * scalars + [VMEM] * (len(operands) - scalars),
        out_specs=jax.tree.map(lambda _: VMEM, outs),
        scratch_shapes=list(scratch),
        compiler_params=PARAMS,
    )(*operands)


def shards(transmission, probe_wave, fresnel_phase, measured, positions, extents):
    tiles, depths = lax.axis_size("tile"), lax.axis_size("depth")
    strip, columns = transmission.shape[2:]
    window = probe_wave.shape[1]
    assert positions.shape[0] == depths == 4 and transmission.shape[1] == 1 and tiles % 2 == 0
    assert strip == 2 * BAND == window
    order = (2, 3, 1, 0)
    wide = [pltpu.VMEM((2, columns // LANES + 1, strip + 2 * BAND, LANES), jnp.float32)]
    patch = jax.ShapeDtypeStruct((2, window, window), jnp.bfloat16)
    band = jax.ShapeDtypeStruct((2, 1, BAND, columns), jnp.bfloat16)
    odd = lax.axis_index("tile") % 2 == 1

    piece = jax.ShapeDtypeStruct((2, BAND, window), jnp.bfloat16)

    def swap(value, mask):
        if not mask:
            return value
        return lax.ppermute(value, "depth", [(d, d ^ mask) for d in range(depths)])

    def swapped(values):
        return [swap(v, mask) for v, mask in zip(values, order)]

    def outward(value):
        return lax.ppermute(value, "tile", [(t, (t - 1 + 2 * (t % 2)) % tiles) for t in range(tiles)])

    def inward(value):
        return lax.ppermute(value, "tile", [(t, t ^ 1) for t in range(tiles)])

    head, tail = transmission[:, :, :BAND], transmission[:, :, strip - BAND :]
    outer = outward(jnp.where(odd, tail, head).astype(jnp.bfloat16))
    inner = inward(jnp.where(odd, head, tail).astype(jnp.bfloat16))
    square = jax.ShapeDtypeStruct((2, window, window), jnp.float32)
    windows, codes, early = call(
        lambda *refs: cut_kernel(order, tiles, *refs),
        [
            jax.ShapeDtypeStruct((depths, 2, window, window), jnp.float32),
            jax.ShapeDtypeStruct((depths, LANES), jnp.int32),
            piece,
        ],
        [positions.T, transmission],
        wide,
        scalars=1,
    )
    early = swap(early, order[0])
    windows = call(
        lambda *refs: join_kernel(strip, *refs), [piece] + [patch] * (depths - 1), [codes, windows, outer, inner], wide
    )
    probe_wave, fresnel_phase, windows = lax.optimization_barrier((probe_wave, fresnel_phase, windows))
    incident, turn = call(
        lambda *refs: prep_kernel(strip, *refs),
        [square, square],
        [extents, codes, probe_wave, fresnel_phase],
        scalars=1,
    )
    windows = swapped(windows)
    first, late, *pieces = call(
        lambda *refs: wave_kernel(order, strip, *refs),
        [piece] * 2 + [patch] * (depths - 1),
        [codes, incident, turn, measured, *map(jnp.asarray, tables(window)), windows[0], early, *windows[1:]],
        [pltpu.VMEM((depths, 2, window, window), jnp.float32)] * 2,
    )
    first, *pieces = swapped([first, *pieces])
    late = swap(late, order[0])
    outer, inner = call(lambda *refs: shed_kernel(strip, *refs), [band] * 2, [codes, first, *pieces], wide)
    outer, inner = outward(outer), inward(inner)
    total = jax.ShapeDtypeStruct(transmission.shape, jnp.float32)
    own = call(add_kernel, total, [codes, first, late, *pieces], wide)
    return call(edge_kernel, total, [own, outer, inner])


def solution(mesh):
    placed = (
        P(None, "depth", "tile", None),
        P(),
        P(),
        P("tile", None, None),
        P("tile", None),
        P("tile", None),
    )
    return jax.shard_map(
        shards,
        mesh=mesh,
        in_specs=placed,
        out_specs=P(None, "depth", "tile", None),
        check_vma=False,
    )
```

profile of v0, /device:TPU:0, one launch (start us, length us, event | category | flops | bytes accessed | tf_op | source)
XLA Modules:
  0.0 40.1 jit_solution(18390088347082098380)
XLA Ops:
  0.0 0.0 copy-start
  0.0 1.1 %select_convert_fusion = (bf16[2,1,64,512]{3,2,1,0:T(8,128)(2,1)S(1)}, bf16[2,1,64,512]{3,2,1,0:T(8,128)(2,1)S(1)}) fusion(f32[2,1,128,512]{3,2,1,0:T(8,128)} %refs_1_.1, pred[]{:T(512)S(6)} %eq.5), kind=kLoop, calls=%fused_computation | loop fusion | flops 131072 | bytes 524289 | tf_op jit(solution)/shard_map/convert_element_type | solution.py:317
  1.1 0.6 %collective-permute-start.1 = (bf16[2,1,64,512]{3,2,1,0:T(8,128)(2,1)S(1)}, bf16[2,1,64,512]{3,2,1,0:T(8,128)(2,1)S(1)}, u32[]{:S(2)}, u32[]{:S(2)}) collective-permute-start(bf16[2,1,64,512]{3,2,1,0:T(8,128)(2,1)S(1)} %get-tuple-element.49), channel_id=1, source_target_pairs={{0,4},{4,0},{8,12},{12,8},{16,20},{20,16},{24,28},{28,24},{1,5},{5... | collective-permute-start | bytes 393224 | tf_op jit(solution)/shard_map/ppermute | solution.py:313
  1.7 0.0 copy-start.8
  1.7 3.5 %collective-permute-start = (bf16[2,1,64,512]{3,2,1,0:T(8,128)(2,1)S(1)}, bf16[2,1,64,512]{3,2,1,0:T(8,128)(2,1)S(1)}, u32[]{:S(2)}, u32[]{:S(2)}) collective-permute-start(bf16[2,1,64,512]{3,2,1,0:T(8,128)(2,1)S(1)} %get-tuple-element.50), channel_id=1, source_target_pairs={{0,28},{4,8},{8,4},{12,16},{16,12},{20,24},{24,20},{28,0},{1,29},{... | collective-permute-start | bytes 393224 | tf_op jit(solution)/shard_map/ppermute | solution.py:310
  5.2 0.0 copy-done
  5.2 0.0 copy-done.8
  5.2 0.0 copy-start.7
  5.2 0.9 %shard_map.100 = (f32[4,2,128,128]{3,2,1,0:T(8,128)S(1)}, s32[4,128]{1,0:T(4,128)S(1)}, bf16[2,64,128]{2,1,0:T(8,128)(2,1)S(1)}) custom-call(s32[2,4]{1,0:T(2,128)S(1)} %bitcast.1, f32[2,1,128,512]{3,2,1,0:T(8,128)S(1)} %copy-done), custom_call_target="tpu_custom_call" | custom-call | tf_op jit(solution)/shard_map/pallas_call | solution.py:277
  6.2 0.0 collective-permute-done.1.refs_3_
  6.2 2.3 %collective-permute-done.refs_2_ = bf16[2,1,64,512]{3,2,1,0:T(8,128)(2,1)S(1)} collective-permute-done((bf16[2,1,64,512]{3,2,1,0:T(8,128)(2,1)S(1)}, bf16[2,1,64,512]{3,2,1,0:T(8,128)(2,1)S(1)}, u32[]{:S(2)}, u32[]{:S(2)}) %collective-permute-start) | collective-permute-done | bytes 131104 | tf_op jit(solution)/shard_map/ppermute | solution.py:310
  8.5 0.0 copy-start.4
  8.5 0.0 copy-start.5
  8.5 0.2 shard_map.101
  8.7 0.0 copy-start.2
  8.7 4.0 %collective-permute-start.4 = (bf16[2,128,128]{2,1,0:T(8,128)(2,1)S(1)}, bf16[2,128,128]{2,1,0:T(8,128)(2,1)S(1)}, u32[]{:S(2)}, u32[]{:S(2)}) collective-permute-start(bf16[2,128,128]{2,1,0:T(8,128)(2,1)S(1)} %get-tuple-element.39), channel_id=1, source_target_pairs={{0,3},{1,2},{2,1},{3,0},{4,7},{5,6},{6,5},{7,4},{8,11},{9,10},{10,... | collective-permute-start | bytes 196616 | tf_op jit(solution)/shard_map/ppermute | solution.py:304
  12.7 0.0 collective-permute-start.5
  12.7 0.6 %collective-permute-start.3 = (bf16[2,64,128]{2,1,0:T(8,128)(2,1)S(1)}, bf16[2,64,128]{2,1,0:T(8,128)(2,1)S(1)}, u32[]{:S(2)}, u32[]{:S(2)}) collective-permute-start(bf16[2,64,128]{2,1,0:T(8,128)(2,1)S(1)} %get-tuple-element.38), channel_id=1, source_target_pairs={{0,2},{1,3},{2,0},{3,1},{4,6},{5,7},{6,4},{7,5},{8,10},{9,11},{10,... | collective-permute-start | bytes 98312 | tf_op jit(solution)/shard_map/ppermute | solution.py:304
  13.4 2.3 %collective-permute-start.2 = (bf16[2,64,128]{2,1,0:T(8,128)(2,1)S(1)}, bf16[2,64,128]{2,1,0:T(8,128)(2,1)S(1)}, u32[]{:S(2)}, u32[]{:S(2)}) collective-permute-start(bf16[2,64,128]{2,1,0:T(8,128)(2,1)S(1)} %get-tuple-element.37), channel_id=1, source_target_pairs={{0,2},{1,3},{2,0},{3,1},{4,6},{5,7},{6,4},{7,5},{8,10},{9,11},{10,... | collective-permute-start | bytes 98312 | tf_op jit(solution)/shard_map/ppermute | solution.py:304
  15.6 0.0 copy-done.7
  15.6 0.0 copy-done.6
  15.6 0.0 copy-done.9
  15.7 1.0 %shard_map.102 = (f32[2,128,128]{2,1,0:T(8,128)S(1)}, f32[2,128,128]{2,1,0:T(8,128)S(1)}) custom-call(s32[1,2]{1,0:T(1,128)S(1)} %copy-done.9, s32[4,128]{1,0:T(4,128)S(1)} %get-tuple-element.27.refs_0_.refs_1_.codes, f32[2,128,128]{2,1,0:T(8,128)S(1)} %copy-done.6, f32[128,128]{1,0:T(8,128)S(1)} %copy-done.7), custom_call_target="tpu_custom_call" | custom-call | tf_op jit(solution)/shard_map/pallas_call | solution.py:277
  16.7 1.6 %collective-permute-done.3.refs_9_ = bf16[2,64,128]{2,1,0:T(8,128)(2,1)S(1)} collective-permute-done((bf16[2,64,128]{2,1,0:T(8,128)(2,1)S(1)}, bf16[2,64,128]{2,1,0:T(8,128)(2,1)S(1)}, u32[]{:S(2)}, u32[]{:S(2)}) %collective-permute-start.3) | collective-permute-done | bytes 32800 | tf_op jit(solution)/shard_map/ppermute | solution.py:304
  18.2 0.4 collective-permute-done.2.refs_8_
  18.6 0.0 collective-permute-done.4.refs_10_
  18.6 0.0 collective-permute-done.5.refs_11_
  18.6 0.0 copy-done.1
  18.6 0.0 copy-done.3
  18.6 0.0 copy-done.4
  18.6 0.0 copy-done.5
  18.6 0.0 copy-done.2
  18.6 5.2 %shard_map.103 = (bf16[2,64,128]{2,1,0:T(8,128)(2,1)S(1)}, bf16[2,64,128]{2,1,0:T(8,128)(2,1)S(1)}, bf16[2,128,128]{2,1,0:T(8,128)(2,1)S(1)}, bf16[2,128,128]{2,1,0:T(8,128)(2,1)S(1)}, bf16[2,128,128]{2,1,0:T(8,128)(2,1)S(1)}) custom-call(s32[4,128]{1,0:T(4,128)S(1)} %get-tuple-element.27.refs_0_.refs_1_.codes, ...), custom_call_target="tpu_custom_call" | custom-call | tf_op jit(solution)/shard_map/pallas_call | solution.py:277
  23.8 3.4 %collective-permute-start.8 = (bf16[2,128,128]{2,1,0:T(8,128)(2,1)S(1)}, bf16[2,128,128]{2,1,0:T(8,128)(2,1)S(1)}, u32[]{:S(2)}, u32[]{:S(2)}) collective-permute-start(bf16[2,128,128]{2,1,0:T(8,128)(2,1)S(1)} %get-tuple-element.44), channel_id=1, source_target_pairs={{0,3},{1,2},{2,1},{3,0},{4,7},{5,6},{6,5},{7,4},{8,11},{9,10},{10,... | collective-permute-start | bytes 196616 | tf_op jit(solution)/shard_map/ppermute | solution.py:304
  27.2 0.0 collective-permute-start.9
  27.2 1.1 %collective-permute-start.6 = (bf16[2,64,128]{2,1,0:T(8,128)(2,1)S(1)}, bf16[2,64,128]{2,1,0:T(8,128)(2,1)S(1)}, u32[]{:S(2)}, u32[]{:S(2)}) collective-permute-start(bf16[2,64,128]{2,1,0:T(8,128)(2,1)S(1)} %get-tuple-element.42), channel_id=1, source_target_pairs={{0,2},{1,3},{2,0},{3,1},{4,6},{5,7},{6,4},{7,5},{8,10},{9,11},{10,... | collective-permute-start | bytes 98312 | tf_op jit(solution)/shard_map/ppermute | solution.py:304
  28.3 3.7 %collective-permute-done.6.early.refs_1_ = bf16[2,64,128]{2,1,0:T(8,128)(2,1)S(1)} collective-permute-done((bf16[2,64,128]{2,1,0:T(8,128)(2,1)S(1)}, bf16[2,64,128]{2,1,0:T(8,128)(2,1)S(1)}, u32[]{:S(2)}, u32[]{:S(2)}) %collective-permute-start.6) | collective-permute-done | bytes 32800 | tf_op jit(solution)/shard_map/ppermute | solution.py:304
  32.0 0.0 collective-permute-done.8.refs_0_.refs_2_
  32.0 0.0 collective-permute-done.9.refs_1_.refs_3_
  32.0 0.2 shard_map.105
  32.3 0.7 %collective-permute-start.10 = (bf16[2,1,64,512]{3,2,1,0:T(8,128)(2,1)S(1)}, bf16[2,1,64,512]{3,2,1,0:T(8,128)(2,1)S(1)}, u32[]{:S(2)}, u32[]{:S(2)}) collective-permute-start(bf16[2,1,64,512]{3,2,1,0:T(8,128)(2,1)S(1)} %get-tuple-element.47), channel_id=1, source_target_pairs={{0,28},{4,8},{8,4},{12,16},{16,12},{20,24},{24,20},{28,0},{1,29},{... | collective-permute-start | bytes 393224 | tf_op jit(solution)/shard_map/ppermute | solution.py:310
  33.0 0.7 %collective-permute-start.11 = (bf16[2,1,64,512]{3,2,1,0:T(8,128)(2,1)S(1)}, bf16[2,1,64,512]{3,2,1,0:T(8,128)(2,1)S(1)}, u32[]{:S(2)}, u32[]{:S(2)}) collective-permute-start(bf16[2,1,64,512]{3,2,1,0:T(8,128)(2,1)S(1)} %get-tuple-element.48), channel_id=1, source_target_pairs={{0,4},{4,0},{8,12},{12,8},{16,20},{20,16},{24,28},{28,24},{1,5},{5... | collective-permute-start | bytes 393224 | tf_op jit(solution)/shard_map/ppermute | solution.py:313
  33.7 1.9 %collective-permute-start.7 = (bf16[2,64,128]{2,1,0:T(8,128)(2,1)S(1)}, bf16[2,64,128]{2,1,0:T(8,128)(2,1)S(1)}, u32[]{:S(2)}, u32[]{:S(2)}) collective-permute-start(bf16[2,64,128]{2,1,0:T(8,128)(2,1)S(1)} %get-tuple-element.43), channel_id=1, source_target_pairs={{0,2},{1,3},{2,0},{3,1},{4,6},{5,7},{6,4},{7,5},{8,10},{9,11},{10,... | collective-permute-start | bytes 98312 | tf_op jit(solution)/shard_map/ppermute | solution.py:304
  35.7 3.2 %collective-permute-done.7.late = bf16[2,64,128]{2,1,0:T(8,128)(2,1)S(1)} collective-permute-done((bf16[2,64,128]{2,1,0:T(8,128)(2,1)S(1)}, bf16[2,64,128]{2,1,0:T(8,128)(2,1)S(1)}, u32[]{:S(2)}, u32[]{:S(2)}) %collective-permute-start.7) | collective-permute-done | bytes 32800 | tf_op jit(solution)/shard_map/ppermute | solution.py:304
  38.9 0.3 shard_map.104.own
  39.2 0.0 collective-permute-done.10.outer
  39.2 0.0 collective-permute-done.11.inner
  39.2 0.9 %shard_map.106 = f32[2,1,128,512]{3,2,1,0:T(8,128)} custom-call(f32[2,1,128,512]{3,2,1,0:T(8,128)S(1)} %shard_map.104.own, bf16[2,1,64,512]{3,2,1,0:T(8,128)(2,1)S(1)} %collective-permute-done.10.outer, bf16[2,1,64,512]{3,2,1,0:T(8,128)(2,1)S(1)} %collective-permute-done.11.inner), custom_call_target="tpu_custom_call" | custom-call | tf_op jit(solution)/shard_map/pallas_call | solution.py:277
  (4 shorter events, 0.0 us)
Async XLA Ops:
  0.0 5.2 %copy-start = (f32[2,1,128,512]{3,2,1,0:T(8,128)S(1)}, f32[2,1,128,512]{3,2,1,0:T(8,128)}, u32[]{:S(2)}) copy-start(f32[2,1,128,512]{3,2,1,0:T(8,128)} %refs_1_.1) | copy-start | bytes 1572868
  1.1 5.0 %collective-permute-start.1 = (bf16[2,1,64,512]{3,2,1,0:T(8,128)(2,1)S(1)}, bf16[2,1,64,512]{3,2,1,0:T(8,128)(2,1)S(1)}, u32[]{:S(2)}, u32[]{:S(2)}) collective-permute-start(bf16[2,1,64,512]{3,2,1,0:T(8,128)(2,1)S(1)} %get-tuple-element.49), channel_id=1, source_target_pairs={{0,4},{4,0},{8,12},{12,8},{16,20},{20,16},{24,28},{28,24},{1,5},{5... | collective-permute-start | bytes 393224 | tf_op jit(solution)/shard_map/ppermute | solution.py:313
  1.7 3.6 %copy-start.8 = (s32[4,2]{0,1:T(2,128)S(1)}, s32[4,2]{0,1:T(2,128)}, u32[]{:S(2)}) copy-start(s32[4,2]{0,1:T(2,128)} %param.14) | copy-start | bytes 100
  1.7 6.8 %collective-permute-start = (bf16[2,1,64,512]{3,2,1,0:T(8,128)(2,1)S(1)}, bf16[2,1,64,512]{3,2,1,0:T(8,128)(2,1)S(1)}, u32[]{:S(2)}, u32[]{:S(2)}) collective-permute-start(bf16[2,1,64,512]{3,2,1,0:T(8,128)(2,1)S(1)} %get-tuple-element.50), channel_id=1, source_target_pairs={{0,28},{4,8},{8,4},{12,16},{16,12},{20,24},{24,20},{28,0},{1,29},{... | collective-permute-start | bytes 393224 | tf_op jit(solution)/shard_map/ppermute | solution.py:310
  5.2 10.4 %copy-start.7 = (f32[128,128]{1,0:T(8,128)S(1)}, f32[128,128]{1,0:T(8,128)}, u32[]{:S(2)}) copy-start(f32[128,128]{1,0:T(8,128)} %refs_3_.1) | copy-start | bytes 196612
  8.5 7.2 %copy-start.6 = (f32[2,128,128]{2,1,0:T(8,128)S(1)}, f32[2,128,128]{2,1,0:T(8,128)}, u32[]{:S(2)}) copy-start(f32[2,128,128]{2,1,0:T(8,128)} %refs_2_) | copy-start | bytes 393220
  8.5 7.2 %copy-start.9 = (s32[1,2]{1,0:T(1,128)S(1)}, s32[1,2]{1,0:T(1,128)}, u32[]{:S(2)}) copy-start(s32[1,2]{1,0:T(1,128)} %refs_0_.1) | copy-start | bytes 28
  8.5 10.1 %copy-start.1 = (f32[4,128,128]{2,1,0:T(8,128)S(1)}, f32[4,128,128]{2,1,0:T(8,128)}, u32[]{:S(2)}) copy-start(f32[4,128,128]{2,1,0:T(8,128)} %refs_3_.2) | copy-start | bytes 786436
  8.5 10.1 %copy-start.3 = (bf16[256,256]{1,0:T(8,128)(2,1)S(1)}, bf16[256,256]{1,0:T(8,128)(2,1)}, u32[]{:S(2)}) copy-start(bf16[256,256]{1,0:T(8,128)(2,1)} %constant.30.clone.refs_6_) | copy-start | bytes 393220
  8.5 10.1 %copy-start.4 = (bf16[256,256]{1,0:T(8,128)(2,1)S(1)}, bf16[256,256]{1,0:T(8,128)(2,1)}, u32[]{:S(2)}) copy-start(bf16[256,256]{1,0:T(8,128)(2,1)} %constant.29.clone.refs_5_) | copy-start | bytes 393220
  8.5 10.1 %copy-start.5 = (bf16[256,256]{1,0:T(8,128)(2,1)S(1)}, bf16[256,256]{1,0:T(8,128)(2,1)}, u32[]{:S(2)}) copy-start(bf16[256,256]{1,0:T(8,128)(2,1)} %constant.28.clone.refs_4_) | copy-start | bytes 393220
  8.7 9.9 %copy-start.2 = (bf16[256,256]{1,0:T(8,128)(2,1)S(1)}, bf16[256,256]{1,0:T(8,128)(2,1)}, u32[]{:S(2)}) copy-start(bf16[256,256]{1,0:T(8,128)(2,1)} %constant.31.clone.refs_7_) | copy-start | bytes 393220
  8.7 9.9 %collective-permute-start.4 = (bf16[2,128,128]{2,1,0:T(8,128)(2,1)S(1)}, bf16[2,128,128]{2,1,0:T(8,128)(2,1)S(1)}, u32[]{:S(2)}, u32[]{:S(2)}) collective-permute-start(bf16[2,128,128]{2,1,0:T(8,128)(2,1)S(1)} %get-tuple-element.39), channel_id=1, source_target_pairs={{0,3},{1,2},{2,1},{3,0},{4,7},{5,6},{6,5},{7,4},{8,11},{9,10},{10,... | collective-permute-start | bytes 196616 | tf_op jit(solution)/shard_map/ppermute | solution.py:304
  12.7 5.9 %collective-permute-start.5 = (bf16[2,128,128]{2,1,0:T(8,128)(2,1)S(1)}, bf16[2,128,128]{2,1,0:T(8,128)(2,1)S(1)}, u32[]{:S(2)}, u32[]{:S(2)}) collective-permute-start(bf16[2,128,128]{2,1,0:T(8,128)(2,1)S(1)} %get-tuple-element.40), channel_id=1, source_target_pairs={{0,1},{1,0},{2,3},{3,2},{4,5},{5,4},{6,7},{7,6},{8,9},{9,8},{10,11... | collective-permute-start | bytes 196616 | tf_op jit(solution)/shard_map/ppermute | solution.py:304
  12.7 5.5 %collective-permute-start.3 = (bf16[2,64,128]{2,1,0:T(8,128)(2,1)S(1)}, bf16[2,64,128]{2,1,0:T(8,128)(2,1)S(1)}, u32[]{:S(2)}, u32[]{:S(2)}) collective-permute-start(bf16[2,64,128]{2,1,0:T(8,128)(2,1)S(1)} %get-tuple-element.38), channel_id=1, source_target_pairs={{0,2},{1,3},{2,0},{3,1},{4,6},{5,7},{6,4},{7,5},{8,10},{9,11},{10,... | collective-permute-start | bytes 98312 | tf_op jit(solution)/shard_map/ppermute | solution.py:304
  13.4 5.2 %collective-permute-start.2 = (bf16[2,64,128]{2,1,0:T(8,128)(2,1)S(1)}, bf16[2,64,128]{2,1,0:T(8,128)(2,1)S(1)}, u32[]{:S(2)}, u32[]{:S(2)}) collective-permute-start(bf16[2,64,128]{2,1,0:T(8,128)(2,1)S(1)} %get-tuple-element.37), channel_id=1, source_target_pairs={{0,2},{1,3},{2,0},{3,1},{4,6},{5,7},{6,4},{7,5},{8,10},{9,11},{10,... | collective-permute-start | bytes 98312 | tf_op jit(solution)/shard_map/ppermute | solution.py:304
  23.8 8.2 %collective-permute-start.8 = (bf16[2,128,128]{2,1,0:T(8,128)(2,1)S(1)}, bf16[2,128,128]{2,1,0:T(8,128)(2,1)S(1)}, u32[]{:S(2)}, u32[]{:S(2)}) collective-permute-start(bf16[2,128,128]{2,1,0:T(8,128)(2,1)S(1)} %get-tuple-element.44), channel_id=1, source_target_pairs={{0,3},{1,2},{2,1},{3,0},{4,7},{5,6},{6,5},{7,4},{8,11},{9,10},{10,... | collective-permute-start | bytes 196616 | tf_op jit(solution)/shard_map/ppermute | solution.py:304
  27.2 4.8 %collective-permute-start.9 = (bf16[2,128,128]{2,1,0:T(8,128)(2,1)S(1)}, bf16[2,128,128]{2,1,0:T(8,128)(2,1)S(1)}, u32[]{:S(2)}, u32[]{:S(2)}) collective-permute-start(bf16[2,128,128]{2,1,0:T(8,128)(2,1)S(1)} %get-tuple-element.45), channel_id=1, source_target_pairs={{0,1},{1,0},{2,3},{3,2},{4,5},{5,4},{6,7},{7,6},{8,9},{9,8},{10,11... | collective-permute-start | bytes 196616 | tf_op jit(solution)/shard_map/ppermute | solution.py:304
  27.2 4.8 %collective-permute-start.6 = (bf16[2,64,128]{2,1,0:T(8,128)(2,1)S(1)}, bf16[2,64,128]{2,1,0:T(8,128)(2,1)S(1)}, u32[]{:S(2)}, u32[]{:S(2)}) collective-permute-start(bf16[2,64,128]{2,1,0:T(8,128)(2,1)S(1)} %get-tuple-element.42), channel_id=1, source_target_pairs={{0,2},{1,3},{2,0},{3,1},{4,6},{5,7},{6,4},{7,5},{8,10},{9,11},{10,... | collective-permute-start | bytes 98312 | tf_op jit(solution)/shard_map/ppermute | solution.py:304
  32.3 7.0 %collective-permute-start.10 = (bf16[2,1,64,512]{3,2,1,0:T(8,128)(2,1)S(1)}, bf16[2,1,64,512]{3,2,1,0:T(8,128)(2,1)S(1)}, u32[]{:S(2)}, u32[]{:S(2)}) collective-permute-start(bf16[2,1,64,512]{3,2,1,0:T(8,128)(2,1)S(1)} %get-tuple-element.47), channel_id=1, source_target_pairs={{0,28},{4,8},{8,4},{12,16},{16,12},{20,24},{24,20},{28,0},{1,29},{... | collective-permute-start | bytes 393224 | tf_op jit(solution)/shard_map/ppermute | solution.py:310
  33.0 6.2 %collective-permute-start.11 = (bf16[2,1,64,512]{3,2,1,0:T(8,128)(2,1)S(1)}, bf16[2,1,64,512]{3,2,1,0:T(8,128)(2,1)S(1)}, u32[]{:S(2)}, u32[]{:S(2)}) collective-permute-start(bf16[2,1,64,512]{3,2,1,0:T(8,128)(2,1)S(1)} %get-tuple-element.48), channel_id=1, source_target_pairs={{0,4},{4,0},{8,12},{12,8},{16,20},{20,16},{24,28},{28,24},{1,5},{5... | collective-permute-start | bytes 393224 | tf_op jit(solution)/shard_map/ppermute | solution.py:313
  33.7 5.2 %collective-permute-start.7 = (bf16[2,64,128]{2,1,0:T(8,128)(2,1)S(1)}, bf16[2,64,128]{2,1,0:T(8,128)(2,1)S(1)}, u32[]{:S(2)}, u32[]{:S(2)}) collective-permute-start(bf16[2,64,128]{2,1,0:T(8,128)(2,1)S(1)} %get-tuple-element.43), channel_id=1, source_target_pairs={{0,2},{1,3},{2,0},{3,1},{4,6},{5,7},{6,4},{7,5},{8,10},{9,11},{10,... | collective-permute-start | bytes 98312 | tf_op jit(solution)/shard_map/ppermute | solution.py:304
where the time goes:
time: 40.3 us; the launch traced here: 40.1 us
  starting transfers between devices  18.9 us (47%)
  waiting for transfers between devices  11.2 us (28%)
  Pallas kernels  8.76 us (22%)
  other arithmetic  1.12 us (3%)
    ppermute x8, starting transfers between devices, swap(): return lax.ppermute(value, 'depth', [(d, d ^ mask) for d in range(depths)])  13.3 us
    ppermute x8, waiting for transfers between devices, swap(): return lax.ppermute(value, 'depth', [(d, d ^ mask) for d in range(depths)])  8.9 us
    pallas_call x7, Pallas kernels, call(): pl.pallas_call(kernel, out_shape=outs, in_specs=[SMEM] * scalars + [VMEM]...  8.76 us
    ppermute x2, starting transfers between devices, outward(): lax.ppermute(value, 'tile', [(t, (t - 1 + 2 * (t % 2)) % tiles) for t in...  4.27 us
    ppermute x2, waiting for transfers between devices, outward(): lax.ppermute(value, 'tile', [(t, (t - 1 + 2 * (t % 2)) % tiles) for t in...  2.28 us
    ppermute x2, starting transfers between devices, inward(): return lax.ppermute(value, 'tile', [(t, t ^ 1) for t in range(tiles)])  1.28 us
    convert_element_type x1, other arithmetic, shards(): inner = inward(jnp.where(odd, head, tail).astype(jnp.bfloat16))  1.12 us
  transfers between devices with their start and end apart: 12, of which 5 were waited for; matrix products, arithmetic and copies ran while one was open for 0% of the time, Pallas kernels for 6%

commit v1 on v0

--- a/solution.py
+++ b/solution.py
@@ -11,6 +11,9 @@
 BAND = 64
 LANES = 128
 SPAN = 1 << 16
+ORDER = (2, 3, 1, 0)
+EARLY = 2
+LATE = 2
 
 
 SMEM = pl.BlockSpec(memory_space=pltpu.SMEM)
@@ -58,7 +61,8 @@
     return jnp.where(lane < LANES - offset, left, right)
 
 
-def cut_kernel(order, tiles, positions, own, out, codes, early, wide):
+def cut_kernel(order, tiles, positions, own, out, codes, *refs):
+    early, wide = refs[:-1], refs[-1]
     strip, columns = own.shape[2:]
     window = out.shape[2]
     tile, depth = lax.axis_index("tile"), lax.axis_index("depth")
@@ -74,10 +78,10 @@
         offset = column - block * LANES
         for part in range(2):
             out[place, part] = turned_pair(wide, part, block, pl.ds(row, window), offset, lane)
-        if place == 0:
+        if place < len(early):
             half, _ = edge_half(row, strip)
             other = pl.multiple_of(window - BAND - half, BAND)
-            early[...] = out[0, :, pl.ds(other, BAND)].astype(early.dtype)
+            early[place][...] = out[place, :, pl.ds(other, BAND)].astype(jnp.bfloat16)
 
 
 def prep_kernel(strip, extents, codes, probe_wave, fresnel_phase, incident, turn):
@@ -116,7 +120,7 @@
         for part in range(2):
             band = turned_pair(wide, part, block, pl.ds(start, BAND), offset, lane)
             joined = jnp.where(outside, band, windows[place, part, pl.ds(half, BAND)]).astype(jnp.bfloat16)
-            if place == 0:
+            if out.shape[1] == BAND:
                 out[part] = joined
                 continue
             out[part, pl.ds(half, BAND)] = joined
@@ -160,8 +164,8 @@
 
 def wave_kernel(order, strip, codes, incident, turn, measured, *refs):
     depths = len(order)
-    matrices, arrived, outs = refs[:4], refs[4 : 5 + depths], refs[5 + depths : 6 + 2 * depths]
-    layers, waves = refs[6 + 2 * depths :]
+    matrices, refs, (layers, waves) = refs[:4], refs[4:-2], refs[-2:]
+    arrived, outs = refs[: len(refs) // 2], refs[len(refs) // 2 :]
     window = incident.shape[1]
     ahead = [matrices[0][...], matrices[1][...]]
     back = [matrices[2][...], matrices[3][...]]
@@ -176,10 +180,18 @@
     half, _ = edge_half(placed(codes, depths - 1)[0], strip)
     half = pl.multiple_of(half, BAND)
     other = pl.multiple_of(window - BAND - half, BAND)
-    for mask, value in zip(order[1:], arrived[2:]):
-        layers[depth ^ mask] = value[...].astype(jnp.float32)
-    layers[depth ^ order[0], :, pl.ds(half, BAND)] = arrived[0][...].astype(jnp.float32)
-    layers[depth ^ order[0], :, pl.ds(other, BAND)] = arrived[1][...].astype(jnp.float32)
+    whole = pl.ds(0, window)
+
+    def shares(values):
+        count = len(values) - depths
+        for place, value in enumerate(values):
+            split_place = place < 2 * count
+            mask = order[place % count] if split_place else order[place - count]
+            rows = whole if not split_place else pl.ds(half if place < count else other, BAND)
+            yield value, depth ^ mask, rows
+
+    for value, index, rows in shares(arrived):
+        layers[index, :, rows] = value[...].astype(jnp.float32)
     real, imag = incident[0], incident[1]
     cosine, sine = turn[0], turn[1]
     scale = 1.0 / window
@@ -206,10 +218,8 @@
                 False,
             )
             adjoint = inverse((real * cosine + imag * sine, imag * cosine - real * sine), False)
-    outs[0][...] = waves[depth ^ order[0], :, pl.ds(half, BAND)].astype(jnp.bfloat16)
-    outs[1][...] = waves[depth ^ order[0], :, pl.ds(other, BAND)].astype(jnp.bfloat16)
-    for mask, out in zip(order[1:], outs[2:]):
-        out[...] = waves[depth ^ mask].astype(jnp.bfloat16)
+    for value, index, rows in shares(outs):
+        value[...] = waves[index, :, rows].astype(jnp.bfloat16)
 
 
 def added(wide, part, block, rows, value, offset, lane):
@@ -230,7 +240,7 @@
         half, start = edge_half(row, strip)
         half = pl.multiple_of(half, BAND)
         for part in range(2):
-            piece = value[part] if place == 0 else value[part, pl.ds(half, BAND)]
+            piece = value[part] if value.shape[1] == BAND else value[part, pl.ds(half, BAND)]
             piece = piece.astype(jnp.float32)
             added(wide, part, block, pl.ds(start, BAND), piece, offset, lane)
     far = pl.multiple_of(odd * (strip + BAND), BAND)
@@ -242,22 +252,21 @@
             inner[part, 0, :, cols] = wide[part, block, pl.ds(near, BAND)].astype(jnp.bfloat16)
 
 
-def add_kernel(codes, early, late, *refs):
+def add_kernel(codes, *refs):
     arrived, (own, wide) = refs[:-2], refs[-2:]
     strip, columns = own.shape[2:]
-    window = arrived[0].shape[1]
+    window = arrived[-1].shape[1]
+    count = len(arrived) - codes.shape[0]
     wide[...] = jnp.zeros_like(wide)
     lane = lax.broadcasted_iota(jnp.int32, (window, LANES), 1)
-    row, block, offset = placed(codes, 0)
-    half, _ = edge_half(row, strip)
-    for value, start in ((early, half), (late, window - BAND - half)):
-        for part in range(2):
-            piece = value[part].astype(jnp.float32)
-            added(wide, part, block, pl.ds(row + start, BAND), piece, offset, lane[:BAND])
     for place, value in enumerate(arrived):
-        row, block, offset = placed(codes, place + 1)
-        for part in range(2):
-            added(wide, part, block, pl.ds(row, window), value[part].astype(jnp.float32), offset, lane)
+        length = value.shape[1]
+        row, block, offset = placed(codes, place % count if place < 2 * count else place - count)
+        if place < 2 * count:
+            half, _ = edge_half(row, strip)
+            row += half if place < count else window - BAND - half
+        for part in range(2):
+            added(wide, part, block, pl.ds(row, length), value[part].astype(jnp.float32), offset, lane[:length])
     for block in range(columns // LANES):
         for part in range(2):
             own[part, 0, :, block * LANES : (block + 1) * LANES] = wide[part, block, BAND : BAND + strip]
@@ -290,7 +299,7 @@
     window = probe_wave.shape[1]
     assert positions.shape[0] == depths == 4 and transmission.shape[1] == 1 and tiles % 2 == 0
     assert strip == 2 * BAND == window
-    order = (2, 3, 1, 0)
+    order = ORDER
     wide = [pltpu.VMEM((2, columns // LANES + 1, strip + 2 * BAND, LANES), jnp.float32)]
     patch = jax.ShapeDtypeStruct((2, window, window), jnp.bfloat16)
     band = jax.ShapeDtypeStruct((2, 1, BAND, columns), jnp.bfloat16)
@@ -316,20 +325,23 @@
     outer = outward(jnp.where(odd, tail, head).astype(jnp.bfloat16))
     inner = inward(jnp.where(odd, head, tail).astype(jnp.bfloat16))
     square = jax.ShapeDtypeStruct((2, window, window), jnp.float32)
-    windows, codes, early = call(
+    windows, codes, *early = call(
         lambda *refs: cut_kernel(order, tiles, *refs),
         [
             jax.ShapeDtypeStruct((depths, 2, window, window), jnp.float32),
             jax.ShapeDtypeStruct((depths, LANES), jnp.int32),
-            piece,
+            *[piece] * EARLY,
         ],
         [positions.T, transmission],
         wide,
         scalars=1,
     )
-    early = swap(early, order[0])
+    early = swapped(early)
     windows = call(
-        lambda *refs: join_kernel(strip, *refs), [piece] + [patch] * (depths - 1), [codes, windows, outer, inner], wide
+        lambda *refs: join_kernel(strip, *refs),
+        [piece] * EARLY + [patch] * (depths - EARLY),
+        [codes, windows, outer, inner],
+        wide,
     )
     probe_wave, fresnel_phase, windows = lax.optimization_barrier((probe_wave, fresnel_phase, windows))
     incident, turn = call(
@@ -339,18 +351,27 @@
         scalars=1,
     )
     windows = swapped(windows)
-    first, late, *pieces = call(
+    pieces = call(
         lambda *refs: wave_kernel(order, strip, *refs),
-        [piece] * 2 + [patch] * (depths - 1),
-        [codes, incident, turn, measured, *map(jnp.asarray, tables(window)), windows[0], early, *windows[1:]],
+        [piece] * (2 * LATE) + [patch] * (depths - LATE),
+        [
+            codes,
+            incident,
+            turn,
+            measured,
+            *map(jnp.asarray, tables(window)),
+            *windows[:EARLY],
+            *early,
+            *windows[EARLY:],
+        ],
         [pltpu.VMEM((depths, 2, window, window), jnp.float32)] * 2,
     )
-    first, *pieces = swapped([first, *pieces])
-    late = swap(late, order[0])
-    outer, inner = call(lambda *refs: shed_kernel(strip, *refs), [band] * 2, [codes, first, *pieces], wide)
+    late = swapped(pieces[LATE : 2 * LATE])
+    pieces = swapped([*pieces[:LATE], *pieces[2 * LATE :]])
+    outer, inner = call(lambda *refs: shed_kernel(strip, *refs), [band] * 2, [codes, *pieces], wide)
     outer, inner = outward(outer), inward(inner)
     total = jax.ShapeDtypeStruct(transmission.shape, jnp.float32)
-    own = call(add_kernel, total, [codes, first, late, *pieces], wide)
+    own = call(add_kernel, total, [codes, *pieces[:LATE], *late, *pieces[LATE:]], wide)
     return call(edge_kernel, total, [own, outer, inner])
 
 

time: 40.3 us -> 42.3 us (1.050)
  the two profiles are of different devices: /device:TPU:0 before, /device:TPU:2 now
where the time goes in v1:
time: 42.3 us; the launch traced here: 42.1 us
  starting transfers between devices  18.1 us (43%)
  waiting for transfers between devices  13.3 us (31%)
  Pallas kernels  8.77 us (21%)
  other arithmetic  1.12 us (3%)
  local copies, waits for them, and re-layouts  0.63 us (1%)
    ppermute x10, starting transfers between devices, swap(): return lax.ppermute(value, 'depth', [(d, d ^ mask) for d in range(depths)])  14.5 us
    ppermute x10, waiting for transfers between devices, swap(): return lax.ppermute(value, 'depth', [(d, d ^ mask) for d in range(depths)])  10.5 us
    pallas_call x7, Pallas kernels, call(): pl.pallas_call(kernel, out_shape=outs, in_specs=[SMEM] * scalars + [VMEM]...  8.77 us
    ppermute x2, starting transfers between devices, inward(): return lax.ppermute(value, 'tile', [(t, t ^ 1) for t in range(tiles)])  3.51 us
    ppermute x2, waiting for transfers between devices, outward(): lax.ppermute(value, 'tile', [(t, (t - 1 + 2 * (t % 2)) % tiles) for t in...  2.85 us
    convert_element_type x1, other arithmetic, shards(): inner = inward(jnp.where(odd, head, tail).astype(jnp.bfloat16))  1.12 us
  transfers between devices with their start and end apart: 14, of which 7 were waited for; matrix products, arithmetic and copies ran while one was open for 0% of the time, Pallas kernels for 5%

profile of v1, /device:TPU:2, one launch (start us, length us, event | category | flops | bytes accessed | tf_op | source)
XLA Modules:
  0.0 42.1 jit_solution(651276191751747164)
XLA Ops:
  0.0 1.1 %select_convert_fusion = (bf16[2,1,64,512]{3,2,1,0:T(8,128)(2,1)S(1)}, bf16[2,1,64,512]{3,2,1,0:T(8,128)(2,1)S(1)}) fusion(f32[2,1,128,512]{3,2,1,0:T(8,128)} %refs_1_.1, pred[]{:T(512)S(6)} %eq.5), kind=kLoop, calls=%fused_computation | loop fusion | flops 131072 | bytes 524289 | tf_op jit(solution)/shard_map/convert_element_type | solution.py:326
  1.1 0.1 collective-permute-start.1
  1.2 0.0 copy-start.8
  1.2 0.1 collective-permute-start
  1.3 0.0 copy-done
  1.3 0.6 %copy-done.8 = s32[4,2]{0,1:T(2,128)S(1)} copy-done((s32[4,2]{0,1:T(2,128)S(1)}, s32[4,2]{0,1:T(2,128)}, u32[]{:S(2)}) %copy-start.8) | copy-done | bytes 56
  1.9 0.9 %shard_map.100 = (f32[4,2,128,128]{3,2,1,0:T(8,128)S(1)}, s32[4,128]{1,0:T(4,128)S(1)}, bf16[2,64,128]{2,1,0:T(8,128)(2,1)S(1)}, bf16[2,64,128]{2,1,0:T(8,128)(2,1)S(1)}) custom-call(s32[2,4]{1,0:T(2,128)S(1)} %bitcast.1, f32[2,1,128,512]{3,2,1,0:T(8,128)S(1)} %copy-done), custom_call_target="tpu_custom_call" | custom-call | tf_op jit(solution)/shard_map/pallas_call | solution.py:286
  2.8 0.0 collective-permute-done.1.refs_3_
  2.8 2.8 %collective-permute-done.refs_2_ = bf16[2,1,64,512]{3,2,1,0:T(8,128)(2,1)S(1)} collective-permute-done((bf16[2,1,64,512]{3,2,1,0:T(8,128)(2,1)S(1)}, bf16[2,1,64,512]{3,2,1,0:T(8,128)(2,1)S(1)}, u32[]{:S(2)}, u32[]{:S(2)}) %collective-permute-start) | collective-permute-done | bytes 131104 | tf_op jit(solution)/shard_map/ppermute | solution.py:319
  5.7 0.0 copy-start.4
  5.7 0.0 copy-start.5
  5.7 0.2 shard_map.101
  5.9 0.0 copy-start.2
  5.9 1.6 %collective-permute-start.6 = (bf16[2,128,128]{2,1,0:T(8,128)(2,1)S(1)}, bf16[2,128,128]{2,1,0:T(8,128)(2,1)S(1)}, u32[]{:S(2)}, u32[]{:S(2)}) collective-permute-start(bf16[2,128,128]{2,1,0:T(8,128)(2,1)S(1)} %get-tuple-element.43), channel_id=1, source_target_pairs={{0,1},{1,0},{2,3},{3,2},{4,5},{5,4},{6,7},{7,6},{8,9},{9,8},{10,11... | collective-permute-start | bytes 196616 | tf_op jit(solution)/shard_map/ppermute | solution.py:313
  7.6 2.6 %collective-permute-start.4 = (bf16[2,64,128]{2,1,0:T(8,128)(2,1)S(1)}, bf16[2,64,128]{2,1,0:T(8,128)(2,1)S(1)}, u32[]{:S(2)}, u32[]{:S(2)}) collective-permute-start(bf16[2,64,128]{2,1,0:T(8,128)(2,1)S(1)} %get-tuple-element.41), channel_id=1, source_target_pairs={{0,2},{1,3},{2,0},{3,1},{4,6},{5,7},{6,4},{7,5},{8,10},{9,11},{10,... | collective-permute-start | bytes 98312 | tf_op jit(solution)/shard_map/ppermute | solution.py:313
  10.2 0.2 collective-permute-start.5
  10.4 1.7 %collective-permute-start.2 = (bf16[2,64,128]{2,1,0:T(8,128)(2,1)S(1)}, bf16[2,64,128]{2,1,0:T(8,128)(2,1)S(1)}, u32[]{:S(2)}, u32[]{:S(2)}) collective-permute-start(bf16[2,64,128]{2,1,0:T(8,128)(2,1)S(1)} %get-tuple-element.39), channel_id=1, source_target_pairs={{0,2},{1,3},{2,0},{3,1},{4,6},{5,7},{6,4},{7,5},{8,10},{9,11},{10,... | collective-permute-start | bytes 98312 | tf_op jit(solution)/shard_map/ppermute | solution.py:313
  12.1 1.9 %collective-permute-start.3 = (bf16[2,64,128]{2,1,0:T(8,128)(2,1)S(1)}, bf16[2,64,128]{2,1,0:T(8,128)(2,1)S(1)}, u32[]{:S(2)}, u32[]{:S(2)}) collective-permute-start(bf16[2,64,128]{2,1,0:T(8,128)(2,1)S(1)} %get-tuple-element.40), channel_id=1, source_target_pairs={{0,3},{1,2},{2,1},{3,0},{4,7},{5,6},{6,5},{7,4},{8,11},{9,10},{10,... | collective-permute-start | bytes 98312 | tf_op jit(solution)/shard_map/ppermute | solution.py:313
  14.0 0.0 copy-done.7
  14.0 0.0 copy-done.6
  14.0 0.0 copy-done.9
  14.0 1.0 %shard_map.102 = (f32[2,128,128]{2,1,0:T(8,128)S(1)}, f32[2,128,128]{2,1,0:T(8,128)S(1)}) custom-call(s32[1,2]{1,0:T(1,128)S(1)} %copy-done.9, s32[4,128]{1,0:T(4,128)S(1)} %get-tuple-element.29.refs_0_.refs_1_.codes, f32[2,128,128]{2,1,0:T(8,128)S(1)} %copy-done.6, f32[128,128]{1,0:T(8,128)S(1)} %copy-done.7), custom_call_target="tpu_custom_call" | custom-call | tf_op jit(solution)/shard_map/pallas_call | solution.py:286
  15.0 0.0 collective-permute-done.4.refs_10_
  15.0 1.0 %collective-permute-done.5.refs_11_ = bf16[2,64,128]{2,1,0:T(8,128)(2,1)S(1)} collective-permute-done((bf16[2,64,128]{2,1,0:T(8,128)(2,1)S(1)}, bf16[2,64,128]{2,1,0:T(8,128)(2,1)S(1)}, u32[]{:S(2)}, u32[]{:S(2)}) %collective-permute-start.5) | collective-permute-done | bytes 32800 | tf_op jit(solution)/shard_map/ppermute | solution.py:313
  16.0 0.0 collective-permute-done.2.refs_8_
  16.0 2.1 %collective-permute-done.3.refs_9_ = bf16[2,64,128]{2,1,0:T(8,128)(2,1)S(1)} collective-permute-done((bf16[2,64,128]{2,1,0:T(8,128)(2,1)S(1)}, bf16[2,64,128]{2,1,0:T(8,128)(2,1)S(1)}, u32[]{:S(2)}, u32[]{:S(2)}) %collective-permute-start.3) | collective-permute-done | bytes 32800 | tf_op jit(solution)/shard_map/ppermute | solution.py:313
  18.0 0.0 collective-permute-done.6.refs_12_
  18.0 0.0 copy-done.1
  18.0 0.0 copy-done.3
  18.1 0.0 copy-done.4
  18.1 5.2 %shard_map.103 = (bf16[2,64,128]{2,1,0:T(8,128)(2,1)S(1)}, bf16[2,64,128]{2,1,0:T(8,128)(2,1)S(1)}, bf16[2,64,128]{2,1,0:T(8,128)(2,1)S(1)}, bf16[2,64,128]{2,1,...) custom-call(s32[4,128]{1,0:T(4,128)S(1)} %get-tuple-element.29.refs_0_.refs_1_.codes, ...), custom_call_target="tpu_custom_call" | custom-call | tf_op jit(solution)/shard_map/pallas_call | solution.py:286
  23.3 1.4 %collective-permute-start.11 = (bf16[2,128,128]{2,1,0:T(8,128)(2,1)S(1)}, bf16[2,128,128]{2,1,0:T(8,128)(2,1)S(1)}, u32[]{:S(2)}, u32[]{:S(2)}) collective-permute-start(bf16[2,128,128]{2,1,0:T(8,128)(2,1)S(1)} %get-tuple-element.49), channel_id=1, source_target_pairs={{0,1},{1,0},{2,3},{3,2},{4,5},{5,4},{6,7},{7,6},{8,9},{9,8},{10,11... | collective-permute-start | bytes 196616 | tf_op jit(solution)/shard_map/ppermute | solution.py:313
  24.7 1.0 %collective-permute-start.7 = (bf16[2,64,128]{2,1,0:T(8,128)(2,1)S(1)}, bf16[2,64,128]{2,1,0:T(8,128)(2,1)S(1)}, u32[]{:S(2)}, u32[]{:S(2)}) collective-permute-start(bf16[2,64,128]{2,1,0:T(8,128)(2,1)S(1)} %get-tuple-element.45), channel_id=1, source_target_pairs={{0,2},{1,3},{2,0},{3,1},{4,6},{5,7},{6,4},{7,5},{8,10},{9,11},{10,... | collective-permute-start | bytes 98312 | tf_op jit(solution)/shard_map/ppermute | solution.py:313
  25.7 2.1 %collective-permute-start.8 = (bf16[2,64,128]{2,1,0:T(8,128)(2,1)S(1)}, bf16[2,64,128]{2,1,0:T(8,128)(2,1)S(1)}, u32[]{:S(2)}, u32[]{:S(2)}) collective-permute-start(bf16[2,64,128]{2,1,0:T(8,128)(2,1)S(1)} %get-tuple-element.46), channel_id=1, source_target_pairs={{0,3},{1,2},{2,1},{3,0},{4,7},{5,6},{6,5},{7,4},{8,11},{9,10},{10,... | collective-permute-start | bytes 98312 | tf_op jit(solution)/shard_map/ppermute | solution.py:313
  27.7 2.5 %collective-permute-done.7.refs_0_.refs_1_ = bf16[2,64,128]{2,1,0:T(8,128)(2,1)S(1)} collective-permute-done((bf16[2,64,128]{2,1,0:T(8,128)(2,1)S(1)}, bf16[2,64,128]{2,1,0:T(8,128)(2,1)S(1)}, u32[]{:S(2)}, u32[]{:S(2)}) %collective-permute-start.7) | collective-permute-done | bytes 32800 | tf_op jit(solution)/shard_map/ppermute | solution.py:313
  30.2 1.2 %collective-permute-done.8.refs_1_.refs_2_ = bf16[2,64,128]{2,1,0:T(8,128)(2,1)S(1)} collective-permute-done((bf16[2,64,128]{2,1,0:T(8,128)(2,1)S(1)}, bf16[2,64,128]{2,1,0:T(8,128)(2,1)S(1)}, u32[]{:S(2)}, u32[]{:S(2)}) %collective-permute-start.8) | collective-permute-done | bytes 32800 | tf_op jit(solution)/shard_map/ppermute | solution.py:313
  31.4 0.0 collective-permute-done.11.refs_4_.refs_3_
  31.4 0.2 shard_map.105
  31.6 0.1 collective-permute-start.12
  31.7 3.4 %collective-permute-start.13 = (bf16[2,1,64,512]{3,2,1,0:T(8,128)(2,1)S(1)}, bf16[2,1,64,512]{3,2,1,0:T(8,128)(2,1)S(1)}, u32[]{:S(2)}, u32[]{:S(2)}) collective-permute-start(bf16[2,1,64,512]{3,2,1,0:T(8,128)(2,1)S(1)} %get-tuple-element.52), channel_id=1, source_target_pairs={{0,4},{4,0},{8,12},{12,8},{16,20},{20,16},{24,28},{28,24},{1,5},{5... | collective-permute-start | bytes 393224 | tf_op jit(solution)/shard_map/ppermute | solution.py:322
  35.1 0.0 collective-permute-start.9
  35.1 1.9 %collective-permute-start.10 = (bf16[2,64,128]{2,1,0:T(8,128)(2,1)S(1)}, bf16[2,64,128]{2,1,0:T(8,128)(2,1)S(1)}, u32[]{:S(2)}, u32[]{:S(2)}) collective-permute-start(bf16[2,64,128]{2,1,0:T(8,128)(2,1)S(1)} %get-tuple-element.48), channel_id=1, source_target_pairs={{0,3},{1,2},{2,1},{3,0},{4,7},{5,6},{6,5},{7,4},{8,11},{9,10},{10,... | collective-permute-start | bytes 98312 | tf_op jit(solution)/shard_map/ppermute | solution.py:313
  37.1 3.4 %collective-permute-done.9.refs_2_ = bf16[2,64,128]{2,1,0:T(8,128)(2,1)S(1)} collective-permute-done((bf16[2,64,128]{2,1,0:T(8,128)(2,1)S(1)}, bf16[2,64,128]{2,1,0:T(8,128)(2,1)S(1)}, u32[]{:S(2)}, u32[]{:S(2)}) %collective-permute-start.9) | collective-permute-done | bytes 32800 | tf_op jit(solution)/shard_map/ppermute | solution.py:313
  40.4 0.4 %collective-permute-done.10.refs_3_ = bf16[2,64,128]{2,1,0:T(8,128)(2,1)S(1)} collective-permute-done((bf16[2,64,128]{2,1,0:T(8,128)(2,1)S(1)}, bf16[2,64,128]{2,1,0:T(8,128)(2,1)S(1)}, u32[]{:S(2)}, u32[]{:S(2)}) %collective-permute-start.10) | collective-permute-done | bytes 32800 | tf_op jit(solution)/shard_map/ppermute | solution.py:313
  40.9 0.3 shard_map.104.own
  41.2 0.0 collective-permute-done.12.outer
  41.2 0.0 collective-permute-done.13.inner
  41.2 0.9 %shard_map.106 = f32[2,1,128,512]{3,2,1,0:T(8,128)} custom-call(f32[2,1,128,512]{3,2,1,0:T(8,128)S(1)} %shard_map.104.own, bf16[2,1,64,512]{3,2,1,0:T(8,128)(2,1)S(1)} %collective-permute-done.12.outer, bf16[2,1,64,512]{3,2,1,0:T(8,128)(2,1)S(1)} %collective-permute-done.13.inner), custom_call_target="tpu_custom_call" | custom-call | tf_op jit(solution)/shard_map/pallas_call | solution.py:286
  (8 shorter events, 0.0 us)
Async XLA Ops:
  0.0 1.3 %copy-start = (f32[2,1,128,512]{3,2,1,0:T(8,128)S(1)}, f32[2,1,128,512]{3,2,1,0:T(8,128)}, u32[]{:S(2)}) copy-start(f32[2,1,128,512]{3,2,1,0:T(8,128)} %refs_1_.1) | copy-start | bytes 1572868
  1.1 1.7 %collective-permute-start.1 = (bf16[2,1,64,512]{3,2,1,0:T(8,128)(2,1)S(1)}, bf16[2,1,64,512]{3,2,1,0:T(8,128)(2,1)S(1)}, u32[]{:S(2)}, u32[]{:S(2)}) collective-permute-start(bf16[2,1,64,512]{3,2,1,0:T(8,128)(2,1)S(1)} %get-tuple-element.53), channel_id=1, source_target_pairs={{0,4},{4,0},{8,12},{12,8},{16,20},{20,16},{24,28},{28,24},{1,5},{5... | collective-permute-start | bytes 393224 | tf_op jit(solution)/shard_map/ppermute | solution.py:322
  1.2 0.7 %copy-start.8 = (s32[4,2]{0,1:T(2,128)S(1)}, s32[4,2]{0,1:T(2,128)}, u32[]{:S(2)}) copy-start(s32[4,2]{0,1:T(2,128)} %param.14) | copy-start | bytes 100
  1.2 4.5 %collective-permute-start = (bf16[2,1,64,512]{3,2,1,0:T(8,128)(2,1)S(1)}, bf16[2,1,64,512]{3,2,1,0:T(8,128)(2,1)S(1)}, u32[]{:S(2)}, u32[]{:S(2)}) collective-permute-start(bf16[2,1,64,512]{3,2,1,0:T(8,128)(2,1)S(1)} %get-tuple-element.54), channel_id=1, source_target_pairs={{0,28},{4,8},{8,4},{12,16},{16,12},{20,24},{24,20},{28,0},{1,29},{... | collective-permute-start | bytes 393224 | tf_op jit(solution)/shard_map/ppermute | solution.py:319
  1.9 12.1 %copy-start.7 = (f32[128,128]{1,0:T(8,128)S(1)}, f32[128,128]{1,0:T(8,128)}, u32[]{:S(2)}) copy-start(f32[128,128]{1,0:T(8,128)} %refs_3_.1) | copy-start | bytes 196612
  5.7 8.3 %copy-start.6 = (f32[2,128,128]{2,1,0:T(8,128)S(1)}, f32[2,128,128]{2,1,0:T(8,128)}, u32[]{:S(2)}) copy-start(f32[2,128,128]{2,1,0:T(8,128)} %refs_2_) | copy-start | bytes 393220
  5.7 8.3 %copy-start.9 = (s32[1,2]{1,0:T(1,128)S(1)}, s32[1,2]{1,0:T(1,128)}, u32[]{:S(2)}) copy-start(s32[1,2]{1,0:T(1,128)} %refs_0_.1) | copy-start | bytes 28
  5.7 12.4 %copy-start.1 = (f32[4,128,128]{2,1,0:T(8,128)S(1)}, f32[4,128,128]{2,1,0:T(8,128)}, u32[]{:S(2)}) copy-start(f32[4,128,128]{2,1,0:T(8,128)} %refs_3_.2) | copy-start | bytes 786436
  5.7 12.4 %copy-start.3 = (bf16[256,256]{1,0:T(8,128)(2,1)S(1)}, bf16[256,256]{1,0:T(8,128)(2,1)}, u32[]{:S(2)}) copy-start(bf16[256,256]{1,0:T(8,128)(2,1)} %constant.30.clone.refs_6_) | copy-start | bytes 393220
  5.7 12.4 %copy-start.4 = (bf16[256,256]{1,0:T(8,128)(2,1)S(1)}, bf16[256,256]{1,0:T(8,128)(2,1)}, u32[]{:S(2)}) copy-start(bf16[256,256]{1,0:T(8,128)(2,1)} %constant.29.clone.refs_5_) | copy-start | bytes 393220
  5.7 12.4 %copy-start.5 = (bf16[256,256]{1,0:T(8,128)(2,1)S(1)}, bf16[256,256]{1,0:T(8,128)(2,1)}, u32[]{:S(2)}) copy-start(bf16[256,256]{1,0:T(8,128)(2,1)} %constant.28.clone.refs_4_) | copy-start | bytes 393220
  5.9 12.2 %copy-start.2 = (bf16[256,256]{1,0:T(8,128)(2,1)S(1)}, bf16[256,256]{1,0:T(8,128)(2,1)}, u32[]{:S(2)}) copy-start(bf16[256,256]{1,0:T(8,128)(2,1)} %constant.31.clone.refs_7_) | copy-start | bytes 393220
  5.9 12.1 %collective-permute-start.6 = (bf16[2,128,128]{2,1,0:T(8,128)(2,1)S(1)}, bf16[2,128,128]{2,1,0:T(8,128)(2,1)S(1)}, u32[]{:S(2)}, u32[]{:S(2)}) collective-permute-start(bf16[2,128,128]{2,1,0:T(8,128)(2,1)S(1)} %get-tuple-element.43), channel_id=1, source_target_pairs={{0,1},{1,0},{2,3},{3,2},{4,5},{5,4},{6,7},{7,6},{8,9},{9,8},{10,11... | collective-permute-start | bytes 196616 | tf_op jit(solution)/shard_map/ppermute | solution.py:313
  7.6 7.4 %collective-permute-start.4 = (bf16[2,64,128]{2,1,0:T(8,128)(2,1)S(1)}, bf16[2,64,128]{2,1,0:T(8,128)(2,1)S(1)}, u32[]{:S(2)}, u32[]{:S(2)}) collective-permute-start(bf16[2,64,128]{2,1,0:T(8,128)(2,1)S(1)} %get-tuple-element.41), channel_id=1, source_target_pairs={{0,2},{1,3},{2,0},{3,1},{4,6},{5,7},{6,4},{7,5},{8,10},{9,11},{10,... | collective-permute-start | bytes 98312 | tf_op jit(solution)/shard_map/ppermute | solution.py:313
  10.2 5.8 %collective-permute-start.5 = (bf16[2,64,128]{2,1,0:T(8,128)(2,1)S(1)}, bf16[2,64,128]{2,1,0:T(8,128)(2,1)S(1)}, u32[]{:S(2)}, u32[]{:S(2)}) collective-permute-start(bf16[2,64,128]{2,1,0:T(8,128)(2,1)S(1)} %get-tuple-element.42), channel_id=1, source_target_pairs={{0,3},{1,2},{2,1},{3,0},{4,7},{5,6},{6,5},{7,4},{8,11},{9,10},{10,... | collective-permute-start | bytes 98312 | tf_op jit(solution)/shard_map/ppermute | solution.py:313
  10.4 5.6 %collective-permute-start.2 = (bf16[2,64,128]{2,1,0:T(8,128)(2,1)S(1)}, bf16[2,64,128]{2,1,0:T(8,128)(2,1)S(1)}, u32[]{:S(2)}, u32[]{:S(2)}) collective-permute-start(bf16[2,64,128]{2,1,0:T(8,128)(2,1)S(1)} %get-tuple-element.39), channel_id=1, source_target_pairs={{0,2},{1,3},{2,0},{3,1},{4,6},{5,7},{6,4},{7,5},{8,10},{9,11},{10,... | collective-permute-start | bytes 98312 | tf_op jit(solution)/shard_map/ppermute | solution.py:313
  12.1 6.0 %collective-permute-start.3 = (bf16[2,64,128]{2,1,0:T(8,128)(2,1)S(1)}, bf16[2,64,128]{2,1,0:T(8,128)(2,1)S(1)}, u32[]{:S(2)}, u32[]{:S(2)}) collective-permute-start(bf16[2,64,128]{2,1,0:T(8,128)(2,1)S(1)} %get-tuple-element.40), channel_id=1, source_target_pairs={{0,3},{1,2},{2,1},{3,0},{4,7},{5,6},{6,5},{7,4},{8,11},{9,10},{10,... | collective-permute-start | bytes 98312 | tf_op jit(solution)/shard_map/ppermute | solution.py:313
  23.3 8.1 %collective-permute-start.11 = (bf16[2,128,128]{2,1,0:T(8,128)(2,1)S(1)}, bf16[2,128,128]{2,1,0:T(8,128)(2,1)S(1)}, u32[]{:S(2)}, u32[]{:S(2)}) collective-permute-start(bf16[2,128,128]{2,1,0:T(8,128)(2,1)S(1)} %get-tuple-element.49), channel_id=1, source_target_pairs={{0,1},{1,0},{2,3},{3,2},{4,5},{5,4},{6,7},{7,6},{8,9},{9,8},{10,11... | collective-permute-start | bytes 196616 | tf_op jit(solution)/shard_map/ppermute | solution.py:313
  24.7 5.5 %collective-permute-start.7 = (bf16[2,64,128]{2,1,0:T(8,128)(2,1)S(1)}, bf16[2,64,128]{2,1,0:T(8,128)(2,1)S(1)}, u32[]{:S(2)}, u32[]{:S(2)}) collective-permute-start(bf16[2,64,128]{2,1,0:T(8,128)(2,1)S(1)} %get-tuple-element.45), channel_id=1, source_target_pairs={{0,2},{1,3},{2,0},{3,1},{4,6},{5,7},{6,4},{7,5},{8,10},{9,11},{10,... | collective-permute-start | bytes 98312 | tf_op jit(solution)/shard_map/ppermute | solution.py:313
  25.7 5.7 %collective-permute-start.8 = (bf16[2,64,128]{2,1,0:T(8,128)(2,1)S(1)}, bf16[2,64,128]{2,1,0:T(8,128)(2,1)S(1)}, u32[]{:S(2)}, u32[]{:S(2)}) collective-permute-start(bf16[2,64,128]{2,1,0:T(8,128)(2,1)S(1)} %get-tuple-element.46), channel_id=1, source_target_pairs={{0,3},{1,2},{2,1},{3,0},{4,7},{5,6},{6,5},{7,4},{8,11},{9,10},{10,... | collective-permute-start | bytes 98312 | tf_op jit(solution)/shard_map/ppermute | solution.py:313
  31.6 9.6 %collective-permute-start.12 = (bf16[2,1,64,512]{3,2,1,0:T(8,128)(2,1)S(1)}, bf16[2,1,64,512]{3,2,1,0:T(8,128)(2,1)S(1)}, u32[]{:S(2)}, u32[]{:S(2)}) collective-permute-start(bf16[2,1,64,512]{3,2,1,0:T(8,128)(2,1)S(1)} %get-tuple-element.51), channel_id=1, source_target_pairs={{0,28},{4,8},{8,4},{12,16},{16,12},{20,24},{24,20},{28,0},{1,29},{... | collective-permute-start | bytes 393224 | tf_op jit(solution)/shard_map/ppermute | solution.py:319
  31.7 9.5 %collective-permute-start.13 = (bf16[2,1,64,512]{3,2,1,0:T(8,128)(2,1)S(1)}, bf16[2,1,64,512]{3,2,1,0:T(8,128)(2,1)S(1)}, u32[]{:S(2)}, u32[]{:S(2)}) collective-permute-start(bf16[2,1,64,512]{3,2,1,0:T(8,128)(2,1)S(1)} %get-tuple-element.52), channel_id=1, source_target_pairs={{0,4},{4,0},{8,12},{12,8},{16,20},{20,16},{24,28},{28,24},{1,5},{5... | collective-permute-start | bytes 393224 | tf_op jit(solution)/shard_map/ppermute | solution.py:322
  35.1 5.3 %collective-permute-start.9 = (bf16[2,64,128]{2,1,0:T(8,128)(2,1)S(1)}, bf16[2,64,128]{2,1,0:T(8,128)(2,1)S(1)}, u32[]{:S(2)}, u32[]{:S(2)}) collective-permute-start(bf16[2,64,128]{2,1,0:T(8,128)(2,1)S(1)} %get-tuple-element.47), channel_id=1, source_target_pairs={{0,2},{1,3},{2,0},{3,1},{4,6},{5,7},{6,4},{7,5},{8,10},{9,11},{10,... | collective-permute-start | bytes 98312 | tf_op jit(solution)/shard_map/ppermute | solution.py:313
  35.1 5.7 %collective-permute-start.10 = (bf16[2,64,128]{2,1,0:T(8,128)(2,1)S(1)}, bf16[2,64,128]{2,1,0:T(8,128)(2,1)S(1)}, u32[]{:S(2)}, u32[]{:S(2)}) collective-permute-start(bf16[2,64,128]{2,1,0:T(8,128)(2,1)S(1)} %get-tuple-element.48), channel_id=1, source_target_pairs={{0,3},{1,2},{2,1},{3,0},{4,7},{5,6},{6,5},{7,4},{8,11},{9,10},{10,... | collective-permute-start | bytes 98312 | tf_op jit(solution)/shard_map/ppermute | solution.py:313

commit v2 on v1

--- a/solution.py
+++ b/solution.py
@@ -12,12 +12,13 @@
 LANES = 128
 SPAN = 1 << 16
 ORDER = (2, 3, 1, 0)
-EARLY = 2
+EARLY = 3
 LATE = 2
 
 
 SMEM = pl.BlockSpec(memory_space=pltpu.SMEM)
 VMEM = pl.BlockSpec(memory_space=pltpu.VMEM)
+HBM = pl.BlockSpec(memory_space=pltpu.HBM)
 PARAMS = pltpu.CompilerParams(vmem_limit_bytes=12 << 20)
 
 
@@ -61,21 +62,38 @@
     return jnp.where(lane < LANES - offset, left, right)
 
 
-def cut_kernel(order, tiles, positions, own, out, codes, *refs):
+def band_kernel(order, tiles, positions_in, own, strip_out, outer, inner, codes, positions, sems):
+    strip = strip_out.shape[2]
+    tile, depth = lax.axis_index("tile"), lax.axis_index("depth")
+    odd = lax.rem(tile, 2)
+    outs, copies = (outer, inner), []
+    for index, side in enumerate((odd, 1 - odd)):
+        rows = pl.ds(pl.multiple_of(side * (strip - BAND), BAND), BAND)
+        copies.append(pltpu.make_async_copy(own.at[:, :, rows], strip_out.at[:, :, rows], sems.at[index]))
+        copies[-1].start()
+    fetch = pltpu.make_async_copy(positions_in, positions, sems.at[2])
+    fetch.start()
+    fetch.wait()
+    for place, mask in enumerate(order):
+        probe = depth ^ mask
+        row = first_row(positions, probe, tile, strip, tiles)
+        codes[place : place + 1] = jnp.full((1, LANES), row * SPAN + positions[1, probe], jnp.int32)
+    for copy, side, out in zip(copies, (odd, 1 - odd), outs):
+        copy.wait()
+        rows = pl.ds(pl.multiple_of(side * (strip - BAND), BAND), BAND)
+        out[...] = strip_out[:, :, rows].astype(jnp.bfloat16)
+
+
+def cut_kernel(codes, own, out, *refs):
     early, wide = refs[:-1], refs[-1]
     strip, columns = own.shape[2:]
     window = out.shape[2]
-    tile, depth = lax.axis_index("tile"), lax.axis_index("depth")
     for block in range(columns // LANES):
         for part in range(2):
             wide[part, block, BAND : BAND + strip] = own[part, 0, :, block * LANES : (block + 1) * LANES]
     lane = lax.broadcasted_iota(jnp.int32, (window, LANES), 1)
-    for place, mask in enumerate(order):
-        probe = depth ^ mask
-        row, column = first_row(positions, probe, tile, strip, tiles), positions[1, probe]
-        codes[place : place + 1] = jnp.full((1, LANES), row * SPAN + column, jnp.int32)
-        block = lax.div(column, LANES)
-        offset = column - block * LANES
+    for place in range(out.shape[0]):
+        row, block, offset = placed(codes, place)
         for part in range(2):
             out[place, part] = turned_pair(wide, part, block, pl.ds(row, window), offset, lane)
         if place < len(early):
@@ -165,7 +183,7 @@
 def wave_kernel(order, strip, codes, incident, turn, measured, *refs):
     depths = len(order)
     matrices, refs, (layers, waves) = refs[:4], refs[4:-2], refs[-2:]
-    arrived, outs = refs[: len(refs) // 2], refs[len(refs) // 2 :]
+    arrived, outs = refs[: depths + EARLY], refs[depths + EARLY :]
     window = incident.shape[1]
     ahead = [matrices[0][...], matrices[1][...]]
     back = [matrices[2][...], matrices[3][...]]
@@ -272,14 +290,26 @@
             own[part, 0, :, block * LANES : (block + 1) * LANES] = wide[part, block, BAND : BAND + strip]
 
 
-def edge_kernel(own, outer, inner, out):
-    strip = own.shape[2]
+def edge_kernel(side, own, band, *refs):
+    out, summed, sem = refs[-3:]
     odd = lax.rem(lax.axis_index("tile"), 2)
-    out[...] = own[...]
-    far = pl.multiple_of(odd * (strip - BAND), BAND)
-    near = pl.multiple_of((1 - odd) * (strip - BAND), BAND)
-    out[:, :, pl.ds(far, BAND)] += outer[...].astype(jnp.float32)
-    out[:, :, pl.ds(near, BAND)] += inner[...].astype(jnp.float32)
+    rows = pl.ds(pl.multiple_of((odd if side == 0 else 1 - odd) * (own.shape[2] - BAND), BAND), BAND)
+    summed[...] = own[:, :, rows] + band[...].astype(jnp.float32)
+    copy = pltpu.make_async_copy(summed, out.at[:, :, rows], sem)
+    copy.start()
+    copy.wait()
+
+
+def edge(side, own, band, *partial):
+    return pl.pallas_call(
+        lambda *refs: edge_kernel(side, *refs),
+        out_shape=jax.ShapeDtypeStruct(own.shape, own.dtype),
+        in_specs=[VMEM, VMEM] + [HBM] * len(partial),
+        out_specs=HBM,
+        scratch_shapes=[pltpu.VMEM(band.shape, own.dtype), pltpu.SemaphoreType.DMA],
+        input_output_aliases={2: 0} if partial else {},
+        compiler_params=PARAMS,
+    )(own, band, *partial)
 
 
 def call(kernel, outs, operands, scratch=(), scalars=0):
@@ -303,7 +333,6 @@
     wide = [pltpu.VMEM((2, columns // LANES + 1, strip + 2 * BAND, LANES), jnp.float32)]
     patch = jax.ShapeDtypeStruct((2, window, window), jnp.bfloat16)
     band = jax.ShapeDtypeStruct((2, 1, BAND, columns), jnp.bfloat16)
-    odd = lax.axis_index("tile") % 2 == 1
 
     piece = jax.ShapeDtypeStruct((2, BAND, window), jnp.bfloat16)
 
@@ -321,21 +350,21 @@
     def inward(value):
         return lax.ppermute(value, "tile", [(t, t ^ 1) for t in range(tiles)])
 
-    head, tail = transmission[:, :, :BAND], transmission[:, :, strip - BAND :]
-    outer = outward(jnp.where(odd, tail, head).astype(jnp.bfloat16))
-    inner = inward(jnp.where(odd, head, tail).astype(jnp.bfloat16))
+    places = jax.ShapeDtypeStruct((depths, LANES), jnp.int32)
+    total = jax.ShapeDtypeStruct(transmission.shape, jnp.float32)
+    own, outer, inner, codes = pl.pallas_call(
+        lambda *refs: band_kernel(order, tiles, *refs),
+        out_shape=[total, band, band, places],
+        in_specs=[HBM, HBM],
+        out_specs=[VMEM] * 4,
+        scratch_shapes=[pltpu.SMEM((2, depths), jnp.int32), pltpu.SemaphoreType.DMA((3,))],
+        compiler_params=PARAMS,
+        name="bands",
+    )(*(pltpu.with_memory_space_constraint(v, pltpu.HBM) for v in (positions.T, transmission)))
+    outer, inner = outward(outer), inward(inner)
     square = jax.ShapeDtypeStruct((2, window, window), jnp.float32)
-    windows, codes, *early = call(
-        lambda *refs: cut_kernel(order, tiles, *refs),
-        [
-            jax.ShapeDtypeStruct((depths, 2, window, window), jnp.float32),
-            jax.ShapeDtypeStruct((depths, LANES), jnp.int32),
-            *[piece] * EARLY,
-        ],
-        [positions.T, transmission],
-        wide,
-        scalars=1,
-    )
+    full = jax.ShapeDtypeStruct((depths, 2, window, window), jnp.float32)
+    windows, *early = call(cut_kernel, [full] + [piece] * EARLY, [codes, own], wide)
     early = swapped(early)
     windows = call(
         lambda *refs: join_kernel(strip, *refs),
@@ -370,9 +399,8 @@
     pieces = swapped([*pieces[:LATE], *pieces[2 * LATE :]])
     outer, inner = call(lambda *refs: shed_kernel(strip, *refs), [band] * 2, [codes, *pieces], wide)
     outer, inner = outward(outer), inward(inner)
-    total = jax.ShapeDtypeStruct(transmission.shape, jnp.float32)
     own = call(add_kernel, total, [codes, *pieces[:LATE], *late, *pieces[LATE:]], wide)
-    return call(edge_kernel, total, [own, outer, inner])
+    return edge(0, own, outer, edge(1, own, inner))
 
 
 def solution(mesh):

time: 42.3 us -> 41.2 us (0.974)
  the two profiles are of different devices: /device:TPU:2 before, /device:TPU:0 now
where the time goes in v2:
time: 41.2 us; the launch traced here: 41.1 us
  starting transfers between devices  19.8 us (48%)
  waiting for transfers between devices  11.1 us (27%)
  Pallas kernels  9.9 us (24%)
    ppermute x11, starting transfers between devices, swap(): return lax.ppermute(value, 'depth', [(d, d ^ mask) for d in range(depths)])  14.8 us
    ppermute x11, waiting for transfers between devices, swap(): return lax.ppermute(value, 'depth', [(d, d ^ mask) for d in range(depths)])  11.1 us
    pallas_call x6, Pallas kernels, call(): pl.pallas_call(kernel, out_shape=outs, in_specs=[SMEM] * scalars + [VMEM]...  7.34 us
    ppermute x2, starting transfers between devices, outward(): lax.ppermute(value, 'tile', [(t, (t - 1 + 2 * (t % 2)) % tiles) for t in...  4.96 us
    pallas_call x2, Pallas kernels, edge(): pl.pallas_call(lambda *refs: edge_kernel(side, *refs), out_shape=jax.Shap...  1.49 us
    pallas_call x1, Pallas kernels, shards(): pl.pallas_call(lambda *refs: band_kernel(order, tiles, *refs), out_shape=...  1.07 us
  transfers between devices with their start and end apart: 15, of which 6 were waited for; matrix products, arithmetic and copies ran while one was open for 0% of the time, Pallas kernels for 7%

profile of v2, /device:TPU:0, one launch (start us, length us, event | category | flops | bytes accessed | tf_op | source)
XLA Modules:
  0.0 41.1 jit_solution(15099157707045328967)
XLA Ops:
  0.0 1.1 %bands.1 = (f32[2,1,128,512]{3,2,1,0:T(8,128)S(1)}, bf16[2,1,64,512]{3,2,1,0:T(8,128)(2,1)S(1)}, bf16[2,1,64,512]{3,2,1,0:T(8,128)(2,1)S(1)}, s32[4,128]{1,0:T(4,128)S(1)}) custom-call(s32[2,4]{1,0:T(2,128)} %bitcast.1, f32[2,1,128,512]{3,2,1,0:T(8,128)} %refs_1_.1), custom_call_target="tpu_custom_call" | custom-call | tf_op jit(solution)/shard_map/bands/pallas_call | solution.py:355
  1.1 3.4 %collective-permute-start = (bf16[2,1,64,512]{3,2,1,0:T(8,128)(2,1)S(1)}, bf16[2,1,64,512]{3,2,1,0:T(8,128)(2,1)S(1)}, u32[]{:S(2)}, u32[]{:S(2)}) collective-permute-start(bf16[2,1,64,512]{3,2,1,0:T(8,128)(2,1)S(1)} %get-tuple-element.36), channel_id=1, source_target_pairs={{0,28},{4,8},{8,4},{12,16},{16,12},{20,24},{24,20},{28,0},{1,29},{... | collective-permute-start | bytes 393224 | tf_op jit(solution)/shard_map/ppermute | solution.py:348
  4.5 0.0 collective-permute-start.1
  4.5 0.4 shard_map.100
  4.9 2.7 %collective-permute-start.5 = (bf16[2,64,128]{2,1,0:T(8,128)(2,1)S(1)}, bf16[2,64,128]{2,1,0:T(8,128)(2,1)S(1)}, u32[]{:S(2)}, u32[]{:S(2)}) collective-permute-start(bf16[2,64,128]{2,1,0:T(8,128)(2,1)S(1)} %get-tuple-element.49), channel_id=1, source_target_pairs={{0,2},{1,3},{2,0},{3,1},{4,6},{5,7},{6,4},{7,5},{8,10},{9,11},{10,... | collective-permute-start | bytes 98312 | tf_op jit(solution)/shard_map/ppermute | solution.py:342
  7.6 1.3 %collective-permute-start.6 = (bf16[2,64,128]{2,1,0:T(8,128)(2,1)S(1)}, bf16[2,64,128]{2,1,0:T(8,128)(2,1)S(1)}, u32[]{:S(2)}, u32[]{:S(2)}) collective-permute-start(bf16[2,64,128]{2,1,0:T(8,128)(2,1)S(1)} %get-tuple-element.50), channel_id=1, source_target_pairs={{0,3},{1,2},{2,1},{3,0},{4,7},{5,6},{6,5},{7,4},{8,11},{9,10},{10,... | collective-permute-start | bytes 98312 | tf_op jit(solution)/shard_map/ppermute | solution.py:342
  8.9 0.2 collective-permute-start.7
  9.1 0.0 collective-permute-done.refs_2_
  9.1 0.0 collective-permute-done.1.refs_3_
  9.2 0.0 copy-start.7
  9.2 0.0 copy-start
  9.2 0.0 copy-start.2
  9.2 0.0 copy-start.3
  9.2 0.0 copy-start.4
  9.2 0.2 shard_map.101
  9.4 0.0 copy-start.1
  9.4 2.9 %collective-permute-start.2 = (bf16[2,64,128]{2,1,0:T(8,128)(2,1)S(1)}, bf16[2,64,128]{2,1,0:T(8,128)(2,1)S(1)}, u32[]{:S(2)}, u32[]{:S(2)}) collective-permute-start(bf16[2,64,128]{2,1,0:T(8,128)(2,1)S(1)} %get-tuple-element.46), channel_id=1, source_target_pairs={{0,2},{1,3},{2,0},{3,1},{4,6},{5,7},{6,4},{7,5},{8,10},{9,11},{10,... | collective-permute-start | bytes 98312 | tf_op jit(solution)/shard_map/ppermute | solution.py:342
  12.3 1.3 %collective-permute-start.3 = (bf16[2,64,128]{2,1,0:T(8,128)(2,1)S(1)}, bf16[2,64,128]{2,1,0:T(8,128)(2,1)S(1)}, u32[]{:S(2)}, u32[]{:S(2)}) collective-permute-start(bf16[2,64,128]{2,1,0:T(8,128)(2,1)S(1)} %get-tuple-element.47), channel_id=1, source_target_pairs={{0,3},{1,2},{2,1},{3,0},{4,7},{5,6},{6,5},{7,4},{8,11},{9,10},{10,... | collective-permute-start | bytes 98312 | tf_op jit(solution)/shard_map/ppermute | solution.py:342
  13.7 0.0 collective-permute-done.5.refs_11_
  13.7 0.1 collective-permute-start.4
  13.7 0.0 copy-done.6
  13.7 0.0 copy-done.7
  13.7 1.0 %shard_map.102 = (f32[2,128,128]{2,1,0:T(8,128)S(1)}, f32[2,128,128]{2,1,0:T(8,128)S(1)}) custom-call(s32[1,2]{1,0:T(1,128)S(1)} %copy-done.7, s32[4,128]{1,0:T(4,128)S(1)} %get-tuple-element.33.codes.refs_0_.refs_1_, f32[2,128,128]{2,1,0:T(8,128)S(1)} %copy-done.5, f32[128,128]{1,0:T(8,128)S(1)} %copy-done.6), custom_call_target="tpu_custom_call" | custom-call | tf_op jit(solution)/shard_map/pallas_call | solution.py:316
  14.7 0.0 collective-permute-done.6.refs_12_
  14.7 0.0 collective-permute-done.7.refs_13_
  14.8 0.1 collective-permute-done.2.refs_8_
  14.9 3.2 %collective-permute-done.3.refs_9_ = bf16[2,64,128]{2,1,0:T(8,128)(2,1)S(1)} collective-permute-done((bf16[2,64,128]{2,1,0:T(8,128)(2,1)S(1)}, bf16[2,64,128]{2,1,0:T(8,128)(2,1)S(1)}, u32[]{:S(2)}, u32[]{:S(2)}) %collective-permute-start.3) | collective-permute-done | bytes 32800 | tf_op jit(solution)/shard_map/ppermute | solution.py:342
  18.0 0.0 collective-permute-done.4.refs_10_
  18.0 0.0 copy-done
  18.1 5.2 %shard_map.103 = (bf16[2,64,128]{2,1,0:T(8,128)(2,1)S(1)}, bf16[2,64,128]{2,1,0:T(8,128)(2,1)S(1)}, bf16[2,64,128]{2,1,0:T(8,128)(2,1)S(1)}, bf16[2,64,128]{2,1,...) custom-call(s32[4,128]{1,0:T(4,128)S(1)} %get-tuple-element.33.codes.refs_0_.refs_1_, ...), custom_call_target="tpu_custom_call" | custom-call | tf_op jit(solution)/shard_map/pallas_call | solution.py:316
  23.2 0.1 collective-permute-start.12
  23.3 2.6 %collective-permute-start.8 = (bf16[2,64,128]{2,1,0:T(8,128)(2,1)S(1)}, bf16[2,64,128]{2,1,0:T(8,128)(2,1)S(1)}, u32[]{:S(2)}, u32[]{:S(2)}) collective-permute-start(bf16[2,64,128]{2,1,0:T(8,128)(2,1)S(1)} %get-tuple-element.53), channel_id=1, source_target_pairs={{0,2},{1,3},{2,0},{3,1},{4,6},{5,7},{6,4},{7,5},{8,10},{9,11},{10,... | collective-permute-start | bytes 98312 | tf_op jit(solution)/shard_map/ppermute | solution.py:342
  25.9 1.8 %collective-permute-start.9 = (bf16[2,64,128]{2,1,0:T(8,128)(2,1)S(1)}, bf16[2,64,128]{2,1,0:T(8,128)(2,1)S(1)}, u32[]{:S(2)}, u32[]{:S(2)}) collective-permute-start(bf16[2,64,128]{2,1,0:T(8,128)(2,1)S(1)} %get-tuple-element.54), channel_id=1, source_target_pairs={{0,3},{1,2},{2,1},{3,0},{4,7},{5,6},{6,5},{7,4},{8,11},{9,10},{10,... | collective-permute-start | bytes 98312 | tf_op jit(solution)/shard_map/ppermute | solution.py:342
  27.7 0.5 %collective-permute-done.8.refs_0_.refs_1_ = bf16[2,64,128]{2,1,0:T(8,128)(2,1)S(1)} collective-permute-done((bf16[2,64,128]{2,1,0:T(8,128)(2,1)S(1)}, bf16[2,64,128]{2,1,0:T(8,128)(2,1)S(1)}, u32[]{:S(2)}, u32[]{:S(2)}) %collective-permute-start.8) | collective-permute-done | bytes 32800 | tf_op jit(solution)/shard_map/ppermute | solution.py:342
  28.2 3.4 %collective-permute-done.9.refs_1_.refs_2_ = bf16[2,64,128]{2,1,0:T(8,128)(2,1)S(1)} collective-permute-done((bf16[2,64,128]{2,1,0:T(8,128)(2,1)S(1)}, bf16[2,64,128]{2,1,0:T(8,128)(2,1)S(1)}, u32[]{:S(2)}, u32[]{:S(2)}) %collective-permute-start.9) | collective-permute-done | bytes 32800 | tf_op jit(solution)/shard_map/ppermute | solution.py:342
  31.6 0.0 collective-permute-done.12.refs_4_.refs_3_
  31.6 0.2 shard_map.105
  31.8 0.1 collective-permute-start.14
  31.9 1.5 %collective-permute-start.13 = (bf16[2,1,64,512]{3,2,1,0:T(8,128)(2,1)S(1)}, bf16[2,1,64,512]{3,2,1,0:T(8,128)(2,1)S(1)}, u32[]{:S(2)}, u32[]{:S(2)}) collective-permute-start(bf16[2,1,64,512]{3,2,1,0:T(8,128)(2,1)S(1)} %get-tuple-element.59), channel_id=1, source_target_pairs={{0,28},{4,8},{8,4},{12,16},{16,12},{20,24},{24,20},{28,0},{1,29},{... | collective-permute-start | bytes 393224 | tf_op jit(solution)/shard_map/ppermute | solution.py:348
  33.5 0.0 collective-permute-start.10
  33.5 1.8 %collective-permute-start.11 = (bf16[2,64,128]{2,1,0:T(8,128)(2,1)S(1)}, bf16[2,64,128]{2,1,0:T(8,128)(2,1)S(1)}, u32[]{:S(2)}, u32[]{:S(2)}) collective-permute-start(bf16[2,64,128]{2,1,0:T(8,128)(2,1)S(1)} %get-tuple-element.56), channel_id=1, source_target_pairs={{0,3},{1,2},{2,1},{3,0},{4,7},{5,6},{6,5},{7,4},{8,11},{9,10},{10,... | collective-permute-start | bytes 98312 | tf_op jit(solution)/shard_map/ppermute | solution.py:342
  35.3 3.3 %collective-permute-done.10.refs_2_ = bf16[2,64,128]{2,1,0:T(8,128)(2,1)S(1)} collective-permute-done((bf16[2,64,128]{2,1,0:T(8,128)(2,1)S(1)}, bf16[2,64,128]{2,1,0:T(8,128)(2,1)S(1)}, u32[]{:S(2)}, u32[]{:S(2)}) %collective-permute-start.10) | collective-permute-done | bytes 32800 | tf_op jit(solution)/shard_map/ppermute | solution.py:342
  38.6 0.6 %collective-permute-done.11.refs_3_ = bf16[2,64,128]{2,1,0:T(8,128)(2,1)S(1)} collective-permute-done((bf16[2,64,128]{2,1,0:T(8,128)(2,1)S(1)}, bf16[2,64,128]{2,1,0:T(8,128)(2,1)S(1)}, u32[]{:S(2)}, u32[]{:S(2)}) %collective-permute-start.11) | collective-permute-done | bytes 32800 | tf_op jit(solution)/shard_map/ppermute | solution.py:342
  39.2 0.3 shard_map.104.refs_0_
  39.6 0.0 collective-permute-done.14.refs_1_
  39.6 0.7 %shard_map.106.refs_2_ = f32[2,1,128,512]{3,2,1,0:T(8,128)} custom-call(f32[2,1,128,512]{3,2,1,0:T(8,128)S(1)} %shard_map.104.refs_0_, bf16[2,1,64,512]{3,2,1,0:T(8,128)(2,1)S(1)} %collective-permute-done.14.refs_1_), custom_call_target="tpu_custom_call" | custom-call | tf_op jit(solution)/shard_map/pallas_call | solution.py:304
  40.3 0.0 collective-permute-done.13.refs_1_
  40.3 0.7 %shard_map.107 = f32[2,1,128,512]{3,2,1,0:T(8,128)} custom-call(f32[2,1,128,512]{3,2,1,0:T(8,128)S(1)} %shard_map.104.refs_0_, bf16[2,1,64,512]{3,2,1,0:T(8,128)(2,1)S(1)} %collective-permute-done.13.refs_1_, f32[2,1,128,512]{3,2,1,0:T(8,128)} %shard_map.106.refs_2_), custom_call_target="tpu_custom_call", output_to_operand_aliasing={{}: (2, {})} | custom-call | tf_op jit(solution)/shard_map/pallas_call | solution.py:304
  (7 shorter events, 0.0 us)
Async XLA Ops:
  1.1 8.1 %collective-permute-start = (bf16[2,1,64,512]{3,2,1,0:T(8,128)(2,1)S(1)}, bf16[2,1,64,512]{3,2,1,0:T(8,128)(2,1)S(1)}, u32[]{:S(2)}, u32[]{:S(2)}) collective-permute-start(bf16[2,1,64,512]{3,2,1,0:T(8,128)(2,1)S(1)} %get-tuple-element.36), channel_id=1, source_target_pairs={{0,28},{4,8},{8,4},{12,16},{16,12},{20,24},{24,20},{28,0},{1,29},{... | collective-permute-start | bytes 393224 | tf_op jit(solution)/shard_map/ppermute | solution.py:348
  4.5 4.6 %collective-permute-start.1 = (bf16[2,1,64,512]{3,2,1,0:T(8,128)(2,1)S(1)}, bf16[2,1,64,512]{3,2,1,0:T(8,128)(2,1)S(1)}, u32[]{:S(2)}, u32[]{:S(2)}) collective-permute-start(bf16[2,1,64,512]{3,2,1,0:T(8,128)(2,1)S(1)} %get-tuple-element.37), channel_id=1, source_target_pairs={{0,4},{4,0},{8,12},{12,8},{16,20},{20,16},{24,28},{28,24},{1,5},{5... | collective-permute-start | bytes 393224 | tf_op jit(solution)/shard_map/ppermute | solution.py:351
  4.5 9.2 %copy-start.6 = (f32[128,128]{1,0:T(8,128)S(1)}, f32[128,128]{1,0:T(8,128)}, u32[]{:S(2)}) copy-start(f32[128,128]{1,0:T(8,128)} %refs_3_.1) | copy-start | bytes 196612
  4.9 8.7 %collective-permute-start.5 = (bf16[2,64,128]{2,1,0:T(8,128)(2,1)S(1)}, bf16[2,64,128]{2,1,0:T(8,128)(2,1)S(1)}, u32[]{:S(2)}, u32[]{:S(2)}) collective-permute-start(bf16[2,64,128]{2,1,0:T(8,128)(2,1)S(1)} %get-tuple-element.49), channel_id=1, source_target_pairs={{0,2},{1,3},{2,0},{3,1},{4,6},{5,7},{6,4},{7,5},{8,10},{9,11},{10,... | collective-permute-start | bytes 98312 | tf_op jit(solution)/shard_map/ppermute | solution.py:342
  7.6 7.2 %collective-permute-start.6 = (bf16[2,64,128]{2,1,0:T(8,128)(2,1)S(1)}, bf16[2,64,128]{2,1,0:T(8,128)(2,1)S(1)}, u32[]{:S(2)}, u32[]{:S(2)}) collective-permute-start(bf16[2,64,128]{2,1,0:T(8,128)(2,1)S(1)} %get-tuple-element.50), channel_id=1, source_target_pairs={{0,3},{1,2},{2,1},{3,0},{4,7},{5,6},{6,5},{7,4},{8,11},{9,10},{10,... | collective-permute-start | bytes 98312 | tf_op jit(solution)/shard_map/ppermute | solution.py:342
  8.9 5.8 %collective-permute-start.7 = (bf16[2,64,128]{2,1,0:T(8,128)(2,1)S(1)}, bf16[2,64,128]{2,1,0:T(8,128)(2,1)S(1)}, u32[]{:S(2)}, u32[]{:S(2)}) collective-permute-start(bf16[2,64,128]{2,1,0:T(8,128)(2,1)S(1)} %get-tuple-element.51), channel_id=1, source_target_pairs={{0,1},{1,0},{2,3},{3,2},{4,5},{5,4},{6,7},{7,6},{8,9},{9,8},{10,11... | collective-permute-start | bytes 98312 | tf_op jit(solution)/shard_map/ppermute | solution.py:342
  9.1 4.6 %copy-start.5 = (f32[2,128,128]{2,1,0:T(8,128)S(1)}, f32[2,128,128]{2,1,0:T(8,128)}, u32[]{:S(2)}) copy-start(f32[2,128,128]{2,1,0:T(8,128)} %refs_2_) | copy-start | bytes 393220
  9.2 4.6 %copy-start.7 = (s32[1,2]{1,0:T(1,128)S(1)}, s32[1,2]{1,0:T(1,128)}, u32[]{:S(2)}) copy-start(s32[1,2]{1,0:T(1,128)} %refs_0_.1) | copy-start | bytes 28
  9.2 8.9 %copy-start = (f32[4,128,128]{2,1,0:T(8,128)S(1)}, f32[4,128,128]{2,1,0:T(8,128)}, u32[]{:S(2)}) copy-start(f32[4,128,128]{2,1,0:T(8,128)} %refs_3_.2) | copy-start | bytes 786436
  9.2 8.8 %copy-start.2 = (bf16[256,256]{1,0:T(8,128)(2,1)S(1)}, bf16[256,256]{1,0:T(8,128)(2,1)}, u32[]{:S(2)}) copy-start(bf16[256,256]{1,0:T(8,128)(2,1)} %constant.10.clone.refs_6_) | copy-start | bytes 393220
  9.2 8.8 %copy-start.3 = (bf16[256,256]{1,0:T(8,128)(2,1)S(1)}, bf16[256,256]{1,0:T(8,128)(2,1)}, u32[]{:S(2)}) copy-start(bf16[256,256]{1,0:T(8,128)(2,1)} %constant.9.clone.refs_5_) | copy-start | bytes 393220
  9.2 8.8 %copy-start.4 = (bf16[256,256]{1,0:T(8,128)(2,1)S(1)}, bf16[256,256]{1,0:T(8,128)(2,1)}, u32[]{:S(2)}) copy-start(bf16[256,256]{1,0:T(8,128)(2,1)} %constant.8.clone.refs_4_) | copy-start | bytes 393220
  9.4 8.6 %copy-start.1 = (bf16[256,256]{1,0:T(8,128)(2,1)S(1)}, bf16[256,256]{1,0:T(8,128)(2,1)}, u32[]{:S(2)}) copy-start(bf16[256,256]{1,0:T(8,128)(2,1)} %constant.11.clone.refs_7_) | copy-start | bytes 393220
  9.4 5.4 %collective-permute-start.2 = (bf16[2,64,128]{2,1,0:T(8,128)(2,1)S(1)}, bf16[2,64,128]{2,1,0:T(8,128)(2,1)S(1)}, u32[]{:S(2)}, u32[]{:S(2)}) collective-permute-start(bf16[2,64,128]{2,1,0:T(8,128)(2,1)S(1)} %get-tuple-element.46), channel_id=1, source_target_pairs={{0,2},{1,3},{2,0},{3,1},{4,6},{5,7},{6,4},{7,5},{8,10},{9,11},{10,... | collective-permute-start | bytes 98312 | tf_op jit(solution)/shard_map/ppermute | solution.py:342
  12.3 5.7 %collective-permute-start.3 = (bf16[2,64,128]{2,1,0:T(8,128)(2,1)S(1)}, bf16[2,64,128]{2,1,0:T(8,128)(2,1)S(1)}, u32[]{:S(2)}, u32[]{:S(2)}) collective-permute-start(bf16[2,64,128]{2,1,0:T(8,128)(2,1)S(1)} %get-tuple-element.47), channel_id=1, source_target_pairs={{0,3},{1,2},{2,1},{3,0},{4,7},{5,6},{6,5},{7,4},{8,11},{9,10},{10,... | collective-permute-start | bytes 98312 | tf_op jit(solution)/shard_map/ppermute | solution.py:342
  13.7 4.4 %collective-permute-start.4 = (bf16[2,64,128]{2,1,0:T(8,128)(2,1)S(1)}, bf16[2,64,128]{2,1,0:T(8,128)(2,1)S(1)}, u32[]{:S(2)}, u32[]{:S(2)}) collective-permute-start(bf16[2,64,128]{2,1,0:T(8,128)(2,1)S(1)} %get-tuple-element.48), channel_id=1, source_target_pairs={{0,1},{1,0},{2,3},{3,2},{4,5},{5,4},{6,7},{7,6},{8,9},{9,8},{10,11... | collective-permute-start | bytes 98312 | tf_op jit(solution)/shard_map/ppermute | solution.py:342
  23.2 8.4 %collective-permute-start.12 = (bf16[2,128,128]{2,1,0:T(8,128)(2,1)S(1)}, bf16[2,128,128]{2,1,0:T(8,128)(2,1)S(1)}, u32[]{:S(2)}, u32[]{:S(2)}) collective-permute-start(bf16[2,128,128]{2,1,0:T(8,128)(2,1)S(1)} %get-tuple-element.57), channel_id=1, source_target_pairs={{0,1},{1,0},{2,3},{3,2},{4,5},{5,4},{6,7},{7,6},{8,9},{9,8},{10,11... | collective-permute-start | bytes 196616 | tf_op jit(solution)/shard_map/ppermute | solution.py:342
  23.3 4.9 %collective-permute-start.8 = (bf16[2,64,128]{2,1,0:T(8,128)(2,1)S(1)}, bf16[2,64,128]{2,1,0:T(8,128)(2,1)S(1)}, u32[]{:S(2)}, u32[]{:S(2)}) collective-permute-start(bf16[2,64,128]{2,1,0:T(8,128)(2,1)S(1)} %get-tuple-element.53), channel_id=1, source_target_pairs={{0,2},{1,3},{2,0},{3,1},{4,6},{5,7},{6,4},{7,5},{8,10},{9,11},{10,... | collective-permute-start | bytes 98312 | tf_op jit(solution)/shard_map/ppermute | solution.py:342
  25.9 5.7 %collective-permute-start.9 = (bf16[2,64,128]{2,1,0:T(8,128)(2,1)S(1)}, bf16[2,64,128]{2,1,0:T(8,128)(2,1)S(1)}, u32[]{:S(2)}, u32[]{:S(2)}) collective-permute-start(bf16[2,64,128]{2,1,0:T(8,128)(2,1)S(1)} %get-tuple-element.54), channel_id=1, source_target_pairs={{0,3},{1,2},{2,1},{3,0},{4,7},{5,6},{6,5},{7,4},{8,11},{9,10},{10,... | collective-permute-start | bytes 98312 | tf_op jit(solution)/shard_map/ppermute | solution.py:342
  31.8 7.7 %collective-permute-start.14 = (bf16[2,1,64,512]{3,2,1,0:T(8,128)(2,1)S(1)}, bf16[2,1,64,512]{3,2,1,0:T(8,128)(2,1)S(1)}, u32[]{:S(2)}, u32[]{:S(2)}) collective-permute-start(bf16[2,1,64,512]{3,2,1,0:T(8,128)(2,1)S(1)} %get-tuple-element.60), channel_id=1, source_target_pairs={{0,4},{4,0},{8,12},{12,8},{16,20},{20,16},{24,28},{28,24},{1,5},{5... | collective-permute-start | bytes 393224 | tf_op jit(solution)/shard_map/ppermute | solution.py:351
  31.9 8.4 %collective-permute-start.13 = (bf16[2,1,64,512]{3,2,1,0:T(8,128)(2,1)S(1)}, bf16[2,1,64,512]{3,2,1,0:T(8,128)(2,1)S(1)}, u32[]{:S(2)}, u32[]{:S(2)}) collective-permute-start(bf16[2,1,64,512]{3,2,1,0:T(8,128)(2,1)S(1)} %get-tuple-element.59), channel_id=1, source_target_pairs={{0,28},{4,8},{8,4},{12,16},{16,12},{20,24},{24,20},{28,0},{1,29},{... | collective-permute-start | bytes 393224 | tf_op jit(solution)/shard_map/ppermute | solution.py:348
  33.5 5.1 %collective-permute-start.10 = (bf16[2,64,128]{2,1,0:T(8,128)(2,1)S(1)}, bf16[2,64,128]{2,1,0:T(8,128)(2,1)S(1)}, u32[]{:S(2)}, u32[]{:S(2)}) collective-permute-start(bf16[2,64,128]{2,1,0:T(8,128)(2,1)S(1)} %get-tuple-element.55), channel_id=1, source_target_pairs={{0,2},{1,3},{2,0},{3,1},{4,6},{5,7},{6,4},{7,5},{8,10},{9,11},{10,... | collective-permute-start | bytes 98312 | tf_op jit(solution)/shard_map/ppermute | solution.py:342
  33.5 5.7 %collective-permute-start.11 = (bf16[2,64,128]{2,1,0:T(8,128)(2,1)S(1)}, bf16[2,64,128]{2,1,0:T(8,128)(2,1)S(1)}, u32[]{:S(2)}, u32[]{:S(2)}) collective-permute-start(bf16[2,64,128]{2,1,0:T(8,128)(2,1)S(1)} %get-tuple-element.56), channel_id=1, source_target_pairs={{0,3},{1,2},{2,1},{3,0},{4,7},{5,6},{6,5},{7,4},{8,11},{9,10},{10,... | collective-permute-start | bytes 98312 | tf_op jit(solution)/shard_map/ppermute | solution.py:342

commit v3 on v2

--- a/solution.py
+++ b/solution.py
@@ -102,13 +102,14 @@
             early[place][...] = out[place, :, pl.ds(other, BAND)].astype(jnp.bfloat16)
 
 
-def prep_kernel(strip, extents, codes, probe_wave, fresnel_phase, incident, turn):
+def prep_kernel(strip, extents, codes, probe_wave, fresnel_phase, incident, turn, upper):
     window = probe_wave.shape[1]
     row, _, _ = placed(codes, codes.shape[0] - 1)
     line = row - BAND + lax.broadcasted_iota(jnp.int32, (window, window), 0)
     inside = (line >= -extents[0, 0]) & (line < strip + extents[0, 1])
     for part in range(2):
         incident[part] = jnp.where(inside, probe_wave[part], 0.0)
+    upper[...] = jnp.full(upper.shape, row < BAND).astype(jnp.float32)
     scale = 1.0 / window**2
     turn[0] = jnp.cos(fresnel_phase[...]) * scale
     turn[1] = jnp.sin(fresnel_phase[...]) * scale
@@ -168,19 +169,15 @@
 
 
 def from_right(real, imag, matrix, exact):
-    size = real.shape[0]
-    stacked = jnp.concatenate([real, imag], axis=1)
+    stacked = jnp.concatenate([real, imag], axis=1).astype(jnp.bfloat16)
+    product = dot(stacked, matrix[0])
     if exact:
-        high, low = split(stacked)
-        both = dot(jnp.concatenate([high, low], axis=0), matrix[0])
-        stacked = both[:size] + both[size:] + dot(high, matrix[1])
-    else:
-        stacked = dot(stacked.astype(jnp.bfloat16), matrix[0])
+        product += dot(stacked, matrix[1])
     half = real.shape[1]
-    return stacked[:, :half], stacked[:, half:]
-
-
-def wave_kernel(order, strip, codes, incident, turn, measured, *refs):
+    return product[:, :half], product[:, half:]
+
+
+def wave_kernel(order, incident, turn, upper, measured, *refs):
     depths = len(order)
     matrices, refs, (layers, waves) = refs[:4], refs[4:-2], refs[-2:]
     arrived, outs = refs[: depths + EARLY], refs[depths + EARLY :]
@@ -195,21 +192,15 @@
     def inverse(value, exact):
         return from_right(*from_left(*value, back, exact), ahead, exact)
 
-    half, _ = edge_half(placed(codes, depths - 1)[0], strip)
-    half = pl.multiple_of(half, BAND)
-    other = pl.multiple_of(window - BAND - half, BAND)
-    whole = pl.ds(0, window)
-
-    def shares(values):
-        count = len(values) - depths
-        for place, value in enumerate(values):
-            split_place = place < 2 * count
-            mask = order[place % count] if split_place else order[place - count]
-            rows = whole if not split_place else pl.ds(half if place < count else other, BAND)
-            yield value, depth ^ mask, rows
-
-    for value, index, rows in shares(arrived):
-        layers[index, :, rows] = value[...].astype(jnp.float32)
+    above = upper[...] != 0.0
+    for place, mask in enumerate(order):
+        index = depth ^ mask
+        if place < EARLY:
+            edge_rows, own_rows = (arrived[p][...].astype(jnp.float32) for p in (place, EARLY + place))
+            layers[index, :, :BAND] = jnp.where(above, edge_rows, own_rows)
+            layers[index, :, BAND:] = jnp.where(above, own_rows, edge_rows)
+        else:
+            layers[index] = arrived[EARLY + place][...].astype(jnp.float32)
     real, imag = incident[0], incident[1]
     cosine, sine = turn[0], turn[1]
     scale = 1.0 / window
@@ -236,8 +227,14 @@
                 False,
             )
             adjoint = inverse((real * cosine + imag * sine, imag * cosine - real * sine), False)
-    for value, index, rows in shares(outs):
-        value[...] = waves[index, :, rows].astype(jnp.bfloat16)
+    for place, mask in enumerate(order):
+        index = depth ^ mask
+        if place < LATE:
+            first, second = waves[index, :, :BAND], waves[index, :, BAND:]
+            outs[place][...] = jnp.where(above, first, second).astype(jnp.bfloat16)
+            outs[LATE + place][...] = jnp.where(above, second, first).astype(jnp.bfloat16)
+        else:
+            outs[LATE + place][...] = waves[index].astype(jnp.bfloat16)
 
 
 def added(wide, part, block, rows, value, offset, lane):
@@ -373,20 +370,20 @@
         wide,
     )
     probe_wave, fresnel_phase, windows = lax.optimization_barrier((probe_wave, fresnel_phase, windows))
-    incident, turn = call(
+    incident, turn, upper = call(
         lambda *refs: prep_kernel(strip, *refs),
-        [square, square],
+        [square, square, jax.ShapeDtypeStruct((BAND, window), jnp.float32)],
         [extents, codes, probe_wave, fresnel_phase],
         scalars=1,
     )
     windows = swapped(windows)
     pieces = call(
-        lambda *refs: wave_kernel(order, strip, *refs),
+        lambda *refs: wave_kernel(order, *refs),
         [piece] * (2 * LATE) + [patch] * (depths - LATE),
         [
-            codes,
             incident,
             turn,
+            upper,
             measured,
             *map(jnp.asarray, tables(window)),
             *windows[:EARLY],

time: 41.2 us -> 40.9 us (level)
  no operation moved by 1% of the time
where the time goes in v3:
time: 40.9 us; the launch traced here: 40.8 us
  starting transfers between devices  19.8 us (48%)
  waiting for transfers between devices  11.1 us (27%)
  Pallas kernels  9.6 us (23%)
    ppermute x11, starting transfers between devices, swap(): return lax.ppermute(value, 'depth', [(d, d ^ mask) for d in range(depths)])  14.8 us
    ppermute x11, waiting for transfers between devices, swap(): return lax.ppermute(value, 'depth', [(d, d ^ mask) for d in range(depths)])  11.1 us
    pallas_call x6, Pallas kernels, call(): pl.pallas_call(kernel, out_shape=outs, in_specs=[SMEM] * scalars + [VMEM]...  7.04 us
    ppermute x2, starting transfers between devices, outward(): lax.ppermute(value, 'tile', [(t, (t - 1 + 2 * (t % 2)) % tiles) for t in...  4.97 us
    pallas_call x2, Pallas kernels, edge(): pl.pallas_call(lambda *refs: edge_kernel(side, *refs), out_shape=jax.Shap...  1.49 us
    pallas_call x1, Pallas kernels, shards(): pl.pallas_call(lambda *refs: band_kernel(order, tiles, *refs), out_shape=...  1.07 us
  transfers between devices with their start and end apart: 15, of which 6 were waited for; matrix products, arithmetic and copies ran while one was open for 0% of the time, Pallas kernels for 7%

profile of v3, /device:TPU:0, one launch (start us, length us, event | category | flops | bytes accessed | tf_op | source)
XLA Modules:
  0.0 40.8 jit_solution(11749841600122475289)
XLA Ops:
  0.0 1.1 %bands.1 = (f32[2,1,128,512]{3,2,1,0:T(8,128)S(1)}, bf16[2,1,64,512]{3,2,1,0:T(8,128)(2,1)S(1)}, bf16[2,1,64,512]{3,2,1,0:T(8,128)(2,1)S(1)}, s32[4,128]{1,0:T(4,128)S(1)}) custom-call(s32[2,4]{1,0:T(2,128)} %bitcast.1, f32[2,1,128,512]{3,2,1,0:T(8,128)} %refs_1_.1), custom_call_target="tpu_custom_call" | custom-call | tf_op jit(solution)/shard_map/bands/pallas_call | solution.py:352
  1.1 3.4 %collective-permute-start = (bf16[2,1,64,512]{3,2,1,0:T(8,128)(2,1)S(1)}, bf16[2,1,64,512]{3,2,1,0:T(8,128)(2,1)S(1)}, u32[]{:S(2)}, u32[]{:S(2)}) collective-permute-start(bf16[2,1,64,512]{3,2,1,0:T(8,128)(2,1)S(1)} %get-tuple-element.37), channel_id=1, source_target_pairs={{0,28},{4,8},{8,4},{12,16},{16,12},{20,24},{24,20},{28,0},{1,29},{... | collective-permute-start | bytes 393224 | tf_op jit(solution)/shard_map/ppermute | solution.py:345
  4.5 0.0 collective-permute-start.1
  4.5 0.4 shard_map.100
  4.9 2.7 %collective-permute-start.5 = (bf16[2,64,128]{2,1,0:T(8,128)(2,1)S(1)}, bf16[2,64,128]{2,1,0:T(8,128)(2,1)S(1)}, u32[]{:S(2)}, u32[]{:S(2)}) collective-permute-start(bf16[2,64,128]{2,1,0:T(8,128)(2,1)S(1)} %get-tuple-element.51), channel_id=1, source_target_pairs={{0,2},{1,3},{2,0},{3,1},{4,6},{5,7},{6,4},{7,5},{8,10},{9,11},{10,... | collective-permute-start | bytes 98312 | tf_op jit(solution)/shard_map/ppermute | solution.py:339
  7.6 1.3 %collective-permute-start.6 = (bf16[2,64,128]{2,1,0:T(8,128)(2,1)S(1)}, bf16[2,64,128]{2,1,0:T(8,128)(2,1)S(1)}, u32[]{:S(2)}, u32[]{:S(2)}) collective-permute-start(bf16[2,64,128]{2,1,0:T(8,128)(2,1)S(1)} %get-tuple-element.52), channel_id=1, source_target_pairs={{0,3},{1,2},{2,1},{3,0},{4,7},{5,6},{6,5},{7,4},{8,11},{9,10},{10,... | collective-permute-start | bytes 98312 | tf_op jit(solution)/shard_map/ppermute | solution.py:339
  8.9 0.2 collective-permute-start.7
  9.1 0.0 collective-permute-done.refs_2_
  9.1 0.0 collective-permute-done.1.refs_3_
  9.2 0.0 copy-start.7
  9.2 0.0 copy-start
  9.2 0.0 copy-start.3
  9.2 0.0 copy-start.4
  9.2 0.0 copy-start.5
  9.2 0.2 shard_map.101
  9.4 0.0 copy-start.2
  9.4 2.9 %collective-permute-start.2 = (bf16[2,64,128]{2,1,0:T(8,128)(2,1)S(1)}, bf16[2,64,128]{2,1,0:T(8,128)(2,1)S(1)}, u32[]{:S(2)}, u32[]{:S(2)}) collective-permute-start(bf16[2,64,128]{2,1,0:T(8,128)(2,1)S(1)} %get-tuple-element.48), channel_id=1, source_target_pairs={{0,2},{1,3},{2,0},{3,1},{4,6},{5,7},{6,4},{7,5},{8,10},{9,11},{10,... | collective-permute-start | bytes 98312 | tf_op jit(solution)/shard_map/ppermute | solution.py:339
  12.3 1.3 %collective-permute-start.3 = (bf16[2,64,128]{2,1,0:T(8,128)(2,1)S(1)}, bf16[2,64,128]{2,1,0:T(8,128)(2,1)S(1)}, u32[]{:S(2)}, u32[]{:S(2)}) collective-permute-start(bf16[2,64,128]{2,1,0:T(8,128)(2,1)S(1)} %get-tuple-element.49), channel_id=1, source_target_pairs={{0,3},{1,2},{2,1},{3,0},{4,7},{5,6},{6,5},{7,4},{8,11},{9,10},{10,... | collective-permute-start | bytes 98312 | tf_op jit(solution)/shard_map/ppermute | solution.py:339
  13.7 0.0 collective-permute-done.5.refs_11_
  13.7 0.1 collective-permute-start.4
  13.7 0.0 copy-done.6
  13.7 0.0 copy-done.7
  13.7 1.0 %shard_map.102 = (f32[2,128,128]{2,1,0:T(8,128)S(1)}, f32[2,128,128]{2,1,0:T(8,128)S(1)}, f32[64,128]{1,0:T(8,128)S(1)}) custom-call(s32[1,2]{1,0:T(1,128)S(1)} %copy-done.7, s32[4,128]{1,0:T(4,128)S(1)} %get-tuple-element.34.codes.refs_0_.refs_1_, f32[2,128,128]{2,1,0:T(8,128)S(1)} %copy-done.1, f32[128,128]{1,0:T(8,128)S(1)} %copy-done.6), custom_call_target="tpu_custom_call" | custom-call | tf_op jit(solution)/shard_map/pallas_call | solution.py:313
  14.7 0.0 collective-permute-done.6.refs_12_
  14.7 0.0 collective-permute-done.7.refs_13_
  14.8 0.1 collective-permute-done.2.refs_8_
  14.9 3.2 %collective-permute-done.3.refs_9_ = bf16[2,64,128]{2,1,0:T(8,128)(2,1)S(1)} collective-permute-done((bf16[2,64,128]{2,1,0:T(8,128)(2,1)S(1)}, bf16[2,64,128]{2,1,0:T(8,128)(2,1)S(1)}, u32[]{:S(2)}, u32[]{:S(2)}) %collective-permute-start.3) | collective-permute-done | bytes 32800 | tf_op jit(solution)/shard_map/ppermute | solution.py:339
  18.0 0.0 collective-permute-done.4.refs_10_
  18.0 0.0 copy-done
  18.1 4.9 %shard_map.103 = (bf16[2,64,128]{2,1,0:T(8,128)(2,1)S(1)}, bf16[2,64,128]{2,1,0:T(8,128)(2,1)S(1)}, bf16[2,64,128]{2,1,0:T(8,128)(2,1)S(1)}, bf16[2,64,128]{2,1,...) custom-call(f32[2,128,128]{2,1,0:T(8,128)S(1)} %get-tuple-element.45.refs_0_, ...), custom_call_target="tpu_custom_call" | custom-call | tf_op jit(solution)/shard_map/pallas_call | solution.py:313
  22.9 0.1 collective-permute-start.12
  23.0 2.6 %collective-permute-start.8 = (bf16[2,64,128]{2,1,0:T(8,128)(2,1)S(1)}, bf16[2,64,128]{2,1,0:T(8,128)(2,1)S(1)}, u32[]{:S(2)}, u32[]{:S(2)}) collective-permute-start(bf16[2,64,128]{2,1,0:T(8,128)(2,1)S(1)} %get-tuple-element.55), channel_id=1, source_target_pairs={{0,2},{1,3},{2,0},{3,1},{4,6},{5,7},{6,4},{7,5},{8,10},{9,11},{10,... | collective-permute-start | bytes 98312 | tf_op jit(solution)/shard_map/ppermute | solution.py:339
  25.6 1.8 %collective-permute-start.9 = (bf16[2,64,128]{2,1,0:T(8,128)(2,1)S(1)}, bf16[2,64,128]{2,1,0:T(8,128)(2,1)S(1)}, u32[]{:S(2)}, u32[]{:S(2)}) collective-permute-start(bf16[2,64,128]{2,1,0:T(8,128)(2,1)S(1)} %get-tuple-element.56), channel_id=1, source_target_pairs={{0,3},{1,2},{2,1},{3,0},{4,7},{5,6},{6,5},{7,4},{8,11},{9,10},{10,... | collective-permute-start | bytes 98312 | tf_op jit(solution)/shard_map/ppermute | solution.py:339
  27.4 0.5 %collective-permute-done.8.refs_0_.refs_1_ = bf16[2,64,128]{2,1,0:T(8,128)(2,1)S(1)} collective-permute-done((bf16[2,64,128]{2,1,0:T(8,128)(2,1)S(1)}, bf16[2,64,128]{2,1,0:T(8,128)(2,1)S(1)}, u32[]{:S(2)}, u32[]{:S(2)}) %collective-permute-start.8) | collective-permute-done | bytes 32800 | tf_op jit(solution)/shard_map/ppermute | solution.py:339
  27.9 3.4 %collective-permute-done.9.refs_1_.refs_2_ = bf16[2,64,128]{2,1,0:T(8,128)(2,1)S(1)} collective-permute-done((bf16[2,64,128]{2,1,0:T(8,128)(2,1)S(1)}, bf16[2,64,128]{2,1,0:T(8,128)(2,1)S(1)}, u32[]{:S(2)}, u32[]{:S(2)}) %collective-permute-start.9) | collective-permute-done | bytes 32800 | tf_op jit(solution)/shard_map/ppermute | solution.py:339
  31.3 0.0 collective-permute-done.12.refs_4_.refs_3_
  31.3 0.2 shard_map.105
  31.5 0.1 collective-permute-start.14
  31.6 1.5 %collective-permute-start.13 = (bf16[2,1,64,512]{3,2,1,0:T(8,128)(2,1)S(1)}, bf16[2,1,64,512]{3,2,1,0:T(8,128)(2,1)S(1)}, u32[]{:S(2)}, u32[]{:S(2)}) collective-permute-start(bf16[2,1,64,512]{3,2,1,0:T(8,128)(2,1)S(1)} %get-tuple-element.61), channel_id=1, source_target_pairs={{0,28},{4,8},{8,4},{12,16},{16,12},{20,24},{24,20},{28,0},{1,29},{... | collective-permute-start | bytes 393224 | tf_op jit(solution)/shard_map/ppermute | solution.py:345
  33.2 0.0 collective-permute-start.10
  33.2 1.8 %collective-permute-start.11 = (bf16[2,64,128]{2,1,0:T(8,128)(2,1)S(1)}, bf16[2,64,128]{2,1,0:T(8,128)(2,1)S(1)}, u32[]{:S(2)}, u32[]{:S(2)}) collective-permute-start(bf16[2,64,128]{2,1,0:T(8,128)(2,1)S(1)} %get-tuple-element.58), channel_id=1, source_target_pairs={{0,3},{1,2},{2,1},{3,0},{4,7},{5,6},{6,5},{7,4},{8,11},{9,10},{10,... | collective-permute-start | bytes 98312 | tf_op jit(solution)/shard_map/ppermute | solution.py:339
  35.0 3.3 %collective-permute-done.10.refs_2_ = bf16[2,64,128]{2,1,0:T(8,128)(2,1)S(1)} collective-permute-done((bf16[2,64,128]{2,1,0:T(8,128)(2,1)S(1)}, bf16[2,64,128]{2,1,0:T(8,128)(2,1)S(1)}, u32[]{:S(2)}, u32[]{:S(2)}) %collective-permute-start.10) | collective-permute-done | bytes 32800 | tf_op jit(solution)/shard_map/ppermute | solution.py:339
  38.3 0.6 %collective-permute-done.11.refs_3_ = bf16[2,64,128]{2,1,0:T(8,128)(2,1)S(1)} collective-permute-done((bf16[2,64,128]{2,1,0:T(8,128)(2,1)S(1)}, bf16[2,64,128]{2,1,0:T(8,128)(2,1)S(1)}, u32[]{:S(2)}, u32[]{:S(2)}) %collective-permute-start.11) | collective-permute-done | bytes 32800 | tf_op jit(solution)/shard_map/ppermute | solution.py:339
  38.9 0.3 shard_map.104.refs_0_
  39.3 0.0 collective-permute-done.14.refs_1_
  39.3 0.7 %shard_map.106.refs_2_ = f32[2,1,128,512]{3,2,1,0:T(8,128)} custom-call(f32[2,1,128,512]{3,2,1,0:T(8,128)S(1)} %shard_map.104.refs_0_, bf16[2,1,64,512]{3,2,1,0:T(8,128)(2,1)S(1)} %collective-permute-done.14.refs_1_), custom_call_target="tpu_custom_call" | custom-call | tf_op jit(solution)/shard_map/pallas_call | solution.py:301
  40.0 0.0 collective-permute-done.13.refs_1_
  40.0 0.7 %shard_map.107 = f32[2,1,128,512]{3,2,1,0:T(8,128)} custom-call(f32[2,1,128,512]{3,2,1,0:T(8,128)S(1)} %shard_map.104.refs_0_, bf16[2,1,64,512]{3,2,1,0:T(8,128)(2,1)S(1)} %collective-permute-done.13.refs_1_, f32[2,1,128,512]{3,2,1,0:T(8,128)} %shard_map.106.refs_2_), custom_call_target="tpu_custom_call", output_to_operand_aliasing={{}: (2, {})} | custom-call | tf_op jit(solution)/shard_map/pallas_call | solution.py:301
  (7 shorter events, 0.0 us)
Async XLA Ops:
  1.1 8.1 %collective-permute-start = (bf16[2,1,64,512]{3,2,1,0:T(8,128)(2,1)S(1)}, bf16[2,1,64,512]{3,2,1,0:T(8,128)(2,1)S(1)}, u32[]{:S(2)}, u32[]{:S(2)}) collective-permute-start(bf16[2,1,64,512]{3,2,1,0:T(8,128)(2,1)S(1)} %get-tuple-element.37), channel_id=1, source_target_pairs={{0,28},{4,8},{8,4},{12,16},{16,12},{20,24},{24,20},{28,0},{1,29},{... | collective-permute-start | bytes 393224 | tf_op jit(solution)/shard_map/ppermute | solution.py:345
  4.5 4.6 %collective-permute-start.1 = (bf16[2,1,64,512]{3,2,1,0:T(8,128)(2,1)S(1)}, bf16[2,1,64,512]{3,2,1,0:T(8,128)(2,1)S(1)}, u32[]{:S(2)}, u32[]{:S(2)}) collective-permute-start(bf16[2,1,64,512]{3,2,1,0:T(8,128)(2,1)S(1)} %get-tuple-element.38), channel_id=1, source_target_pairs={{0,4},{4,0},{8,12},{12,8},{16,20},{20,16},{24,28},{28,24},{1,5},{5... | collective-permute-start | bytes 393224 | tf_op jit(solution)/shard_map/ppermute | solution.py:348
  4.5 9.2 %copy-start.6 = (f32[128,128]{1,0:T(8,128)S(1)}, f32[128,128]{1,0:T(8,128)}, u32[]{:S(2)}) copy-start(f32[128,128]{1,0:T(8,128)} %refs_3_.1) | copy-start | bytes 196612
  4.9 8.7 %collective-permute-start.5 = (bf16[2,64,128]{2,1,0:T(8,128)(2,1)S(1)}, bf16[2,64,128]{2,1,0:T(8,128)(2,1)S(1)}, u32[]{:S(2)}, u32[]{:S(2)}) collective-permute-start(bf16[2,64,128]{2,1,0:T(8,128)(2,1)S(1)} %get-tuple-element.51), channel_id=1, source_target_pairs={{0,2},{1,3},{2,0},{3,1},{4,6},{5,7},{6,4},{7,5},{8,10},{9,11},{10,... | collective-permute-start | bytes 98312 | tf_op jit(solution)/shard_map/ppermute | solution.py:339
  7.6 7.2 %collective-permute-start.6 = (bf16[2,64,128]{2,1,0:T(8,128)(2,1)S(1)}, bf16[2,64,128]{2,1,0:T(8,128)(2,1)S(1)}, u32[]{:S(2)}, u32[]{:S(2)}) collective-permute-start(bf16[2,64,128]{2,1,0:T(8,128)(2,1)S(1)} %get-tuple-element.52), channel_id=1, source_target_pairs={{0,3},{1,2},{2,1},{3,0},{4,7},{5,6},{6,5},{7,4},{8,11},{9,10},{10,... | collective-permute-start | bytes 98312 | tf_op jit(solution)/shard_map/ppermute | solution.py:339
  8.9 5.8 %collective-permute-start.7 = (bf16[2,64,128]{2,1,0:T(8,128)(2,1)S(1)}, bf16[2,64,128]{2,1,0:T(8,128)(2,1)S(1)}, u32[]{:S(2)}, u32[]{:S(2)}) collective-permute-start(bf16[2,64,128]{2,1,0:T(8,128)(2,1)S(1)} %get-tuple-element.53), channel_id=1, source_target_pairs={{0,1},{1,0},{2,3},{3,2},{4,5},{5,4},{6,7},{7,6},{8,9},{9,8},{10,11... | collective-permute-start | bytes 98312 | tf_op jit(solution)/shard_map/ppermute | solution.py:339
  9.1 4.6 %copy-start.1 = (f32[2,128,128]{2,1,0:T(8,128)S(1)}, f32[2,128,128]{2,1,0:T(8,128)}, u32[]{:S(2)}) copy-start(f32[2,128,128]{2,1,0:T(8,128)} %refs_2_) | copy-start | bytes 393220
  9.2 4.6 %copy-start.7 = (s32[1,2]{1,0:T(1,128)S(1)}, s32[1,2]{1,0:T(1,128)}, u32[]{:S(2)}) copy-start(s32[1,2]{1,0:T(1,128)} %refs_0_.1) | copy-start | bytes 28
  9.2 8.9 %copy-start = (f32[4,128,128]{2,1,0:T(8,128)S(1)}, f32[4,128,128]{2,1,0:T(8,128)}, u32[]{:S(2)}) copy-start(f32[4,128,128]{2,1,0:T(8,128)} %refs_3_.2) | copy-start | bytes 786436
  9.2 8.8 %copy-start.3 = (bf16[256,256]{1,0:T(8,128)(2,1)S(1)}, bf16[256,256]{1,0:T(8,128)(2,1)}, u32[]{:S(2)}) copy-start(bf16[256,256]{1,0:T(8,128)(2,1)} %constant.10.clone.refs_6_) | copy-start | bytes 393220
  9.2 8.8 %copy-start.4 = (bf16[256,256]{1,0:T(8,128)(2,1)S(1)}, bf16[256,256]{1,0:T(8,128)(2,1)}, u32[]{:S(2)}) copy-start(bf16[256,256]{1,0:T(8,128)(2,1)} %constant.9.clone.refs_5_) | copy-start | bytes 393220
  9.2 8.8 %copy-start.5 = (bf16[256,256]{1,0:T(8,128)(2,1)S(1)}, bf16[256,256]{1,0:T(8,128)(2,1)}, u32[]{:S(2)}) copy-start(bf16[256,256]{1,0:T(8,128)(2,1)} %constant.8.clone.refs_4_) | copy-start | bytes 393220
  9.4 8.6 %copy-start.2 = (bf16[256,256]{1,0:T(8,128)(2,1)S(1)}, bf16[256,256]{1,0:T(8,128)(2,1)}, u32[]{:S(2)}) copy-start(bf16[256,256]{1,0:T(8,128)(2,1)} %constant.11.clone.refs_7_) | copy-start | bytes 393220
  9.4 5.4 %collective-permute-start.2 = (bf16[2,64,128]{2,1,0:T(8,128)(2,1)S(1)}, bf16[2,64,128]{2,1,0:T(8,128)(2,1)S(1)}, u32[]{:S(2)}, u32[]{:S(2)}) collective-permute-start(bf16[2,64,128]{2,1,0:T(8,128)(2,1)S(1)} %get-tuple-element.48), channel_id=1, source_target_pairs={{0,2},{1,3},{2,0},{3,1},{4,6},{5,7},{6,4},{7,5},{8,10},{9,11},{10,... | collective-permute-start | bytes 98312 | tf_op jit(solution)/shard_map/ppermute | solution.py:339
  12.3 5.7 %collective-permute-start.3 = (bf16[2,64,128]{2,1,0:T(8,128)(2,1)S(1)}, bf16[2,64,128]{2,1,0:T(8,128)(2,1)S(1)}, u32[]{:S(2)}, u32[]{:S(2)}) collective-permute-start(bf16[2,64,128]{2,1,0:T(8,128)(2,1)S(1)} %get-tuple-element.49), channel_id=1, source_target_pairs={{0,3},{1,2},{2,1},{3,0},{4,7},{5,6},{6,5},{7,4},{8,11},{9,10},{10,... | collective-permute-start | bytes 98312 | tf_op jit(solution)/shard_map/ppermute | solution.py:339
  13.7 4.4 %collective-permute-start.4 = (bf16[2,64,128]{2,1,0:T(8,128)(2,1)S(1)}, bf16[2,64,128]{2,1,0:T(8,128)(2,1)S(1)}, u32[]{:S(2)}, u32[]{:S(2)}) collective-permute-start(bf16[2,64,128]{2,1,0:T(8,128)(2,1)S(1)} %get-tuple-element.50), channel_id=1, source_target_pairs={{0,1},{1,0},{2,3},{3,2},{4,5},{5,4},{6,7},{7,6},{8,9},{9,8},{10,11... | collective-permute-start | bytes 98312 | tf_op jit(solution)/shard_map/ppermute | solution.py:339
  22.9 8.4 %collective-permute-start.12 = (bf16[2,128,128]{2,1,0:T(8,128)(2,1)S(1)}, bf16[2,128,128]{2,1,0:T(8,128)(2,1)S(1)}, u32[]{:S(2)}, u32[]{:S(2)}) collective-permute-start(bf16[2,128,128]{2,1,0:T(8,128)(2,1)S(1)} %get-tuple-element.59), channel_id=1, source_target_pairs={{0,1},{1,0},{2,3},{3,2},{4,5},{5,4},{6,7},{7,6},{8,9},{9,8},{10,11... | collective-permute-start | bytes 196616 | tf_op jit(solution)/shard_map/ppermute | solution.py:339
  23.0 4.9 %collective-permute-start.8 = (bf16[2,64,128]{2,1,0:T(8,128)(2,1)S(1)}, bf16[2,64,128]{2,1,0:T(8,128)(2,1)S(1)}, u32[]{:S(2)}, u32[]{:S(2)}) collective-permute-start(bf16[2,64,128]{2,1,0:T(8,128)(2,1)S(1)} %get-tuple-element.55), channel_id=1, source_target_pairs={{0,2},{1,3},{2,0},{3,1},{4,6},{5,7},{6,4},{7,5},{8,10},{9,11},{10,... | collective-permute-start | bytes 98312 | tf_op jit(solution)/shard_map/ppermute | solution.py:339
  25.6 5.7 %collective-permute-start.9 = (bf16[2,64,128]{2,1,0:T(8,128)(2,1)S(1)}, bf16[2,64,128]{2,1,0:T(8,128)(2,1)S(1)}, u32[]{:S(2)}, u32[]{:S(2)}) collective-permute-start(bf16[2,64,128]{2,1,0:T(8,128)(2,1)S(1)} %get-tuple-element.56), channel_id=1, source_target_pairs={{0,3},{1,2},{2,1},{3,0},{4,7},{5,6},{6,5},{7,4},{8,11},{9,10},{10,... | collective-permute-start | bytes 98312 | tf_op jit(solution)/shard_map/ppermute | solution.py:339
  31.5 7.7 %collective-permute-start.14 = (bf16[2,1,64,512]{3,2,1,0:T(8,128)(2,1)S(1)}, bf16[2,1,64,512]{3,2,1,0:T(8,128)(2,1)S(1)}, u32[]{:S(2)}, u32[]{:S(2)}) collective-permute-start(bf16[2,1,64,512]{3,2,1,0:T(8,128)(2,1)S(1)} %get-tuple-element.62), channel_id=1, source_target_pairs={{0,4},{4,0},{8,12},{12,8},{16,20},{20,16},{24,28},{28,24},{1,5},{5... | collective-permute-start | bytes 393224 | tf_op jit(solution)/shard_map/ppermute | solution.py:348
  31.6 8.4 %collective-permute-start.13 = (bf16[2,1,64,512]{3,2,1,0:T(8,128)(2,1)S(1)}, bf16[2,1,64,512]{3,2,1,0:T(8,128)(2,1)S(1)}, u32[]{:S(2)}, u32[]{:S(2)}) collective-permute-start(bf16[2,1,64,512]{3,2,1,0:T(8,128)(2,1)S(1)} %get-tuple-element.61), channel_id=1, source_target_pairs={{0,28},{4,8},{8,4},{12,16},{16,12},{20,24},{24,20},{28,0},{1,29},{... | collective-permute-start | bytes 393224 | tf_op jit(solution)/shard_map/ppermute | solution.py:345
  33.2 5.1 %collective-permute-start.10 = (bf16[2,64,128]{2,1,0:T(8,128)(2,1)S(1)}, bf16[2,64,128]{2,1,0:T(8,128)(2,1)S(1)}, u32[]{:S(2)}, u32[]{:S(2)}) collective-permute-start(bf16[2,64,128]{2,1,0:T(8,128)(2,1)S(1)} %get-tuple-element.57), channel_id=1, source_target_pairs={{0,2},{1,3},{2,0},{3,1},{4,6},{5,7},{6,4},{7,5},{8,10},{9,11},{10,... | collective-permute-start | bytes 98312 | tf_op jit(solution)/shard_map/ppermute | solution.py:339
  33.2 5.7 %collective-permute-start.11 = (bf16[2,64,128]{2,1,0:T(8,128)(2,1)S(1)}, bf16[2,64,128]{2,1,0:T(8,128)(2,1)S(1)}, u32[]{:S(2)}, u32[]{:S(2)}) collective-permute-start(bf16[2,64,128]{2,1,0:T(8,128)(2,1)S(1)} %get-tuple-element.58), channel_id=1, source_target_pairs={{0,3},{1,2},{2,1},{3,0},{4,7},{5,6},{6,5},{7,4},{8,11},{9,10},{10,... | collective-permute-start | bytes 98312 | tf_op jit(solution)/shard_map/ppermute | solution.py:339

commit v4 on v3

--- a/solution.py
+++ b/solution.py
@@ -67,12 +67,12 @@
     tile, depth = lax.axis_index("tile"), lax.axis_index("depth")
     odd = lax.rem(tile, 2)
     outs, copies = (outer, inner), []
+    fetch = pltpu.make_async_copy(positions_in, positions, sems.at[2])
+    fetch.start()
     for index, side in enumerate((odd, 1 - odd)):
         rows = pl.ds(pl.multiple_of(side * (strip - BAND), BAND), BAND)
         copies.append(pltpu.make_async_copy(own.at[:, :, rows], strip_out.at[:, :, rows], sems.at[index]))
         copies[-1].start()
-    fetch = pltpu.make_async_copy(positions_in, positions, sems.at[2])
-    fetch.start()
     fetch.wait()
     for place, mask in enumerate(order):
         probe = depth ^ mask
@@ -156,25 +156,29 @@
 
 
 def from_left(real, imag, matrix, exact):
-    half = real.shape[1]
-    stacked = jnp.concatenate([real, imag], axis=0)
+    size = real.shape[0]
     if exact:
-        high, low = split(stacked)
+        high, low = split(jnp.concatenate([real, imag], axis=0))
         both = dot(matrix[0], jnp.concatenate([high, low], axis=1))
-        stacked = both[:, :half] + both[:, half:] + dot(matrix[1], high)
+        stacked = both[:, :size] + both[:, size:] + dot(matrix[1], high)
+        return stacked[:size], stacked[size:]
+    real, imag = real.astype(jnp.bfloat16), imag.astype(jnp.bfloat16)
+    columns = jnp.concatenate(
+        [jnp.concatenate([real, imag], axis=1), jnp.concatenate([imag, -real], axis=1)], axis=0
+    )
+    both = dot(matrix[0][:size], columns)
+    return both[:, :size], both[:, size:]
+
+
+def from_right(real, imag, matrix, exact):
+    size = real.shape[0]
+    stacked = jnp.concatenate([real, imag], axis=1).astype(jnp.bfloat16)
+    if exact:
+        product = dot(stacked, matrix[0]) + dot(stacked, matrix[1])
     else:
-        stacked = dot(matrix[0], stacked.astype(jnp.bfloat16))
-    size = real.shape[0]
-    return stacked[:size], stacked[size:]
-
-
-def from_right(real, imag, matrix, exact):
-    stacked = jnp.concatenate([real, imag], axis=1).astype(jnp.bfloat16)
-    product = dot(stacked, matrix[0])
-    if exact:
-        product += dot(stacked, matrix[1])
-    half = real.shape[1]
-    return product[:, :half], product[:, half:]
+        halves = stacked[: size // 2], stacked[size // 2 :]
+        product = jnp.concatenate([dot(half, matrix[0]) for half in halves], axis=0)
+    return product[:, :size], product[:, size:]
 
 
 def wave_kernel(order, incident, turn, upper, measured, *refs):

time: 40.9 us -> 40.8 us (level)
  no operation moved by 1% of the time
where the time goes in v4:
time: 40.8 us; the launch traced here: 40.6 us
  starting transfers between devices  19.8 us (49%)
  waiting for transfers between devices  11.1 us (27%)
  Pallas kernels  9.47 us (23%)
    ppermute x11, starting transfers between devices, swap(): return lax.ppermute(value, 'depth', [(d, d ^ mask) for d in range(depths)])  14.8 us
    ppermute x11, waiting for transfers between devices, swap(): return lax.ppermute(value, 'depth', [(d, d ^ mask) for d in range(depths)])  11.1 us
    pallas_call x6, Pallas kernels, call(): pl.pallas_call(kernel, out_shape=outs, in_specs=[SMEM] * scalars + [VMEM]...  6.91 us
    ppermute x2, starting transfers between devices, outward(): lax.ppermute(value, 'tile', [(t, (t - 1 + 2 * (t % 2)) % tiles) for t in...  4.97 us
    pallas_call x2, Pallas kernels, edge(): pl.pallas_call(lambda *refs: edge_kernel(side, *refs), out_shape=jax.Shap...  1.49 us
    pallas_call x1, Pallas kernels, shards(): pl.pallas_call(lambda *refs: band_kernel(order, tiles, *refs), out_shape=...  1.07 us
  transfers between devices with their start and end apart: 15, of which 6 were waited for; matrix products, arithmetic and copies ran while one was open for 0% of the time, Pallas kernels for 7%

profile of v4, /device:TPU:0, one launch (start us, length us, event | category | flops | bytes accessed | tf_op | source)
XLA Modules:
  0.0 40.6 jit_solution(9608461349930833100)
XLA Ops:
  0.0 1.1 %bands.1 = (f32[2,1,128,512]{3,2,1,0:T(8,128)S(1)}, bf16[2,1,64,512]{3,2,1,0:T(8,128)(2,1)S(1)}, bf16[2,1,64,512]{3,2,1,0:T(8,128)(2,1)S(1)}, s32[4,128]{1,0:T(4,128)S(1)}) custom-call(s32[2,4]{1,0:T(2,128)} %bitcast.1, f32[2,1,128,512]{3,2,1,0:T(8,128)} %refs_1_.1), custom_call_target="tpu_custom_call" | custom-call | tf_op jit(solution)/shard_map/bands/pallas_call | solution.py:356
  1.1 3.4 %collective-permute-start = (bf16[2,1,64,512]{3,2,1,0:T(8,128)(2,1)S(1)}, bf16[2,1,64,512]{3,2,1,0:T(8,128)(2,1)S(1)}, u32[]{:S(2)}, u32[]{:S(2)}) collective-permute-start(bf16[2,1,64,512]{3,2,1,0:T(8,128)(2,1)S(1)} %get-tuple-element.37), channel_id=1, source_target_pairs={{0,28},{4,8},{8,4},{12,16},{16,12},{20,24},{24,20},{28,0},{1,29},{... | collective-permute-start | bytes 393224 | tf_op jit(solution)/shard_map/ppermute | solution.py:349
  4.5 0.0 collective-permute-start.1
  4.5 0.4 shard_map.100
  4.9 2.7 %collective-permute-start.5 = (bf16[2,64,128]{2,1,0:T(8,128)(2,1)S(1)}, bf16[2,64,128]{2,1,0:T(8,128)(2,1)S(1)}, u32[]{:S(2)}, u32[]{:S(2)}) collective-permute-start(bf16[2,64,128]{2,1,0:T(8,128)(2,1)S(1)} %get-tuple-element.51), channel_id=1, source_target_pairs={{0,2},{1,3},{2,0},{3,1},{4,6},{5,7},{6,4},{7,5},{8,10},{9,11},{10,... | collective-permute-start | bytes 98312 | tf_op jit(solution)/shard_map/ppermute | solution.py:343
  7.6 1.3 %collective-permute-start.6 = (bf16[2,64,128]{2,1,0:T(8,128)(2,1)S(1)}, bf16[2,64,128]{2,1,0:T(8,128)(2,1)S(1)}, u32[]{:S(2)}, u32[]{:S(2)}) collective-permute-start(bf16[2,64,128]{2,1,0:T(8,128)(2,1)S(1)} %get-tuple-element.52), channel_id=1, source_target_pairs={{0,3},{1,2},{2,1},{3,0},{4,7},{5,6},{6,5},{7,4},{8,11},{9,10},{10,... | collective-permute-start | bytes 98312 | tf_op jit(solution)/shard_map/ppermute | solution.py:343
  8.9 0.2 collective-permute-start.7
  9.1 0.0 collective-permute-done.refs_2_
  9.1 0.0 collective-permute-done.1.refs_3_
  9.2 0.0 copy-start.7
  9.2 0.0 copy-start
  9.2 0.0 copy-start.3
  9.2 0.0 copy-start.4
  9.2 0.0 copy-start.5
  9.2 0.2 shard_map.101
  9.4 0.0 copy-start.2
  9.4 2.9 %collective-permute-start.2 = (bf16[2,64,128]{2,1,0:T(8,128)(2,1)S(1)}, bf16[2,64,128]{2,1,0:T(8,128)(2,1)S(1)}, u32[]{:S(2)}, u32[]{:S(2)}) collective-permute-start(bf16[2,64,128]{2,1,0:T(8,128)(2,1)S(1)} %get-tuple-element.48), channel_id=1, source_target_pairs={{0,2},{1,3},{2,0},{3,1},{4,6},{5,7},{6,4},{7,5},{8,10},{9,11},{10,... | collective-permute-start | bytes 98312 | tf_op jit(solution)/shard_map/ppermute | solution.py:343
  12.3 1.3 %collective-permute-start.3 = (bf16[2,64,128]{2,1,0:T(8,128)(2,1)S(1)}, bf16[2,64,128]{2,1,0:T(8,128)(2,1)S(1)}, u32[]{:S(2)}, u32[]{:S(2)}) collective-permute-start(bf16[2,64,128]{2,1,0:T(8,128)(2,1)S(1)} %get-tuple-element.49), channel_id=1, source_target_pairs={{0,3},{1,2},{2,1},{3,0},{4,7},{5,6},{6,5},{7,4},{8,11},{9,10},{10,... | collective-permute-start | bytes 98312 | tf_op jit(solution)/shard_map/ppermute | solution.py:343
  13.7 0.0 collective-permute-done.5.refs_11_
  13.7 0.1 collective-permute-start.4
  13.7 0.0 copy-done.6
  13.7 0.0 copy-done.1
  13.7 1.0 %shard_map.102 = (f32[2,128,128]{2,1,0:T(8,128)S(1)}, f32[2,128,128]{2,1,0:T(8,128)S(1)}, f32[64,128]{1,0:T(8,128)S(1)}) custom-call(s32[1,2]{1,0:T(1,128)S(1)} %copy-done.7, s32[4,128]{1,0:T(4,128)S(1)} %get-tuple-element.34.codes.refs_0_.refs_1_, f32[2,128,128]{2,1,0:T(8,128)S(1)} %copy-done.1, f32[128,128]{1,0:T(8,128)S(1)} %copy-done.6), custom_call_target="tpu_custom_call" | custom-call | tf_op jit(solution)/shard_map/pallas_call | solution.py:317
  14.7 0.0 collective-permute-done.6.refs_12_
  14.7 0.0 collective-permute-done.7.refs_13_
  14.8 0.1 collective-permute-done.2.refs_8_
  14.9 3.2 %collective-permute-done.3.refs_9_ = bf16[2,64,128]{2,1,0:T(8,128)(2,1)S(1)} collective-permute-done((bf16[2,64,128]{2,1,0:T(8,128)(2,1)S(1)}, bf16[2,64,128]{2,1,0:T(8,128)(2,1)S(1)}, u32[]{:S(2)}, u32[]{:S(2)}) %collective-permute-start.3) | collective-permute-done | bytes 32800 | tf_op jit(solution)/shard_map/ppermute | solution.py:343
  18.0 0.0 collective-permute-done.4.refs_10_
  18.0 0.0 copy-done.3
  18.1 4.7 %shard_map.103 = (bf16[2,64,128]{2,1,0:T(8,128)(2,1)S(1)}, bf16[2,64,128]{2,1,0:T(8,128)(2,1)S(1)}, bf16[2,64,128]{2,1,0:T(8,128)(2,1)S(1)}, bf16[2,64,128]{2,1,...) custom-call(f32[2,128,128]{2,1,0:T(8,128)S(1)} %get-tuple-element.45.refs_0_, ...), custom_call_target="tpu_custom_call" | custom-call | tf_op jit(solution)/shard_map/pallas_call | solution.py:317
  22.8 0.1 collective-permute-start.12
  22.9 2.6 %collective-permute-start.8 = (bf16[2,64,128]{2,1,0:T(8,128)(2,1)S(1)}, bf16[2,64,128]{2,1,0:T(8,128)(2,1)S(1)}, u32[]{:S(2)}, u32[]{:S(2)}) collective-permute-start(bf16[2,64,128]{2,1,0:T(8,128)(2,1)S(1)} %get-tuple-element.55), channel_id=1, source_target_pairs={{0,2},{1,3},{2,0},{3,1},{4,6},{5,7},{6,4},{7,5},{8,10},{9,11},{10,... | collective-permute-start | bytes 98312 | tf_op jit(solution)/shard_map/ppermute | solution.py:343
  25.4 1.8 %collective-permute-start.9 = (bf16[2,64,128]{2,1,0:T(8,128)(2,1)S(1)}, bf16[2,64,128]{2,1,0:T(8,128)(2,1)S(1)}, u32[]{:S(2)}, u32[]{:S(2)}) collective-permute-start(bf16[2,64,128]{2,1,0:T(8,128)(2,1)S(1)} %get-tuple-element.56), channel_id=1, source_target_pairs={{0,3},{1,2},{2,1},{3,0},{4,7},{5,6},{6,5},{7,4},{8,11},{9,10},{10,... | collective-permute-start | bytes 98312 | tf_op jit(solution)/shard_map/ppermute | solution.py:343
  27.3 0.5 %collective-permute-done.8.refs_0_.refs_1_ = bf16[2,64,128]{2,1,0:T(8,128)(2,1)S(1)} collective-permute-done((bf16[2,64,128]{2,1,0:T(8,128)(2,1)S(1)}, bf16[2,64,128]{2,1,0:T(8,128)(2,1)S(1)}, u32[]{:S(2)}, u32[]{:S(2)}) %collective-permute-start.8) | collective-permute-done | bytes 32800 | tf_op jit(solution)/shard_map/ppermute | solution.py:343
  27.8 3.4 %collective-permute-done.9.refs_1_.refs_2_ = bf16[2,64,128]{2,1,0:T(8,128)(2,1)S(1)} collective-permute-done((bf16[2,64,128]{2,1,0:T(8,128)(2,1)S(1)}, bf16[2,64,128]{2,1,0:T(8,128)(2,1)S(1)}, u32[]{:S(2)}, u32[]{:S(2)}) %collective-permute-start.9) | collective-permute-done | bytes 32800 | tf_op jit(solution)/shard_map/ppermute | solution.py:343
  31.2 0.0 collective-permute-done.12.refs_4_.refs_3_
  31.2 0.2 shard_map.105
  31.4 0.1 collective-permute-start.14
  31.5 1.5 %collective-permute-start.13 = (bf16[2,1,64,512]{3,2,1,0:T(8,128)(2,1)S(1)}, bf16[2,1,64,512]{3,2,1,0:T(8,128)(2,1)S(1)}, u32[]{:S(2)}, u32[]{:S(2)}) collective-permute-start(bf16[2,1,64,512]{3,2,1,0:T(8,128)(2,1)S(1)} %get-tuple-element.61), channel_id=1, source_target_pairs={{0,28},{4,8},{8,4},{12,16},{16,12},{20,24},{24,20},{28,0},{1,29},{... | collective-permute-start | bytes 393224 | tf_op jit(solution)/shard_map/ppermute | solution.py:349
  33.0 0.0 collective-permute-start.10
  33.0 1.8 %collective-permute-start.11 = (bf16[2,64,128]{2,1,0:T(8,128)(2,1)S(1)}, bf16[2,64,128]{2,1,0:T(8,128)(2,1)S(1)}, u32[]{:S(2)}, u32[]{:S(2)}) collective-permute-start(bf16[2,64,128]{2,1,0:T(8,128)(2,1)S(1)} %get-tuple-element.58), channel_id=1, source_target_pairs={{0,3},{1,2},{2,1},{3,0},{4,7},{5,6},{6,5},{7,4},{8,11},{9,10},{10,... | collective-permute-start | bytes 98312 | tf_op jit(solution)/shard_map/ppermute | solution.py:343
  34.8 3.3 %collective-permute-done.10.refs_2_ = bf16[2,64,128]{2,1,0:T(8,128)(2,1)S(1)} collective-permute-done((bf16[2,64,128]{2,1,0:T(8,128)(2,1)S(1)}, bf16[2,64,128]{2,1,0:T(8,128)(2,1)S(1)}, u32[]{:S(2)}, u32[]{:S(2)}) %collective-permute-start.10) | collective-permute-done | bytes 32800 | tf_op jit(solution)/shard_map/ppermute | solution.py:343
  38.1 0.7 %collective-permute-done.11.refs_3_ = bf16[2,64,128]{2,1,0:T(8,128)(2,1)S(1)} collective-permute-done((bf16[2,64,128]{2,1,0:T(8,128)(2,1)S(1)}, bf16[2,64,128]{2,1,0:T(8,128)(2,1)S(1)}, u32[]{:S(2)}, u32[]{:S(2)}) %collective-permute-start.11) | collective-permute-done | bytes 32800 | tf_op jit(solution)/shard_map/ppermute | solution.py:343
  38.8 0.3 shard_map.104.refs_0_
  39.1 0.0 collective-permute-done.14.refs_1_
  39.1 0.7 %shard_map.106.refs_2_ = f32[2,1,128,512]{3,2,1,0:T(8,128)} custom-call(f32[2,1,128,512]{3,2,1,0:T(8,128)S(1)} %shard_map.104.refs_0_, bf16[2,1,64,512]{3,2,1,0:T(8,128)(2,1)S(1)} %collective-permute-done.14.refs_1_), custom_call_target="tpu_custom_call" | custom-call | tf_op jit(solution)/shard_map/pallas_call | solution.py:305
  39.9 0.0 collective-permute-done.13.refs_1_
  39.9 0.7 %shard_map.107 = f32[2,1,128,512]{3,2,1,0:T(8,128)} custom-call(f32[2,1,128,512]{3,2,1,0:T(8,128)S(1)} %shard_map.104.refs_0_, bf16[2,1,64,512]{3,2,1,0:T(8,128)(2,1)S(1)} %collective-permute-done.13.refs_1_, f32[2,1,128,512]{3,2,1,0:T(8,128)} %shard_map.106.refs_2_), custom_call_target="tpu_custom_call", output_to_operand_aliasing={{}: (2, {})} | custom-call | tf_op jit(solution)/shard_map/pallas_call | solution.py:305
  (7 shorter events, 0.0 us)
Async XLA Ops:
  1.1 8.1 %collective-permute-start = (bf16[2,1,64,512]{3,2,1,0:T(8,128)(2,1)S(1)}, bf16[2,1,64,512]{3,2,1,0:T(8,128)(2,1)S(1)}, u32[]{:S(2)}, u32[]{:S(2)}) collective-permute-start(bf16[2,1,64,512]{3,2,1,0:T(8,128)(2,1)S(1)} %get-tuple-element.37), channel_id=1, source_target_pairs={{0,28},{4,8},{8,4},{12,16},{16,12},{20,24},{24,20},{28,0},{1,29},{... | collective-permute-start | bytes 393224 | tf_op jit(solution)/shard_map/ppermute | solution.py:349
  4.5 4.6 %collective-permute-start.1 = (bf16[2,1,64,512]{3,2,1,0:T(8,128)(2,1)S(1)}, bf16[2,1,64,512]{3,2,1,0:T(8,128)(2,1)S(1)}, u32[]{:S(2)}, u32[]{:S(2)}) collective-permute-start(bf16[2,1,64,512]{3,2,1,0:T(8,128)(2,1)S(1)} %get-tuple-element.38), channel_id=1, source_target_pairs={{0,4},{4,0},{8,12},{12,8},{16,20},{20,16},{24,28},{28,24},{1,5},{5... | collective-permute-start | bytes 393224 | tf_op jit(solution)/shard_map/ppermute | solution.py:352
  4.5 9.2 %copy-start.6 = (f32[128,128]{1,0:T(8,128)S(1)}, f32[128,128]{1,0:T(8,128)}, u32[]{:S(2)}) copy-start(f32[128,128]{1,0:T(8,128)} %refs_3_.1) | copy-start | bytes 196612
  4.9 8.7 %collective-permute-start.5 = (bf16[2,64,128]{2,1,0:T(8,128)(2,1)S(1)}, bf16[2,64,128]{2,1,0:T(8,128)(2,1)S(1)}, u32[]{:S(2)}, u32[]{:S(2)}) collective-permute-start(bf16[2,64,128]{2,1,0:T(8,128)(2,1)S(1)} %get-tuple-element.51), channel_id=1, source_target_pairs={{0,2},{1,3},{2,0},{3,1},{4,6},{5,7},{6,4},{7,5},{8,10},{9,11},{10,... | collective-permute-start | bytes 98312 | tf_op jit(solution)/shard_map/ppermute | solution.py:343
  7.6 7.2 %collective-permute-start.6 = (bf16[2,64,128]{2,1,0:T(8,128)(2,1)S(1)}, bf16[2,64,128]{2,1,0:T(8,128)(2,1)S(1)}, u32[]{:S(2)}, u32[]{:S(2)}) collective-permute-start(bf16[2,64,128]{2,1,0:T(8,128)(2,1)S(1)} %get-tuple-element.52), channel_id=1, source_target_pairs={{0,3},{1,2},{2,1},{3,0},{4,7},{5,6},{6,5},{7,4},{8,11},{9,10},{10,... | collective-permute-start | bytes 98312 | tf_op jit(solution)/shard_map/ppermute | solution.py:343
  8.9 5.8 %collective-permute-start.7 = (bf16[2,64,128]{2,1,0:T(8,128)(2,1)S(1)}, bf16[2,64,128]{2,1,0:T(8,128)(2,1)S(1)}, u32[]{:S(2)}, u32[]{:S(2)}) collective-permute-start(bf16[2,64,128]{2,1,0:T(8,128)(2,1)S(1)} %get-tuple-element.53), channel_id=1, source_target_pairs={{0,1},{1,0},{2,3},{3,2},{4,5},{5,4},{6,7},{7,6},{8,9},{9,8},{10,11... | collective-permute-start | bytes 98312 | tf_op jit(solution)/shard_map/ppermute | solution.py:343
  9.1 4.6 %copy-start.1 = (f32[2,128,128]{2,1,0:T(8,128)S(1)}, f32[2,128,128]{2,1,0:T(8,128)}, u32[]{:S(2)}) copy-start(f32[2,128,128]{2,1,0:T(8,128)} %refs_2_) | copy-start | bytes 393220
  9.2 4.6 %copy-start.7 = (s32[1,2]{1,0:T(1,128)S(1)}, s32[1,2]{1,0:T(1,128)}, u32[]{:S(2)}) copy-start(s32[1,2]{1,0:T(1,128)} %refs_0_.1) | copy-start | bytes 28
  9.2 8.9 %copy-start = (f32[4,128,128]{2,1,0:T(8,128)S(1)}, f32[4,128,128]{2,1,0:T(8,128)}, u32[]{:S(2)}) copy-start(f32[4,128,128]{2,1,0:T(8,128)} %refs_3_.2) | copy-start | bytes 786436
  9.2 8.8 %copy-start.3 = (bf16[256,256]{1,0:T(8,128)(2,1)S(1)}, bf16[256,256]{1,0:T(8,128)(2,1)}, u32[]{:S(2)}) copy-start(bf16[256,256]{1,0:T(8,128)(2,1)} %constant.10.clone.refs_6_) | copy-start | bytes 393220
  9.2 8.8 %copy-start.4 = (bf16[256,256]{1,0:T(8,128)(2,1)S(1)}, bf16[256,256]{1,0:T(8,128)(2,1)}, u32[]{:S(2)}) copy-start(bf16[256,256]{1,0:T(8,128)(2,1)} %constant.9.clone.refs_5_) | copy-start | bytes 393220
  9.2 8.8 %copy-start.5 = (bf16[256,256]{1,0:T(8,128)(2,1)S(1)}, bf16[256,256]{1,0:T(8,128)(2,1)}, u32[]{:S(2)}) copy-start(bf16[256,256]{1,0:T(8,128)(2,1)} %constant.8.clone.refs_4_) | copy-start | bytes 393220
  9.4 8.6 %copy-start.2 = (bf16[256,256]{1,0:T(8,128)(2,1)S(1)}, bf16[256,256]{1,0:T(8,128)(2,1)}, u32[]{:S(2)}) copy-start(bf16[256,256]{1,0:T(8,128)(2,1)} %constant.11.clone.refs_7_) | copy-start | bytes 393220
  9.4 5.4 %collective-permute-start.2 = (bf16[2,64,128]{2,1,0:T(8,128)(2,1)S(1)}, bf16[2,64,128]{2,1,0:T(8,128)(2,1)S(1)}, u32[]{:S(2)}, u32[]{:S(2)}) collective-permute-start(bf16[2,64,128]{2,1,0:T(8,128)(2,1)S(1)} %get-tuple-element.48), channel_id=1, source_target_pairs={{0,2},{1,3},{2,0},{3,1},{4,6},{5,7},{6,4},{7,5},{8,10},{9,11},{10,... | collective-permute-start | bytes 98312 | tf_op jit(solution)/shard_map/ppermute | solution.py:343
  12.3 5.7 %collective-permute-start.3 = (bf16[2,64,128]{2,1,0:T(8,128)(2,1)S(1)}, bf16[2,64,128]{2,1,0:T(8,128)(2,1)S(1)}, u32[]{:S(2)}, u32[]{:S(2)}) collective-permute-start(bf16[2,64,128]{2,1,0:T(8,128)(2,1)S(1)} %get-tuple-element.49), channel_id=1, source_target_pairs={{0,3},{1,2},{2,1},{3,0},{4,7},{5,6},{6,5},{7,4},{8,11},{9,10},{10,... | collective-permute-start | bytes 98312 | tf_op jit(solution)/shard_map/ppermute | solution.py:343
  13.7 4.4 %collective-permute-start.4 = (bf16[2,64,128]{2,1,0:T(8,128)(2,1)S(1)}, bf16[2,64,128]{2,1,0:T(8,128)(2,1)S(1)}, u32[]{:S(2)}, u32[]{:S(2)}) collective-permute-start(bf16[2,64,128]{2,1,0:T(8,128)(2,1)S(1)} %get-tuple-element.50), channel_id=1, source_target_pairs={{0,1},{1,0},{2,3},{3,2},{4,5},{5,4},{6,7},{7,6},{8,9},{9,8},{10,11... | collective-permute-start | bytes 98312 | tf_op jit(solution)/shard_map/ppermute | solution.py:343
  22.8 8.4 %collective-permute-start.12 = (bf16[2,128,128]{2,1,0:T(8,128)(2,1)S(1)}, bf16[2,128,128]{2,1,0:T(8,128)(2,1)S(1)}, u32[]{:S(2)}, u32[]{:S(2)}) collective-permute-start(bf16[2,128,128]{2,1,0:T(8,128)(2,1)S(1)} %get-tuple-element.59), channel_id=1, source_target_pairs={{0,1},{1,0},{2,3},{3,2},{4,5},{5,4},{6,7},{7,6},{8,9},{9,8},{10,11... | collective-permute-start | bytes 196616 | tf_op jit(solution)/shard_map/ppermute | solution.py:343
  22.9 4.9 %collective-permute-start.8 = (bf16[2,64,128]{2,1,0:T(8,128)(2,1)S(1)}, bf16[2,64,128]{2,1,0:T(8,128)(2,1)S(1)}, u32[]{:S(2)}, u32[]{:S(2)}) collective-permute-start(bf16[2,64,128]{2,1,0:T(8,128)(2,1)S(1)} %get-tuple-element.55), channel_id=1, source_target_pairs={{0,2},{1,3},{2,0},{3,1},{4,6},{5,7},{6,4},{7,5},{8,10},{9,11},{10,... | collective-permute-start | bytes 98312 | tf_op jit(solution)/shard_map/ppermute | solution.py:343
  25.4 5.7 %collective-permute-start.9 = (bf16[2,64,128]{2,1,0:T(8,128)(2,1)S(1)}, bf16[2,64,128]{2,1,0:T(8,128)(2,1)S(1)}, u32[]{:S(2)}, u32[]{:S(2)}) collective-permute-start(bf16[2,64,128]{2,1,0:T(8,128)(2,1)S(1)} %get-tuple-element.56), channel_id=1, source_target_pairs={{0,3},{1,2},{2,1},{3,0},{4,7},{5,6},{6,5},{7,4},{8,11},{9,10},{10,... | collective-permute-start | bytes 98312 | tf_op jit(solution)/shard_map/ppermute | solution.py:343
  31.4 7.7 %collective-permute-start.14 = (bf16[2,1,64,512]{3,2,1,0:T(8,128)(2,1)S(1)}, bf16[2,1,64,512]{3,2,1,0:T(8,128)(2,1)S(1)}, u32[]{:S(2)}, u32[]{:S(2)}) collective-permute-start(bf16[2,1,64,512]{3,2,1,0:T(8,128)(2,1)S(1)} %get-tuple-element.62), channel_id=1, source_target_pairs={{0,4},{4,0},{8,12},{12,8},{16,20},{20,16},{24,28},{28,24},{1,5},{5... | collective-permute-start | bytes 393224 | tf_op jit(solution)/shard_map/ppermute | solution.py:352
  31.5 8.4 %collective-permute-start.13 = (bf16[2,1,64,512]{3,2,1,0:T(8,128)(2,1)S(1)}, bf16[2,1,64,512]{3,2,1,0:T(8,128)(2,1)S(1)}, u32[]{:S(2)}, u32[]{:S(2)}) collective-permute-start(bf16[2,1,64,512]{3,2,1,0:T(8,128)(2,1)S(1)} %get-tuple-element.61), channel_id=1, source_target_pairs={{0,28},{4,8},{8,4},{12,16},{16,12},{20,24},{24,20},{28,0},{1,29},{... | collective-permute-start | bytes 393224 | tf_op jit(solution)/shard_map/ppermute | solution.py:349
  33.0 5.1 %collective-permute-start.10 = (bf16[2,64,128]{2,1,0:T(8,128)(2,1)S(1)}, bf16[2,64,128]{2,1,0:T(8,128)(2,1)S(1)}, u32[]{:S(2)}, u32[]{:S(2)}) collective-permute-start(bf16[2,64,128]{2,1,0:T(8,128)(2,1)S(1)} %get-tuple-element.57), channel_id=1, source_target_pairs={{0,2},{1,3},{2,0},{3,1},{4,6},{5,7},{6,4},{7,5},{8,10},{9,11},{10,... | collective-permute-start | bytes 98312 | tf_op jit(solution)/shard_map/ppermute | solution.py:343
  33.0 5.7 %collective-permute-start.11 = (bf16[2,64,128]{2,1,0:T(8,128)(2,1)S(1)}, bf16[2,64,128]{2,1,0:T(8,128)(2,1)S(1)}, u32[]{:S(2)}, u32[]{:S(2)}) collective-permute-start(bf16[2,64,128]{2,1,0:T(8,128)(2,1)S(1)} %get-tuple-element.58), channel_id=1, source_target_pairs={{0,3},{1,2},{2,1},{3,0},{4,7},{5,6},{6,5},{7,4},{8,11},{9,10},{10,... | collective-permute-start | bytes 98312 | tf_op jit(solution)/shard_map/ppermute | solution.py:343

commit v5 on v4

--- a/solution.py
+++ b/solution.py
@@ -13,7 +13,7 @@
 SPAN = 1 << 16
 ORDER = (2, 3, 1, 0)
 EARLY = 3
-LATE = 2
+LATE = 3
 
 
 SMEM = pl.BlockSpec(memory_space=pltpu.SMEM)
@@ -109,7 +109,7 @@
     inside = (line >= -extents[0, 0]) & (line < strip + extents[0, 1])
     for part in range(2):
         incident[part] = jnp.where(inside, probe_wave[part], 0.0)
-    upper[...] = jnp.full(upper.shape, row < BAND).astype(jnp.float32)
+    upper[...] = jnp.full(upper.shape, row < BAND).astype(jnp.float32).astype(upper.dtype)
     scale = 1.0 / window**2
     turn[0] = jnp.cos(fresnel_phase[...]) * scale
     turn[1] = jnp.sin(fresnel_phase[...]) * scale
@@ -196,21 +196,22 @@
     def inverse(value, exact):
         return from_right(*from_left(*value, back, exact), ahead, exact)
 
-    above = upper[...] != 0.0
+    above = upper[...] != 0
+    above_wide = upper[...].astype(jnp.float32) != 0.0
     for place, mask in enumerate(order):
         index = depth ^ mask
         if place < EARLY:
-            edge_rows, own_rows = (arrived[p][...].astype(jnp.float32) for p in (place, EARLY + place))
+            edge_rows, own_rows = arrived[place][...], arrived[EARLY + place][...]
             layers[index, :, :BAND] = jnp.where(above, edge_rows, own_rows)
             layers[index, :, BAND:] = jnp.where(above, own_rows, edge_rows)
         else:
-            layers[index] = arrived[EARLY + place][...].astype(jnp.float32)
+            layers[index] = arrived[EARLY + place][...]
     real, imag = incident[0], incident[1]
     cosine, sine = turn[0], turn[1]
     scale = 1.0 / window
     for index in range(depths):
         waves[index, 0], waves[index, 1] = real, imag
-        layer_real, layer_imag = layers[index, 0], layers[index, 1]
+        layer_real, layer_imag = layers[index, 0].astype(jnp.float32), layers[index, 1].astype(jnp.float32)
         mixed = (real * layer_real - imag * layer_imag, real * layer_imag + imag * layer_real)
         real, imag = transform(mixed, True)
         if index + 1 < depths:
@@ -225,7 +226,7 @@
         waves[index, 0] = held_real * adj_real + held_imag * adj_imag
         waves[index, 1] = held_real * adj_imag - held_imag * adj_real
         if index > 0:
-            layer_real, layer_imag = layers[index, 0], layers[index, 1]
+            layer_real, layer_imag = layers[index, 0].astype(jnp.float32), layers[index, 1].astype(jnp.float32)
             real, imag = transform(
                 (layer_real * adj_real + layer_imag * adj_imag, layer_real * adj_imag - layer_imag * adj_real),
                 False,
@@ -235,8 +236,8 @@
         index = depth ^ mask
         if place < LATE:
             first, second = waves[index, :, :BAND], waves[index, :, BAND:]
-            outs[place][...] = jnp.where(above, first, second).astype(jnp.bfloat16)
-            outs[LATE + place][...] = jnp.where(above, second, first).astype(jnp.bfloat16)
+            outs[place][...] = jnp.where(above_wide, first, second).astype(jnp.bfloat16)
+            outs[LATE + place][...] = jnp.where(above_wide, second, first).astype(jnp.bfloat16)
         else:
             outs[LATE + place][...] = waves[index].astype(jnp.bfloat16)
 
@@ -376,7 +377,7 @@
     probe_wave, fresnel_phase, windows = lax.optimization_barrier((probe_wave, fresnel_phase, windows))
     incident, turn, upper = call(
         lambda *refs: prep_kernel(strip, *refs),
-        [square, square, jax.ShapeDtypeStruct((BAND, window), jnp.float32)],
+        [square, square, jax.ShapeDtypeStruct((BAND, window), jnp.bfloat16)],
         [extents, codes, probe_wave, fresnel_phase],
         scalars=1,
     )
@@ -394,7 +395,7 @@
             *early,
             *windows[EARLY:],
         ],
-        [pltpu.VMEM((depths, 2, window, window), jnp.float32)] * 2,
+        [pltpu.VMEM((depths, 2, window, window), kind) for kind in (jnp.bfloat16, jnp.float32)],
     )
     late = swapped(pieces[LATE : 2 * LATE])
     pieces = swapped([*pieces[:LATE], *pieces[2 * LATE :]])

time: 40.8 us -> 40.8 us (level)
  starting transfers between devices: 19.8 us -> 20.8 us
  waiting for transfers between devices: 11.1 us -> 10.1 us
    ppermute x11 -> x12, waiting for transfers between devices: 11.1 us -> 10.1 us  [swap(): return lax.ppermute(value, 'depth', [(d, d ^ mask) for d in range(depths)])]
    ppermute x11 -> x12, starting transfers between devices: 14.8 us -> 15.6 us  [swap(): return lax.ppermute(value, 'depth', [(d, d ^ mask) for d in range(depths)])]
  transfers between devices with their start and end apart: 15 -> 16, of which waited for: 6 -> 7; matrix products, arithmetic and copies ran while one was open for 0% -> 0% of each run, Pallas kernels for 7% -> 7%
where the time goes in v5:
time: 40.8 us; the launch traced here: 40.6 us
  starting transfers between devices  20.8 us (51%)
  waiting for transfers between devices  10.1 us (25%)
  Pallas kernels  9.48 us (23%)
    ppermute x12, starting transfers between devices, swap(): return lax.ppermute(value, 'depth', [(d, d ^ mask) for d in range(depths)])  15.6 us
    ppermute x12, waiting for transfers between devices, swap(): return lax.ppermute(value, 'depth', [(d, d ^ mask) for d in range(depths)])  10.1 us
    pallas_call x6, Pallas kernels, call(): pl.pallas_call(kernel, out_shape=outs, in_specs=[SMEM] * scalars + [VMEM]...  6.92 us
    ppermute x2, starting transfers between devices, outward(): lax.ppermute(value, 'tile', [(t, (t - 1 + 2 * (t % 2)) % tiles) for t in...  5.14 us
    pallas_call x2, Pallas kernels, edge(): pl.pallas_call(lambda *refs: edge_kernel(side, *refs), out_shape=jax.Shap...  1.49 us
    pallas_call x1, Pallas kernels, shards(): pl.pallas_call(lambda *refs: band_kernel(order, tiles, *refs), out_shape=...  1.07 us
  transfers between devices with their start and end apart: 16, of which 7 were waited for; matrix products, arithmetic and copies ran while one was open for 0% of the time, Pallas kernels for 7%

profile of v5, /device:TPU:0, one launch (start us, length us, event | category | flops | bytes accessed | tf_op | source)
XLA Modules:
  0.0 40.6 jit_solution(13038647061767826679)
XLA Ops:
  0.0 1.1 %bands.1 = (f32[2,1,128,512]{3,2,1,0:T(8,128)S(1)}, bf16[2,1,64,512]{3,2,1,0:T(8,128)(2,1)S(1)}, bf16[2,1,64,512]{3,2,1,0:T(8,128)(2,1)S(1)}, s32[4,128]{1,0:T(4,128)S(1)}) custom-call(s32[2,4]{1,0:T(2,128)} %bitcast.1, f32[2,1,128,512]{3,2,1,0:T(8,128)} %refs_1_.1), custom_call_target="tpu_custom_call" | custom-call | tf_op jit(solution)/shard_map/bands/pallas_call | solution.py:357
  1.1 3.4 %collective-permute-start = (bf16[2,1,64,512]{3,2,1,0:T(8,128)(2,1)S(1)}, bf16[2,1,64,512]{3,2,1,0:T(8,128)(2,1)S(1)}, u32[]{:S(2)}, u32[]{:S(2)}) collective-permute-start(bf16[2,1,64,512]{3,2,1,0:T(8,128)(2,1)S(1)} %get-tuple-element.38), channel_id=1, source_target_pairs={{0,28},{4,8},{8,4},{12,16},{16,12},{20,24},{24,20},{28,0},{1,29},{... | collective-permute-start | bytes 393224 | tf_op jit(solution)/shard_map/ppermute | solution.py:350
  4.5 0.0 collective-permute-start.1
  4.5 0.4 shard_map.100
  4.9 2.7 %collective-permute-start.5 = (bf16[2,64,128]{2,1,0:T(8,128)(2,1)S(1)}, bf16[2,64,128]{2,1,0:T(8,128)(2,1)S(1)}, u32[]{:S(2)}, u32[]{:S(2)}) collective-permute-start(bf16[2,64,128]{2,1,0:T(8,128)(2,1)S(1)} %get-tuple-element.52), channel_id=1, source_target_pairs={{0,2},{1,3},{2,0},{3,1},{4,6},{5,7},{6,4},{7,5},{8,10},{9,11},{10,... | collective-permute-start | bytes 98312 | tf_op jit(solution)/shard_map/ppermute | solution.py:344
  7.6 1.3 %collective-permute-start.6 = (bf16[2,64,128]{2,1,0:T(8,128)(2,1)S(1)}, bf16[2,64,128]{2,1,0:T(8,128)(2,1)S(1)}, u32[]{:S(2)}, u32[]{:S(2)}) collective-permute-start(bf16[2,64,128]{2,1,0:T(8,128)(2,1)S(1)} %get-tuple-element.53), channel_id=1, source_target_pairs={{0,3},{1,2},{2,1},{3,0},{4,7},{5,6},{6,5},{7,4},{8,11},{9,10},{10,... | collective-permute-start | bytes 98312 | tf_op jit(solution)/shard_map/ppermute | solution.py:344
  8.9 0.2 collective-permute-start.7
  9.1 0.0 collective-permute-done.refs_2_
  9.1 0.0 collective-permute-done.1.refs_3_
  9.2 0.0 copy-start.7
  9.2 0.0 copy-start
  9.2 0.0 copy-start.3
  9.2 0.0 copy-start.4
  9.2 0.0 copy-start.5
  9.2 0.2 shard_map.101
  9.4 0.0 copy-start.2
  9.4 2.9 %collective-permute-start.2 = (bf16[2,64,128]{2,1,0:T(8,128)(2,1)S(1)}, bf16[2,64,128]{2,1,0:T(8,128)(2,1)S(1)}, u32[]{:S(2)}, u32[]{:S(2)}) collective-permute-start(bf16[2,64,128]{2,1,0:T(8,128)(2,1)S(1)} %get-tuple-element.49), channel_id=1, source_target_pairs={{0,2},{1,3},{2,0},{3,1},{4,6},{5,7},{6,4},{7,5},{8,10},{9,11},{10,... | collective-permute-start | bytes 98312 | tf_op jit(solution)/shard_map/ppermute | solution.py:344
  12.3 1.3 %collective-permute-start.3 = (bf16[2,64,128]{2,1,0:T(8,128)(2,1)S(1)}, bf16[2,64,128]{2,1,0:T(8,128)(2,1)S(1)}, u32[]{:S(2)}, u32[]{:S(2)}) collective-permute-start(bf16[2,64,128]{2,1,0:T(8,128)(2,1)S(1)} %get-tuple-element.50), channel_id=1, source_target_pairs={{0,3},{1,2},{2,1},{3,0},{4,7},{5,6},{6,5},{7,4},{8,11},{9,10},{10,... | collective-permute-start | bytes 98312 | tf_op jit(solution)/shard_map/ppermute | solution.py:344
  13.7 0.0 collective-permute-done.5.refs_11_
  13.7 0.1 collective-permute-start.4
  13.7 1.0 %shard_map.102 = (f32[2,128,128]{2,1,0:T(8,128)S(1)}, f32[2,128,128]{2,1,0:T(8,128)S(1)}, bf16[64,128]{1,0:T(8,128)(2,1)S(1)}) custom-call(s32[1,2]{1,0:T(1,128)S(1)} %copy-done.7, s32[4,128]{1,0:T(4,128)S(1)} %get-tuple-element.35.codes.refs_0_.refs_1_, f32[2,128,128]{2,1,0:T(8,128)S(1)} %copy-done.1, f32[128,128]{1,0:T(8,128)S(1)} %copy-done.6), custom_call_target="tpu_custom_call" | custom-call | tf_op jit(solution)/shard_map/pallas_call | solution.py:318
  14.7 0.0 collective-permute-done.6.refs_12_
  14.7 0.0 collective-permute-done.7.refs_13_
  14.8 0.1 collective-permute-done.2.refs_8_
  14.9 3.2 %collective-permute-done.3.refs_9_ = bf16[2,64,128]{2,1,0:T(8,128)(2,1)S(1)} collective-permute-done((bf16[2,64,128]{2,1,0:T(8,128)(2,1)S(1)}, bf16[2,64,128]{2,1,0:T(8,128)(2,1)S(1)}, u32[]{:S(2)}, u32[]{:S(2)}) %collective-permute-start.3) | collective-permute-done | bytes 32800 | tf_op jit(solution)/shard_map/ppermute | solution.py:344
  18.0 0.0 collective-permute-done.4.refs_10_
  18.0 0.0 copy-done.3
  18.1 4.8 %shard_map.103 = (bf16[2,64,128]{2,1,0:T(8,128)(2,1)S(1)}, bf16[2,64,128]{2,1,0:T(8,128)(2,1)S(1)}, bf16[2,64,128]{2,1,0:T(8,128)(2,1)S(1)}, bf16[2,64,128]{2,1,...) custom-call(f32[2,128,128]{2,1,0:T(8,128)S(1)} %get-tuple-element.46, ...), custom_call_target="tpu_custom_call" | custom-call | tf_op jit(solution)/shard_map/pallas_call | solution.py:318
  22.8 1.1 %collective-permute-start.8 = (bf16[2,64,128]{2,1,0:T(8,128)(2,1)S(1)}, bf16[2,64,128]{2,1,0:T(8,128)(2,1)S(1)}, u32[]{:S(2)}, u32[]{:S(2)}) collective-permute-start(bf16[2,64,128]{2,1,0:T(8,128)(2,1)S(1)} %get-tuple-element.56), channel_id=1, source_target_pairs={{0,2},{1,3},{2,0},{3,1},{4,6},{5,7},{6,4},{7,5},{8,10},{9,11},{10,... | collective-permute-start | bytes 98312 | tf_op jit(solution)/shard_map/ppermute | solution.py:344
  23.9 1.2 %collective-permute-start.9 = (bf16[2,64,128]{2,1,0:T(8,128)(2,1)S(1)}, bf16[2,64,128]{2,1,0:T(8,128)(2,1)S(1)}, u32[]{:S(2)}, u32[]{:S(2)}) collective-permute-start(bf16[2,64,128]{2,1,0:T(8,128)(2,1)S(1)} %get-tuple-element.57), channel_id=1, source_target_pairs={{0,3},{1,2},{2,1},{3,0},{4,7},{5,6},{6,5},{7,4},{8,11},{9,10},{10,... | collective-permute-start | bytes 98312 | tf_op jit(solution)/shard_map/ppermute | solution.py:344
  25.1 1.2 %collective-permute-start.10 = (bf16[2,64,128]{2,1,0:T(8,128)(2,1)S(1)}, bf16[2,64,128]{2,1,0:T(8,128)(2,1)S(1)}, u32[]{:S(2)}, u32[]{:S(2)}) collective-permute-start(bf16[2,64,128]{2,1,0:T(8,128)(2,1)S(1)} %get-tuple-element.58), channel_id=1, source_target_pairs={{0,1},{1,0},{2,3},{3,2},{4,5},{5,4},{6,7},{7,6},{8,9},{9,8},{10,11... | collective-permute-start | bytes 98312 | tf_op jit(solution)/shard_map/ppermute | solution.py:344
  26.4 1.3 %collective-permute-done.8.refs_0_.refs_1_ = bf16[2,64,128]{2,1,0:T(8,128)(2,1)S(1)} collective-permute-done((bf16[2,64,128]{2,1,0:T(8,128)(2,1)S(1)}, bf16[2,64,128]{2,1,0:T(8,128)(2,1)S(1)}, u32[]{:S(2)}, u32[]{:S(2)}) %collective-permute-start.8) | collective-permute-done | bytes 32800 | tf_op jit(solution)/shard_map/ppermute | solution.py:344
  27.7 2.0 %collective-permute-done.9.refs_1_.refs_2_ = bf16[2,64,128]{2,1,0:T(8,128)(2,1)S(1)} collective-permute-done((bf16[2,64,128]{2,1,0:T(8,128)(2,1)S(1)}, bf16[2,64,128]{2,1,0:T(8,128)(2,1)S(1)}, u32[]{:S(2)}, u32[]{:S(2)}) %collective-permute-start.9) | collective-permute-done | bytes 32800 | tf_op jit(solution)/shard_map/ppermute | solution.py:344
  29.7 0.0 collective-permute-done.10.refs_2_.refs_3_
  29.7 0.2 shard_map.105
  29.9 0.1 collective-permute-start.15
  30.0 1.7 %collective-permute-start.14 = (bf16[2,1,64,512]{3,2,1,0:T(8,128)(2,1)S(1)}, bf16[2,1,64,512]{3,2,1,0:T(8,128)(2,1)S(1)}, u32[]{:S(2)}, u32[]{:S(2)}) collective-permute-start(bf16[2,1,64,512]{3,2,1,0:T(8,128)(2,1)S(1)} %get-tuple-element.63), channel_id=1, source_target_pairs={{0,28},{4,8},{8,4},{12,16},{16,12},{20,24},{24,20},{28,0},{1,29},{... | collective-permute-start | bytes 393224 | tf_op jit(solution)/shard_map/ppermute | solution.py:350
  31.7 1.0 %collective-permute-start.11 = (bf16[2,64,128]{2,1,0:T(8,128)(2,1)S(1)}, bf16[2,64,128]{2,1,0:T(8,128)(2,1)S(1)}, u32[]{:S(2)}, u32[]{:S(2)}) collective-permute-start(bf16[2,64,128]{2,1,0:T(8,128)(2,1)S(1)} %get-tuple-element.59), channel_id=1, source_target_pairs={{0,2},{1,3},{2,0},{3,1},{4,6},{5,7},{6,4},{7,5},{8,10},{9,11},{10,... | collective-permute-start | bytes 98312 | tf_op jit(solution)/shard_map/ppermute | solution.py:344
  32.7 1.8 %collective-permute-start.12 = (bf16[2,64,128]{2,1,0:T(8,128)(2,1)S(1)}, bf16[2,64,128]{2,1,0:T(8,128)(2,1)S(1)}, u32[]{:S(2)}, u32[]{:S(2)}) collective-permute-start(bf16[2,64,128]{2,1,0:T(8,128)(2,1)S(1)} %get-tuple-element.60), channel_id=1, source_target_pairs={{0,3},{1,2},{2,1},{3,0},{4,7},{5,6},{6,5},{7,4},{8,11},{9,10},{10,... | collective-permute-start | bytes 98312 | tf_op jit(solution)/shard_map/ppermute | solution.py:344
  34.5 0.7 %collective-permute-start.13 = (bf16[2,64,128]{2,1,0:T(8,128)(2,1)S(1)}, bf16[2,64,128]{2,1,0:T(8,128)(2,1)S(1)}, u32[]{:S(2)}, u32[]{:S(2)}) collective-permute-start(bf16[2,64,128]{2,1,0:T(8,128)(2,1)S(1)} %get-tuple-element.61), channel_id=1, source_target_pairs={{0,1},{1,0},{2,3},{3,2},{4,5},{5,4},{6,7},{7,6},{8,9},{9,8},{10,11... | collective-permute-start | bytes 98312 | tf_op jit(solution)/shard_map/ppermute | solution.py:344
  35.2 2.0 %collective-permute-done.11.refs_3_ = bf16[2,64,128]{2,1,0:T(8,128)(2,1)S(1)} collective-permute-done((bf16[2,64,128]{2,1,0:T(8,128)(2,1)S(1)}, bf16[2,64,128]{2,1,0:T(8,128)(2,1)S(1)}, u32[]{:S(2)}, u32[]{:S(2)}) %collective-permute-start.11) | collective-permute-done | bytes 32800 | tf_op jit(solution)/shard_map/ppermute | solution.py:344
  37.2 1.2 %collective-permute-done.12.refs_4_ = bf16[2,64,128]{2,1,0:T(8,128)(2,1)S(1)} collective-permute-done((bf16[2,64,128]{2,1,0:T(8,128)(2,1)S(1)}, bf16[2,64,128]{2,1,0:T(8,128)(2,1)S(1)}, u32[]{:S(2)}, u32[]{:S(2)}) %collective-permute-start.12) | collective-permute-done | bytes 32800 | tf_op jit(solution)/shard_map/ppermute | solution.py:344
  38.5 0.3 collective-permute-done.13.refs_5_
  38.8 0.3 shard_map.104.refs_0_
  39.1 0.0 collective-permute-done.15.refs_1_
  39.1 0.7 %shard_map.106.refs_2_ = f32[2,1,128,512]{3,2,1,0:T(8,128)} custom-call(f32[2,1,128,512]{3,2,1,0:T(8,128)S(1)} %shard_map.104.refs_0_, bf16[2,1,64,512]{3,2,1,0:T(8,128)(2,1)S(1)} %collective-permute-done.15.refs_1_), custom_call_target="tpu_custom_call" | custom-call | tf_op jit(solution)/shard_map/pallas_call | solution.py:306
  39.9 0.0 collective-permute-done.14.refs_1_
  39.9 0.7 %shard_map.107 = f32[2,1,128,512]{3,2,1,0:T(8,128)} custom-call(f32[2,1,128,512]{3,2,1,0:T(8,128)S(1)} %shard_map.104.refs_0_, bf16[2,1,64,512]{3,2,1,0:T(8,128)(2,1)S(1)} %collective-permute-done.14.refs_1_, f32[2,1,128,512]{3,2,1,0:T(8,128)} %shard_map.106.refs_2_), custom_call_target="tpu_custom_call", output_to_operand_aliasing={{}: (2, {})} | custom-call | tf_op jit(solution)/shard_map/pallas_call | solution.py:306
  (9 shorter events, 0.0 us)
Async XLA Ops:
  1.1 8.1 %collective-permute-start = (bf16[2,1,64,512]{3,2,1,0:T(8,128)(2,1)S(1)}, bf16[2,1,64,512]{3,2,1,0:T(8,128)(2,1)S(1)}, u32[]{:S(2)}, u32[]{:S(2)}) collective-permute-start(bf16[2,1,64,512]{3,2,1,0:T(8,128)(2,1)S(1)} %get-tuple-element.38), channel_id=1, source_target_pairs={{0,28},{4,8},{8,4},{12,16},{16,12},{20,24},{24,20},{28,0},{1,29},{... | collective-permute-start | bytes 393224 | tf_op jit(solution)/shard_map/ppermute | solution.py:350
  4.5 4.6 %collective-permute-start.1 = (bf16[2,1,64,512]{3,2,1,0:T(8,128)(2,1)S(1)}, bf16[2,1,64,512]{3,2,1,0:T(8,128)(2,1)S(1)}, u32[]{:S(2)}, u32[]{:S(2)}) collective-permute-start(bf16[2,1,64,512]{3,2,1,0:T(8,128)(2,1)S(1)} %get-tuple-element.39), channel_id=1, source_target_pairs={{0,4},{4,0},{8,12},{12,8},{16,20},{20,16},{24,28},{28,24},{1,5},{5... | collective-permute-start | bytes 393224 | tf_op jit(solution)/shard_map/ppermute | solution.py:353
  4.5 9.2 %copy-start.6 = (f32[128,128]{1,0:T(8,128)S(1)}, f32[128,128]{1,0:T(8,128)}, u32[]{:S(2)}) copy-start(f32[128,128]{1,0:T(8,128)} %refs_3_.1) | copy-start | bytes 196612
  4.9 8.7 %collective-permute-start.5 = (bf16[2,64,128]{2,1,0:T(8,128)(2,1)S(1)}, bf16[2,64,128]{2,1,0:T(8,128)(2,1)S(1)}, u32[]{:S(2)}, u32[]{:S(2)}) collective-permute-start(bf16[2,64,128]{2,1,0:T(8,128)(2,1)S(1)} %get-tuple-element.52), channel_id=1, source_target_pairs={{0,2},{1,3},{2,0},{3,1},{4,6},{5,7},{6,4},{7,5},{8,10},{9,11},{10,... | collective-permute-start | bytes 98312 | tf_op jit(solution)/shard_map/ppermute | solution.py:344
  7.6 7.2 %collective-permute-start.6 = (bf16[2,64,128]{2,1,0:T(8,128)(2,1)S(1)}, bf16[2,64,128]{2,1,0:T(8,128)(2,1)S(1)}, u32[]{:S(2)}, u32[]{:S(2)}) collective-permute-start(bf16[2,64,128]{2,1,0:T(8,128)(2,1)S(1)} %get-tuple-element.53), channel_id=1, source_target_pairs={{0,3},{1,2},{2,1},{3,0},{4,7},{5,6},{6,5},{7,4},{8,11},{9,10},{10,... | collective-permute-start | bytes 98312 | tf_op jit(solution)/shard_map/ppermute | solution.py:344
  8.9 5.8 %collective-permute-start.7 = (bf16[2,64,128]{2,1,0:T(8,128)(2,1)S(1)}, bf16[2,64,128]{2,1,0:T(8,128)(2,1)S(1)}, u32[]{:S(2)}, u32[]{:S(2)}) collective-permute-start(bf16[2,64,128]{2,1,0:T(8,128)(2,1)S(1)} %get-tuple-element.54), channel_id=1, source_target_pairs={{0,1},{1,0},{2,3},{3,2},{4,5},{5,4},{6,7},{7,6},{8,9},{9,8},{10,11... | collective-permute-start | bytes 98312 | tf_op jit(solution)/shard_map/ppermute | solution.py:344
  9.1 4.6 %copy-start.1 = (f32[2,128,128]{2,1,0:T(8,128)S(1)}, f32[2,128,128]{2,1,0:T(8,128)}, u32[]{:S(2)}) copy-start(f32[2,128,128]{2,1,0:T(8,128)} %refs_2_) | copy-start | bytes 393220
  9.2 4.6 %copy-start.7 = (s32[1,2]{1,0:T(1,128)S(1)}, s32[1,2]{1,0:T(1,128)}, u32[]{:S(2)}) copy-start(s32[1,2]{1,0:T(1,128)} %refs_0_.1) | copy-start | bytes 28
  9.2 8.9 %copy-start = (f32[4,128,128]{2,1,0:T(8,128)S(1)}, f32[4,128,128]{2,1,0:T(8,128)}, u32[]{:S(2)}) copy-start(f32[4,128,128]{2,1,0:T(8,128)} %refs_3_.2) | copy-start | bytes 786436
  9.2 8.8 %copy-start.3 = (bf16[256,256]{1,0:T(8,128)(2,1)S(1)}, bf16[256,256]{1,0:T(8,128)(2,1)}, u32[]{:S(2)}) copy-start(bf16[256,256]{1,0:T(8,128)(2,1)} %constant.10.clone.refs_6_) | copy-start | bytes 393220
  9.2 8.8 %copy-start.4 = (bf16[256,256]{1,0:T(8,128)(2,1)S(1)}, bf16[256,256]{1,0:T(8,128)(2,1)}, u32[]{:S(2)}) copy-start(bf16[256,256]{1,0:T(8,128)(2,1)} %constant.9.clone.refs_5_) | copy-start | bytes 393220
  9.2 8.8 %copy-start.5 = (bf16[256,256]{1,0:T(8,128)(2,1)S(1)}, bf16[256,256]{1,0:T(8,128)(2,1)}, u32[]{:S(2)}) copy-start(bf16[256,256]{1,0:T(8,128)(2,1)} %constant.8.clone.refs_4_) | copy-start | bytes 393220
  9.4 8.6 %copy-start.2 = (bf16[256,256]{1,0:T(8,128)(2,1)S(1)}, bf16[256,256]{1,0:T(8,128)(2,1)}, u32[]{:S(2)}) copy-start(bf16[256,256]{1,0:T(8,128)(2,1)} %constant.11.clone.refs_7_) | copy-start | bytes 393220
  9.4 5.4 %collective-permute-start.2 = (bf16[2,64,128]{2,1,0:T(8,128)(2,1)S(1)}, bf16[2,64,128]{2,1,0:T(8,128)(2,1)S(1)}, u32[]{:S(2)}, u32[]{:S(2)}) collective-permute-start(bf16[2,64,128]{2,1,0:T(8,128)(2,1)S(1)} %get-tuple-element.49), channel_id=1, source_target_pairs={{0,2},{1,3},{2,0},{3,1},{4,6},{5,7},{6,4},{7,5},{8,10},{9,11},{10,... | collective-permute-start | bytes 98312 | tf_op jit(solution)/shard_map/ppermute | solution.py:344
  12.3 5.7 %collective-permute-start.3 = (bf16[2,64,128]{2,1,0:T(8,128)(2,1)S(1)}, bf16[2,64,128]{2,1,0:T(8,128)(2,1)S(1)}, u32[]{:S(2)}, u32[]{:S(2)}) collective-permute-start(bf16[2,64,128]{2,1,0:T(8,128)(2,1)S(1)} %get-tuple-element.50), channel_id=1, source_target_pairs={{0,3},{1,2},{2,1},{3,0},{4,7},{5,6},{6,5},{7,4},{8,11},{9,10},{10,... | collective-permute-start | bytes 98312 | tf_op jit(solution)/shard_map/ppermute | solution.py:344
  13.7 4.4 %collective-permute-start.4 = (bf16[2,64,128]{2,1,0:T(8,128)(2,1)S(1)}, bf16[2,64,128]{2,1,0:T(8,128)(2,1)S(1)}, u32[]{:S(2)}, u32[]{:S(2)}) collective-permute-start(bf16[2,64,128]{2,1,0:T(8,128)(2,1)S(1)} %get-tuple-element.51), channel_id=1, source_target_pairs={{0,1},{1,0},{2,3},{3,2},{4,5},{5,4},{6,7},{7,6},{8,9},{9,8},{10,11... | collective-permute-start | bytes 98312 | tf_op jit(solution)/shard_map/ppermute | solution.py:344
  22.8 4.9 %collective-permute-start.8 = (bf16[2,64,128]{2,1,0:T(8,128)(2,1)S(1)}, bf16[2,64,128]{2,1,0:T(8,128)(2,1)S(1)}, u32[]{:S(2)}, u32[]{:S(2)}) collective-permute-start(bf16[2,64,128]{2,1,0:T(8,128)(2,1)S(1)} %get-tuple-element.56), channel_id=1, source_target_pairs={{0,2},{1,3},{2,0},{3,1},{4,6},{5,7},{6,4},{7,5},{8,10},{9,11},{10,... | collective-permute-start | bytes 98312 | tf_op jit(solution)/shard_map/ppermute | solution.py:344
  23.9 5.7 %collective-permute-start.9 = (bf16[2,64,128]{2,1,0:T(8,128)(2,1)S(1)}, bf16[2,64,128]{2,1,0:T(8,128)(2,1)S(1)}, u32[]{:S(2)}, u32[]{:S(2)}) collective-permute-start(bf16[2,64,128]{2,1,0:T(8,128)(2,1)S(1)} %get-tuple-element.57), channel_id=1, source_target_pairs={{0,3},{1,2},{2,1},{3,0},{4,7},{5,6},{6,5},{7,4},{8,11},{9,10},{10,... | collective-permute-start | bytes 98312 | tf_op jit(solution)/shard_map/ppermute | solution.py:344
  25.1 4.5 %collective-permute-start.10 = (bf16[2,64,128]{2,1,0:T(8,128)(2,1)S(1)}, bf16[2,64,128]{2,1,0:T(8,128)(2,1)S(1)}, u32[]{:S(2)}, u32[]{:S(2)}) collective-permute-start(bf16[2,64,128]{2,1,0:T(8,128)(2,1)S(1)} %get-tuple-element.58), channel_id=1, source_target_pairs={{0,1},{1,0},{2,3},{3,2},{4,5},{5,4},{6,7},{7,6},{8,9},{9,8},{10,11... | collective-permute-start | bytes 98312 | tf_op jit(solution)/shard_map/ppermute | solution.py:344
  29.9 9.2 %collective-permute-start.15 = (bf16[2,1,64,512]{3,2,1,0:T(8,128)(2,1)S(1)}, bf16[2,1,64,512]{3,2,1,0:T(8,128)(2,1)S(1)}, u32[]{:S(2)}, u32[]{:S(2)}) collective-permute-start(bf16[2,1,64,512]{3,2,1,0:T(8,128)(2,1)S(1)} %get-tuple-element.64), channel_id=1, source_target_pairs={{0,4},{4,0},{8,12},{12,8},{16,20},{20,16},{24,28},{28,24},{1,5},{5... | collective-permute-start | bytes 393224 | tf_op jit(solution)/shard_map/ppermute | solution.py:353
  30.0 9.9 %collective-permute-start.14 = (bf16[2,1,64,512]{3,2,1,0:T(8,128)(2,1)S(1)}, bf16[2,1,64,512]{3,2,1,0:T(8,128)(2,1)S(1)}, u32[]{:S(2)}, u32[]{:S(2)}) collective-permute-start(bf16[2,1,64,512]{3,2,1,0:T(8,128)(2,1)S(1)} %get-tuple-element.63), channel_id=1, source_target_pairs={{0,28},{4,8},{8,4},{12,16},{16,12},{20,24},{24,20},{28,0},{1,29},{... | collective-permute-start | bytes 393224 | tf_op jit(solution)/shard_map/ppermute | solution.py:350
  31.7 5.5 %collective-permute-start.11 = (bf16[2,64,128]{2,1,0:T(8,128)(2,1)S(1)}, bf16[2,64,128]{2,1,0:T(8,128)(2,1)S(1)}, u32[]{:S(2)}, u32[]{:S(2)}) collective-permute-start(bf16[2,64,128]{2,1,0:T(8,128)(2,1)S(1)} %get-tuple-element.59), channel_id=1, source_target_pairs={{0,2},{1,3},{2,0},{3,1},{4,6},{5,7},{6,4},{7,5},{8,10},{9,11},{10,... | collective-permute-start | bytes 98312 | tf_op jit(solution)/shard_map/ppermute | solution.py:344
  32.7 5.7 %collective-permute-start.12 = (bf16[2,64,128]{2,1,0:T(8,128)(2,1)S(1)}, bf16[2,64,128]{2,1,0:T(8,128)(2,1)S(1)}, u32[]{:S(2)}, u32[]{:S(2)}) collective-permute-start(bf16[2,64,128]{2,1,0:T(8,128)(2,1)S(1)} %get-tuple-element.60), channel_id=1, source_target_pairs={{0,3},{1,2},{2,1},{3,0},{4,7},{5,6},{6,5},{7,4},{8,11},{9,10},{10,... | collective-permute-start | bytes 98312 | tf_op jit(solution)/shard_map/ppermute | solution.py:344
  34.5 4.3 %collective-permute-start.13 = (bf16[2,64,128]{2,1,0:T(8,128)(2,1)S(1)}, bf16[2,64,128]{2,1,0:T(8,128)(2,1)S(1)}, u32[]{:S(2)}, u32[]{:S(2)}) collective-permute-start(bf16[2,64,128]{2,1,0:T(8,128)(2,1)S(1)} %get-tuple-element.61), channel_id=1, source_target_pairs={{0,1},{1,0},{2,3},{3,2},{4,5},{5,4},{6,7},{7,6},{8,9},{9,8},{10,11... | collective-permute-start | bytes 98312 | tf_op jit(solution)/shard_map/ppermute | solution.py:344
